TPU v7x, 256 devices: a whole 4x4x8 slice. The times are simulated.
256 devices in a mesh: ctx: 64 (over y, z, x_hi), tp: 4 (over x_lo, core).
Axes of the slice: x: 4 (x_hi: 2, x_lo: 2; x = x_hi * 2 + x_lo), y: 4, z: 8, core: 2. Of those that a mesh axis runs over, the one named last changes fastest.
Arguments:
- queries: bfloat16 [4096, 3584], P('ctx', 'tp'), may hold values from -6 to 6
- keys: bfloat16 [4096, 512], P('ctx', 'tp'), may hold values from -5 to 5
- values: bfloat16 [4096, 512], P('ctx', 'tp'), may hold values from -6 to 6
- block_table: int32 [64], replicated, may hold values from 0 to 63, each once
- residual: bfloat16 [4096, 3584], P(('ctx', 'tp')), may hold values from -6 to 6
- out_weight: bfloat16 [3584, 3584], P('tp'), may hold values from -0.5 to 0.5
- norm_gain: bfloat16 [3584], replicated, may hold values from 0.099609375 to 1.8984375
- gate_logit_weight: bfloat16 [3584], replicated, may hold values from -0.09375 to 0.09375
- gate_weight: bfloat16 [3584, 20480], P(None, 'ctx'), may hold values from -0.09375 to 0.09375
- up_weight: bfloat16 [3584, 20480], P(None, 'ctx'), may hold values from -0.09375 to 0.09375
- down_weight: bfloat16 [20480, 3584], P('ctx'), may hold values from -0.0390625 to 0.0390625
Outputs:
- layer_out: bfloat16 [4096, 3584], P(('ctx', 'tp'))
Inputs may be any that keep to these rules, and one draw needn't show every extreme that they name: Each entry names a different pair; slot c holds blocks block_table[c] and its mirror, counted from the end of the prompt.
All inputs are finite; a program needn't handle non-finite values.
Results may differ from a plain program's by a relative error of at most 0.017.
Values may be sent and summed in bfloat16 or wider, within the bound.
No kernel may reach another device: no remote copies, remote signals or barrier semaphores. Data moves between devices by JAX's collectives and lax.ppermute only.
A program may use at most 128 MiB of HBM per device.

v0:
```python
import functools

import jax
import jax.numpy as jnp
from jax import lax
from jax.experimental import pallas as pl
from jax.experimental.pallas import tpu as pltpu
from jax.sharding import Mesh
from jax.sharding import PartitionSpec as P

HEADS = 28
KV_HEADS = 4
HEAD_DIM = 128
GROUP = HEADS // KV_HEADS
SIZES = {"y": 4, "z": 8, "xh": 2, "xl": 2, "core": 2}
CTX = ("y", "z", "xh")
TP = ("xl", "core")
f32 = jnp.float32
bf16 = jnp.bfloat16
VMEM = pl.BlockSpec(memory_space=pltpu.VMEM)
SMEM = pl.BlockSpec(memory_space=pltpu.SMEM)
HBM = pl.BlockSpec(memory_space=pltpu.HBM)
SMALL = pltpu.CompilerParams(vmem_limit_bytes=8 << 20)
NEG = -1e30
FLOOR = -1e29
EXP2 = 1.4426950408889634


def fetch(x, axis, k):
    n = SIZES[axis]
    k %= n
    if k == 0:
        return x
    return lax.ppermute(x, axis, [((i + k) % n, i) for i in range(n)])


def gather_direct(x, axis):
    return [fetch(x, axis, k) for k in range(SIZES[axis])]


def gather_ring(x, axis):
    n = SIZES[axis]
    h = n // 2
    ahead, behind = [x], [x]
    for k in range(1, h):
        ahead.append(fetch(ahead[-1], axis, 1))
        behind.append(fetch(behind[-1], axis, -1))
    rows = x.shape[0] // 2
    far = [fetch(ahead[-1][:rows], axis, 1), fetch(behind[-1][rows:], axis, -1)]
    return ahead, behind, far


def add_kernel(n_in, first, *refs):
    ins, outs = refs[:n_in], refs[n_in:]
    rows = outs[0].shape[0]
    for i, out in enumerate(outs):
        part = ins[0][i * rows : (i + 1) * rows, :].astype(f32)
        for other in ins[1:]:
            if other.shape[0] == ins[0].shape[0]:
                part += other[i * rows : (i + 1) * rows, :].astype(f32)
        out[...] = part.astype(out.dtype)
    last = ins[-1]
    if last.shape[0] < ins[0].shape[0]:
        mine = slice(first, first + last.shape[0])
        outs[0][mine, :] = (ins[0][mine, :].astype(f32) + last[...].astype(f32)).astype(bf16)


def add(xs, pieces=1, first=0):
    rows, width = xs[0].shape
    size = rows * width
    out = pl.pallas_call(
        functools.partial(add_kernel, len(xs), first),
        out_shape=[jax.ShapeDtypeStruct((rows // pieces, width), bf16)] * pieces,
        in_specs=[VMEM] * len(xs),
        out_specs=[VMEM] * pieces,
        compiler_params=SMALL,
        cost_estimate=pl.CostEstimate(
            flops=size * len(xs), bytes_accessed=2 * size * (len(xs) + 1), transcendentals=0
        ),
    )(*xs)
    return out[0] if pieces == 1 else out


def scatter_direct(chunks, axis):
    return [chunks[0]] + [fetch(chunks[k], axis, -k) for k in range(1, SIZES[axis])]


def scatter_ring(near, far, axis):
    n = SIZES[axis]
    h = n // 2
    up = fetch(far[0], axis, -1)
    down = fetch(far[1], axis, 1)
    for k in range(h - 1, 0, -1):
        first = near[k].shape[0] - down.shape[0]
        up = fetch(add([near[k], up]), axis, -1)
        down = fetch(add([near[n - k], down], first=first), axis, 1)
    return [near[0], up, down]


def attention_kernel(at_ref, table_ref, q_ref, *refs):
    kvs, w_any, keep_ref, send_ref = refs[:9], refs[9], refs[10], refs[11]
    w_ref, kv_ref, q_all, kp_ref, sems = refs[12:]
    half_rows = kvs[7].shape[0]
    places = [kv_ref.at[j] for j in (0, 1, 2, 3, 5, 6, 7)]
    places += [kv_ref.at[4, pl.ds(i * half_rows, half_rows)] for i in range(2)]
    copies = [
        pltpu.make_async_copy(src, dst, sems.at[i]) for i, (src, dst) in enumerate(zip(kvs, places))
    ]
    copy = pltpu.make_async_copy(w_any, w_ref, sems.at[9])
    for one in copies:
        one.start()
    copy.start()
    y, z, xh, t = (at_ref[i] for i in range(4))
    tokens = q_ref.shape[0]
    half = tokens // 2
    mirror = 2 * table_ref.shape[0] - 1

    def place(pair, local):
        return jnp.where(local < half, pair * half + local, (mirror - pair) * half + local - half)

    def pair_of(dy, dz, dx):
        slot = ((y + dy) % 4 * 8 + (z + dz) % 8) * 2 + (xh + dx) % 2
        return table_ref[slot]

    lane = lax.broadcasted_iota(jnp.int32, (1, 8 * tokens), 1)
    for j in range(8):
        pair = jnp.zeros_like(lane)
        for b in range(8):
            pair = jnp.where(lane // tokens == b, pair_of(b // 2, j, b % 2), pair)
        kp_ref[j : j + 1, :] = place(pair, lane % tokens)
    quarter = tokens // 4
    parts = [
        q_ref[pl.ds(pl.multiple_of((t ^ k) * quarter, quarter), quarter), :] for k in (0, 2, 1, 3)
    ]
    q = jnp.concatenate(parts, axis=0)
    q = jnp.concatenate([q[:, g * HEAD_DIM : (g + 1) * HEAD_DIM] for g in range(GROUP)], axis=0)
    row = lax.broadcasted_iota(jnp.int32, (tokens, 1), 0)
    order = row // quarter
    order = (order % 2) * 2 + order // 2
    qp = place(pair_of(0, 0, 0), (order ^ t) * quarter + row % quarter)
    total_rows = GROUP * tokens
    top = jnp.full((total_rows, 1), FLOOR, f32)
    total = jnp.zeros((total_rows, 1), f32)
    acc = jnp.zeros((total_rows, HEAD_DIM), f32)
    q_all[...] = q
    for one in copies:
        one.wait()

    def step(j, carry):
        top, total, acc = carry
        k = kv_ref[j, :, :HEAD_DIM]
        v = kv_ref[j, :, HEAD_DIM:]
        count = k.shape[0]
        score = lax.dot_general(
            q_all[...], k, (((1,), (1,)), ((), ())), preferred_element_type=f32
        )
        score = score * (HEAD_DIM**-0.5 * EXP2)
        visible = kp_ref[pl.ds(j, 1), :] <= qp
        score = jnp.where(visible[None], score.reshape(GROUP, tokens, count), NEG)
        score = score.reshape(total_rows, count)
        new_top = jnp.maximum(top, jnp.max(score, axis=-1, keepdims=True))
        weight = jnp.exp2(score - new_top)
        keep = jnp.exp2(top - new_top)
        total = total * keep + jnp.sum(weight, axis=-1, keepdims=True)
        acc = acc * keep + jnp.dot(weight.astype(bf16), v, preferred_element_type=f32)
        return new_top, total, acc

    top, total, acc = lax.fori_loop(0, 8, step, (top, total, acc))
    summed = (acc / total).astype(bf16)
    heads = jnp.concatenate([summed[g * tokens : (g + 1) * tokens] for g in range(GROUP)], axis=1)
    copy.wait()
    width = 512

    @pl.loop(0, w_ref.shape[1] // width)
    def _(n):
        cols = pl.ds(pl.multiple_of(n * width, width), width)
        part = jnp.dot(heads, w_ref[:, cols], preferred_element_type=f32).astype(bf16)
        keep_ref[:, cols] = part[:half]
        send_ref[:, cols] = part[half:]


def norm_kernel(keep, near, far, residual, gain, gate_w, attended, normed_ref, prob):
    rows = far.shape[0]
    head_sum = keep[:rows, :].astype(f32) + near[:rows, :].astype(f32) + far[...].astype(f32)
    kept = (residual[...].astype(f32) + head_sum).astype(bf16)
    attended[...] = kept
    wide = kept.astype(f32)
    mean_square = jnp.mean(wide * wide, axis=-1, keepdims=True)
    normed = (wide * lax.rsqrt(mean_square + 1e-06) * gain[...].astype(f32)).astype(bf16)
    normed_ref[...] = normed
    logit = jnp.sum(normed.astype(f32) * gate_w[...].astype(f32), axis=-1, keepdims=True)
    prob[...] = jnp.broadcast_to(1.0 / (1.0 + jnp.exp(-logit)), prob.shape)


def send_kernel(core_ref, g_any, u_any, d_any, out_any, sems):
    n = out_any.shape[0] // 3
    at = pl.multiple_of(core_ref[0] * n, n)
    copies = [
        pltpu.make_async_copy(w.at[pl.ds(at, n)], out_any.at[pl.ds(i * n, n)], sems.at[i])
        for i, w in enumerate((g_any, u_any, d_any))
    ]
    for copy in copies:
        copy.start()
    for copy in copies:
        copy.wait()


def assemble_kernel(g_any, u_any, d_any, a_any, b_any, w_ref, d_ref, sems):
    own = g_any.shape[0]
    swap = a_any.shape[0] // 3
    block = 128
    copies = []

    def start(src, at, dst, to, n):
        copy = pltpu.make_async_copy(
            src.at[pl.ds(at, n)], dst.at[pl.ds(to, n)], sems.at[len(copies)]
        )
        copy.start()
        copies.append(copy)

    for part in range(2):
        pos = 0
        for source, at, length in (
            ((g_any, u_any)[part], 0, own),
            (a_any, part * swap, swap),
            (b_any, part * swap, swap),
        ):
            done = 0
            while done < length:
                b, inside = divmod(pos, block)
                n = min(block - inside, length - done)
                start(source, at + done, w_ref, b * 2 * block + part * block + inside, n)
                done += n
                pos += n
    start(d_any, 0, d_ref, 0, own)
    start(a_any, 2 * swap, d_ref, own, swap)
    start(b_any, 2 * swap, d_ref, own + swap, swap)
    for copy in copies:
        copy.wait()


def expert_kernel(count, *refs):
    xs, w_ref, d_ref, outs = refs[:count], refs[count], refs[count + 1], refs[count + 2 : -2]
    x_ref, h_ref = refs[-2:]
    at = 0
    for x in xs:
        x_ref[at : at + x.shape[0], :] = x[...]
        at += x.shape[0]
    block = 128

    @pl.loop(0, w_ref.shape[0] // (2 * block))
    def _(b):
        both = lax.dot_general(
            x_ref[...],
            w_ref[pl.ds(pl.multiple_of(b * 2 * block, 2 * block), 2 * block), :],
            (((1,), (1,)), ((), ())),
            preferred_element_type=f32,
        )
        gate, up = both[:, :block], both[:, block:]
        value = (gate / (1.0 + jnp.exp(-gate)) * up).astype(bf16)
        h_ref[:, pl.ds(pl.multiple_of(b * block, block), block)] = value

    width = 512

    @pl.loop(0, d_ref.shape[1] // width)
    def _(c):
        cols = pl.ds(pl.multiple_of(c * width, width), width)
        part = jnp.dot(h_ref[...], d_ref[:, cols], preferred_element_type=f32).astype(bf16)
        at = 0
        for out in outs:
            out[:, cols] = part[at : at + out.shape[0]]
            at += out.shape[0]


def join_kernel(*refs):
    out = refs[-1]
    n = refs[0].shape[0]
    for i, ref in enumerate(refs[:-1]):
        out[i * n : (i + 1) * n, :] = ref[...]


def join(xs):
    rows, width = xs[0].shape
    return pl.pallas_call(
        join_kernel,
        out_shape=jax.ShapeDtypeStruct((rows * len(xs), width), bf16),
        in_specs=[VMEM] * len(xs),
        out_specs=VMEM,
        compiler_params=SMALL,
        cost_estimate=pl.CostEstimate(
            flops=0, bytes_accessed=4 * rows * len(xs) * width, transcendentals=0
        ),
    )(*xs)


def expert(xs, weights):
    w, d = weights
    rows, width = sum(x.shape[0] for x in xs), xs[0].shape[1]
    units = d.shape[0]
    return pl.pallas_call(
        functools.partial(expert_kernel, len(xs)),
        out_shape=[jax.ShapeDtypeStruct(x.shape, bf16) for x in xs],
        in_specs=[VMEM] * (len(xs) + 2),
        out_specs=[VMEM] * len(xs),
        scratch_shapes=[pltpu.VMEM((rows, width), bf16), pltpu.VMEM((rows, units), bf16)],
        compiler_params=pltpu.CompilerParams(vmem_limit_bytes=30 << 20),
        cost_estimate=pl.CostEstimate(
            flops=6 * rows * units * width,
            bytes_accessed=6 * units * width + 4 * rows * width,
            transcendentals=rows * units,
        ),
    )(*xs, w, d)


def final_kernel(attended, prob, *refs):
    terms, out = refs[:-1], refs[-1]
    shared = terms[0][...].astype(f32)
    for term in terms[1:]:
        shared += term[...].astype(f32)
    out[...] = (attended[...].astype(f32) + prob[:, :1] * shared).astype(bf16)


def per_device(
    queries,
    keys,
    values,
    block_table,
    residual,
    out_weight,
    norm_gain,
    gate_logit_weight,
    gate_weight,
    up_weight,
    down_weight,
):
    tokens = queries.shape[0]
    half = tokens // 2
    quarter = tokens // 4
    width = residual.shape[1]
    hidden = down_weight.shape[0]
    y, z, xh = (lax.axis_index(a) for a in CTX)
    core = lax.axis_index("core")
    t = lax.axis_index(TP)

    gate_t, up_t = gate_weight.T, up_weight.T
    piece = hidden // 2
    to_send = pl.pallas_call(
        send_kernel,
        out_shape=jax.ShapeDtypeStruct((3 * piece, width), bf16),
        in_specs=[SMEM, HBM, HBM, HBM],
        out_specs=VMEM,
        scratch_shapes=[pltpu.SemaphoreType.DMA((3,))],
        cost_estimate=pl.CostEstimate(
            flops=0, bytes_accessed=12 * piece * width, transcendentals=0
        ),
    )(core.astype(jnp.int32)[None], gate_t, up_t, down_weight)
    swap_a = lax.ppermute(to_send, ("xh", "xl"), [(0, 3), (3, 0), (1, 2), (2, 1)])

    kv = jnp.concatenate([keys, values], axis=1)
    kv = jnp.concatenate([kv, fetch(kv, "xh", 1)], axis=0)
    kv = jnp.concatenate(gather_direct(kv, "y"), axis=0)
    ahead, behind, far = gather_ring(kv, "z")
    kvs = ahead + behind[:0:-1] + far
    at = jnp.stack([y, z, xh, t]).astype(jnp.int32)

    rows = GROUP * tokens
    span = 64 * tokens
    keep, send = pl.pallas_call(
        attention_kernel,
        out_shape=[jax.ShapeDtypeStruct((half, width), bf16)] * 2,
        in_specs=[SMEM, SMEM, VMEM] + [HBM] * 10,
        out_specs=[VMEM] * 2,
        scratch_shapes=[
            pltpu.VMEM(out_weight.shape, bf16),
            pltpu.VMEM((8, 8 * tokens, 2 * HEAD_DIM), bf16),
            pltpu.VMEM((GROUP * tokens, HEAD_DIM), bf16),
            pltpu.VMEM((8, 8 * tokens), jnp.int32),
            pltpu.SemaphoreType.DMA((10,)),
        ],
        compiler_params=pltpu.CompilerParams(vmem_limit_bytes=46 << 20),
        cost_estimate=pl.CostEstimate(
            flops=4 * rows * span * HEAD_DIM + 2 * tokens * out_weight.size,
            bytes_accessed=2 * out_weight.size + 4 * span * HEAD_DIM,
            transcendentals=rows * span,
        ),
    )(at, block_table, queries, *kvs, out_weight)

    near = fetch(send, "core", 1)
    _, beyond = add([keep, near], pieces=2)
    beyond = fetch(beyond, "xl", 1)
    attended, normed, prob = pl.pallas_call(
        norm_kernel,
        out_shape=[
            jax.ShapeDtypeStruct((quarter, width), bf16),
            jax.ShapeDtypeStruct((quarter, width), bf16),
            jax.ShapeDtypeStruct((quarter, 128), f32),
        ],
        in_specs=[VMEM] * 6,
        out_specs=[VMEM] * 3,
        compiler_params=SMALL,
        cost_estimate=pl.CostEstimate(
            flops=10 * quarter * width, bytes_accessed=14 * quarter * width, transcendentals=quarter
        ),
    )(keep, near, beyond, residual, norm_gain[None, :], gate_logit_weight[None, :])

    by_y = join(gather_direct(normed, "y"))
    ahead, behind, far = gather_ring(by_y, "z")
    swap_a, _ = lax.optimization_barrier((swap_a, by_y))
    swap_b = fetch(swap_a, "core", 1)
    weights = pl.pallas_call(
        assemble_kernel,
        out_shape=[
            jax.ShapeDtypeStruct((4 * hidden, width), bf16),
            jax.ShapeDtypeStruct((2 * hidden, width), bf16),
        ],
        in_specs=[HBM] * 5,
        out_specs=[VMEM] * 2,
        scratch_shapes=[pltpu.SemaphoreType.DMA((24,))],
        compiler_params=pltpu.CompilerParams(vmem_limit_bytes=16 << 20),
        cost_estimate=pl.CostEstimate(
            flops=0, bytes_accessed=12 * hidden * width, transcendentals=0
        ),
    )(gate_t, up_t, down_weight, swap_a, swap_b)
    own, after, before = expert([ahead[0], ahead[1], behind[1]], weights)
    after_2, before_2, after_3, before_3 = expert([ahead[2], behind[2], ahead[3], behind[3]], weights)
    far_parts = expert(far, weights)
    near_parts = [own, after, after_2, after_3, None, before_3, before_2, before]
    by_y = add(scatter_ring(near_parts, far_parts, "z"), pieces=4)
    terms = scatter_direct(by_y, "y")
    return pl.pallas_call(
        final_kernel,
        out_shape=jax.ShapeDtypeStruct((quarter, width), bf16),
        in_specs=[VMEM] * 6,
        out_specs=VMEM,
        compiler_params=SMALL,
        cost_estimate=pl.CostEstimate(
            flops=10 * quarter * width, bytes_accessed=16 * quarter * width, transcendentals=0
        ),
    )(attended, prob, *terms)


def solution(mesh):
    fine = Mesh(mesh.devices.reshape(tuple(SIZES.values())), tuple(SIZES))
    return jax.shard_map(
        per_device,
        mesh=fine,
        in_specs=(
            P(CTX, TP),
            P(CTX, TP),
            P(CTX, TP),
            P(),
            P(CTX + TP, None),
            P(TP, None),
            P(),
            P(),
            P(None, CTX),
            P(None, CTX),
            P(CTX, None),
        ),
        out_specs=P(CTX + TP, None),
        check_vma=False,
    )
```

profile of v0, /device:TPU:0, one launch (start us, length us, event | category | flops | bytes accessed | tf_op | source)
XLA Modules:
  0.0 197.4 jit_solution(3654265410839373119)
XLA Ops:
  0.0 3.7 %shard_map.113 = bf16[480,3584]{1,0:T(8,128)(2,1)} custom-call(s32[1]{0:T(128)} %bitcast.6.core_ref, bf16[320,3584]{1,0:T(8,128)(2,1)} %bitcast.7, bf16[320,3584]{1,0:T(8,128)(2,1)} %bitcast.9, bf16[320,3584]{1,0:T(8,128)(2,1)} %d_any.3), custom_call_target="tpu_custom_call" | custom-call | bytes 6881280 | tf_op jit(solution)/shard_map/pallas_call | solution.py:347
  7.2 4.7 %collective-permute-done = bf16[64,256]{1,0:T(8,128)(2,1)S(1)} collective-permute-done((bf16[64,256]{1,0:T(8,128)(2,1)S(1)}, bf16[64,256]{1,0:T(8,128)(2,1)S(1)}, u32[]{:S(2)}, u32[]{:S(2)}) %collective-permute-start) | collective-permute-done | bytes 32800 | tf_op jit(solution)/shard_map/ppermute | solution.py:34
  16.8 3.9 %collective-permute-done.2 = bf16[128,256]{1,0:T(8,128)(2,1)S(1)} collective-permute-done((bf16[128,256]{1,0:T(8,128)(2,1)S(1)}, bf16[128,256]{1,0:T(8,128)(2,1)S(1)}, u32[]{:S(2)}, u32[]{:S(2)}) %collective-permute-start.2) | collective-permute-done | bytes 65568 | tf_op jit(solution)/shard_map/ppermute | solution.py:34
  21.3 5.9 %collective-permute-start.4 = (bf16[512,256]{1,0:T(8,128)(2,1)S(1)}, bf16[512,256]{1,0:T(8,128)(2,1)S(1)}, u32[]{:S(2)}, u32[]{:S(2)}) collective-permute-start(bf16[512,256]{1,0:T(8,128)(2,1)S(1)} %constant_dynamic-update-slice_fusion.2.refs_0_), channel_id=1, source_target_pairs={{8,0},{16,8},{24,16},{32,24},{40,32},{48,40},{56,48},{0,56},{9,1},... | collective-permute-start | bytes 786440 | tf_op jit(solution)/shard_map/ppermute | solution.py:34
  31.1 3.7 %collective-permute-start.5 = (bf16[512,256]{1,0:T(8,128)(2,1)S(1)}, bf16[512,256]{1,0:T(8,128)(2,1)S(1)}, u32[]{:S(2)}, u32[]{:S(2)}) collective-permute-start(bf16[512,256]{1,0:T(8,128)(2,1)S(1)} %collective-permute-done.4.refs_1_), channel_id=1, source_target_pairs={{8,0},{16,8},{24,16},{32,24},{40,32},{48,40},{56,48},{0,56},{9,1},... | collective-permute-start | bytes 786440 | tf_op jit(solution)/shard_map/ppermute | solution.py:34
  39.2 3.7 %collective-permute-start.6 = (bf16[512,256]{1,0:T(8,128)(2,1)S(1)}, bf16[512,256]{1,0:T(8,128)(2,1)S(1)}, u32[]{:S(2)}, u32[]{:S(2)}) collective-permute-start(bf16[512,256]{1,0:T(8,128)(2,1)S(1)} %collective-permute-done.5.refs_2_), channel_id=1, source_target_pairs={{8,0},{16,8},{24,16},{32,24},{40,32},{48,40},{56,48},{0,56},{9,1},... | collective-permute-start | bytes 786440 | tf_op jit(solution)/shard_map/ppermute | solution.py:34
  48.1 3.7 %collective-permute-start.10 = (bf16[256,256]{1,0:T(8,128)(2,1)}, bf16[256,256]{1,0:T(8,128)(2,1)}, u32[]{:S(2)}, u32[]{:S(2)}) collective-permute-start(bf16[256,256]{1,0:T(8,128)(2,1)} %slice.16), channel_id=1, source_target_pairs={{8,0},{16,8},{24,16},{32,24},{40,32},{48,40},{56,48},{0,56},{9,1},... | collective-permute-start | bytes 393224 | tf_op jit(solution)/shard_map/ppermute | solution.py:34
  54.6 5.0 %collective-permute-done.11.refs_8_ = bf16[256,256]{1,0:T(8,128)(2,1)} collective-permute-done((bf16[256,256]{1,0:T(8,128)(2,1)}, bf16[256,256]{1,0:T(8,128)(2,1)}, u32[]{:S(2)}, u32[]{:S(2)}) %collective-permute-start.11) | collective-permute-done | bytes 131104 | tf_op jit(solution)/shard_map/ppermute | solution.py:34
  67.0 9.0 %shard_map.109 = (bf16[32,3584]{1,0:T(8,128)(2,1)S(1)}, bf16[32,3584]{1,0:T(8,128)(2,1)S(1)}) custom-call(s32[4]{0:T(128)S(1)} %pad_add_fusion.at_ref, s32[64]{0:T(128)S(1)} %copy-done.19, bf16[64,896]{1,0:T(8,128)(2,1)S(1)} %copy-done.17, bf16[512,256]{1,0:T(8,128)(2,1)S(1)} %copy-done.8, bf16[512,256]{1,0:T(8,128)(2,1)S(1)} %copy-done.10, ...), custom_call_target="tpu_custom_call" | custom-call | flops 1350565888 | bytes 8519680 | tf_op jit(solution)/shard_map/pallas_call | solution.py:368
  80.7 3.4 %collective-permute-done.13.far = bf16[16,3584]{1,0:T(8,128)(2,1)S(1)} collective-permute-done((bf16[16,3584]{1,0:T(8,128)(2,1)S(1)}, bf16[16,3584]{1,0:T(8,128)(2,1)S(1)}, u32[]{:S(2)}, u32[]{:S(2)}) %collective-permute-start.13) | collective-permute-done | bytes 114720 | tf_op jit(solution)/shard_map/ppermute | solution.py:34
  87.4 3.2 %collective-permute-done.14.refs_1_ = bf16[16,3584]{1,0:T(8,128)(2,1)S(1)} collective-permute-done((bf16[16,3584]{1,0:T(8,128)(2,1)S(1)}, bf16[16,3584]{1,0:T(8,128)(2,1)S(1)}, u32[]{:S(2)}, u32[]{:S(2)}) %collective-permute-start.14) | collective-permute-done | bytes 114720 | tf_op jit(solution)/shard_map/ppermute | solution.py:34
  95.7 10.8 %collective-permute-done.17.refs_1_ = bf16[64,3584]{1,0:T(8,128)(2,1)S(1)} collective-permute-done((bf16[64,3584]{1,0:T(8,128)(2,1)S(1)}, bf16[64,3584]{1,0:T(8,128)(2,1)S(1)}, u32[]{:S(2)}, u32[]{:S(2)}) %collective-permute-start.17) | collective-permute-done | bytes 458784 | tf_op jit(solution)/shard_map/ppermute | solution.py:34
  108.5 10.0 %collective-permute-done.21.refs_0_ = bf16[64,3584]{1,0:T(8,128)(2,1)S(1)} collective-permute-done((bf16[64,3584]{1,0:T(8,128)(2,1)S(1)}, bf16[64,3584]{1,0:T(8,128)(2,1)S(1)}, u32[]{:S(2)}, u32[]{:S(2)}) %collective-permute-start.21) | collective-permute-done | bytes 458784 | tf_op jit(solution)/shard_map/ppermute | solution.py:34
  121.4 8.9 %collective-permute-done.23.refs_2_ = bf16[64,3584]{1,0:T(8,128)(2,1)S(1)} collective-permute-done((bf16[64,3584]{1,0:T(8,128)(2,1)S(1)}, bf16[64,3584]{1,0:T(8,128)(2,1)S(1)}, u32[]{:S(2)}, u32[]{:S(2)}) %collective-permute-start.23) | collective-permute-done | bytes 458784 | tf_op jit(solution)/shard_map/ppermute | solution.py:34
  130.4 3.8 %collective-permute-start.25 = (bf16[32,3584]{1,0:T(8,128)(2,1)S(1)}, bf16[32,3584]{1,0:T(8,128)(2,1)S(1)}, u32[]{:S(2)}, u32[]{:S(2)}) collective-permute-start(bf16[32,3584]{1,0:T(8,128)(2,1)S(1)} %slice.18), channel_id=1, source_target_pairs={{8,0},{16,8},{24,16},{32,24},{40,32},{48,40},{56,48},{0,56},{9,1},... | collective-permute-start | bytes 688136 | tf_op jit(solution)/shard_map/ppermute | solution.py:34
  134.3 4.5 %shard_map.114 = (bf16[1280,3584]{1,0:T(8,128)(2,1)S(1)}, bf16[640,3584]{1,0:T(8,128)(2,1)S(1)}) custom-call(bf16[320,3584]{1,0:T(8,128)(2,1)S(1)} %bitcast.8, bf16[320,3584]{1,0:T(8,128)(2,1)S(1)} %bitcast.10, bf16[320,3584]{1,0:T(8,128)(2,1)S(1)} %copy-done.2, bf16[480,3584]{1,0:T(8,128)(2,1)S(1)} %collective-permute-done.19.a_any, ...), custom_call_target="tpu_custom_call" | custom-call | bytes 13762560 | tf_op jit(solution)/shard_map/pallas_call | solution.py:410
  141.5 5.1 %shard_map.117 = (bf16[32,3584]{1,0:T(8,128)(2,1)S(1)}, bf16[32,3584]{1,0:T(8,128)(2,1)S(1)}) custom-call(bf16[32,3584]{1,0:T(8,128)(2,1)S(1)} %collective-permute-done.25.refs_0_, bf16[32,3584]{1,0:T(8,128)(2,1)S(1)} %collective-permute-done.26.refs_1_, bf16[1280,3584]{1,0:T(8,128)(2,1)S(1)} %get-tuple-element.34.refs_3_.refs_4_.refs_2_, ...), custom_call_target="tpu_custom_call" | custom-call | flops 880803840 | bytes 14680064 | tf_op jit(solution)/shard_map/pallas_call | solution.py:300
  148.7 6.2 %shard_map.116 = (bf16[64,3584]{1,0:T(8,128)(2,1)S(1)}, bf16[64,3584]{1,0:T(8,128)(2,1)S(1)}, bf16[64,3584]{1,0:T(8,128)(2,1)S(1)}, bf16[64,3584]{1,0:T(8,128)(2,1)S(1)}) custom-call(bf16[64,3584]{1,0:T(8,128)(2,1)S(1)} %collective-permute-done.21.refs_0_, bf16[64,3584]{1,0:T(8,128)(2,1)S(1)} %collective-permute-done.22.refs_1_, ...), custom_call_target="tpu_custom_call" | custom-call | flops 3523215360 | bytes 17432576 | tf_op jit(solution)/shard_map/pallas_call | solution.py:300
  157.5 7.1 %collective-permute-done.32.refs_1_ = bf16[64,3584]{1,0:T(8,128)(2,1)S(1)} collective-permute-done((bf16[64,3584]{1,0:T(8,128)(2,1)S(1)}, bf16[64,3584]{1,0:T(8,128)(2,1)S(1)}, u32[]{:S(2)}, u32[]{:S(2)}) %collective-permute-start.32) | collective-permute-done | bytes 458784 | tf_op jit(solution)/shard_map/ppermute | solution.py:34
  167.8 6.2 %shard_map.115 = (bf16[64,3584]{1,0:T(8,128)(2,1)S(1)}, bf16[64,3584]{1,0:T(8,128)(2,1)S(1)}, bf16[64,3584]{1,0:T(8,128)(2,1)S(1)}) custom-call(bf16[64,3584]{1,0:T(8,128)(2,1)S(1)} %shard_map.112.refs_0_, bf16[64,3584]{1,0:T(8,128)(2,1)S(1)} %collective-permute-done.17.refs_1_, bf16[64,3584]{1,0:T(8,128)(2,1)S(1)} %collective-permute-done.18.refs_2_, ...), custom_call_target="tpu_custom_call" | custom-call | flops 2642411520 | bytes 16515072 | tf_op jit(solution)/shard_map/pallas_call | solution.py:300
  174.3 3.7 %collective-permute-start.34 = (bf16[64,3584]{1,0:T(8,128)(2,1)S(1)}, bf16[64,3584]{1,0:T(8,128)(2,1)S(1)}, u32[]{:S(2)}, u32[]{:S(2)}) collective-permute-start(bf16[64,3584]{1,0:T(8,128)(2,1)S(1)} %shard_map.123), channel_id=1, source_target_pairs={{8,0},{16,8},{24,16},{32,24},{40,32},{48,40},{56,48},{0,56},{9,1},... | collective-permute-start | bytes 1376264 | tf_op jit(solution)/shard_map/ppermute | solution.py:34
  178.6 5.4 %collective-permute-done.34.refs_2_ = bf16[64,3584]{1,0:T(8,128)(2,1)S(1)} collective-permute-done((bf16[64,3584]{1,0:T(8,128)(2,1)S(1)}, bf16[64,3584]{1,0:T(8,128)(2,1)S(1)}, u32[]{:S(2)}, u32[]{:S(2)}) %collective-permute-start.34) | collective-permute-done | bytes 458784 | tf_op jit(solution)/shard_map/ppermute | solution.py:34
  184.1 4.2 %collective-permute-done.30.refs_1_ = bf16[64,3584]{1,0:T(8,128)(2,1)S(1)} collective-permute-done((bf16[64,3584]{1,0:T(8,128)(2,1)S(1)}, bf16[64,3584]{1,0:T(8,128)(2,1)S(1)}, u32[]{:S(2)}, u32[]{:S(2)}) %collective-permute-start.30) | collective-permute-done | bytes 458784 | tf_op jit(solution)/shard_map/ppermute | solution.py:34
  192.4 3.3 %collective-permute-done.35.refs_1_ = bf16[16,3584]{1,0:T(8,128)(2,1)S(1)} collective-permute-done((bf16[16,3584]{1,0:T(8,128)(2,1)S(1)}, bf16[16,3584]{1,0:T(8,128)(2,1)S(1)}, u32[]{:S(2)}, u32[]{:S(2)}) %collective-permute-start.35) | collective-permute-done | bytes 114720 | tf_op jit(solution)/shard_map/ppermute | solution.py:34
  (127 shorter events, 67.9 us)
Async XLA Ops:
  3.7 89.7 %collective-permute-start.19 = (bf16[480,3584]{1,0:T(8,128)(2,1)}, bf16[480,3584]{1,0:T(8,128)(2,1)S(1)}, u32[]{:S(2)}, u32[]{:S(2)}) collective-permute-start(bf16[480,3584]{1,0:T(8,128)(2,1)} %shard_map.113), channel_id=1, source_target_pairs={{0,6},{6,0},{2,4},{4,2},{1,7},{7,1},{3,5},{5,3},{8,14},{14,8},{10,... | collective-permute-start | bytes 10321928 | tf_op jit(solution)/shard_map/ppermute | solution.py:357
  21.3 9.7 %collective-permute-start.4 = (bf16[512,256]{1,0:T(8,128)(2,1)S(1)}, bf16[512,256]{1,0:T(8,128)(2,1)S(1)}, u32[]{:S(2)}, u32[]{:S(2)}) collective-permute-start(bf16[512,256]{1,0:T(8,128)(2,1)S(1)} %constant_dynamic-update-slice_fusion.2.refs_0_), channel_id=1, source_target_pairs={{8,0},{16,8},{24,16},{32,24},{40,32},{48,40},{56,48},{0,56},{9,1},... | collective-permute-start | bytes 786440 | tf_op jit(solution)/shard_map/ppermute | solution.py:34
  27.2 8.3 %collective-permute-start.7 = (bf16[512,256]{1,0:T(8,128)(2,1)S(1)}, bf16[512,256]{1,0:T(8,128)(2,1)S(1)}, u32[]{:S(2)}, u32[]{:S(2)}) collective-permute-start(bf16[512,256]{1,0:T(8,128)(2,1)S(1)} %constant_dynamic-update-slice_fusion.2.refs_0_), channel_id=1, source_target_pairs={{56,0},{0,8},{8,16},{16,24},{24,32},{32,40},{40,48},{48,56},{57,1}... | collective-permute-start | bytes 786440 | tf_op jit(solution)/shard_map/ppermute | solution.py:34
  31.1 8.1 %collective-permute-start.5 = (bf16[512,256]{1,0:T(8,128)(2,1)S(1)}, bf16[512,256]{1,0:T(8,128)(2,1)S(1)}, u32[]{:S(2)}, u32[]{:S(2)}) collective-permute-start(bf16[512,256]{1,0:T(8,128)(2,1)S(1)} %collective-permute-done.4.refs_1_), channel_id=1, source_target_pairs={{8,0},{16,8},{24,16},{32,24},{40,32},{48,40},{56,48},{0,56},{9,1},... | collective-permute-start | bytes 786440 | tf_op jit(solution)/shard_map/ppermute | solution.py:34
  35.5 8.4 %collective-permute-start.8 = (bf16[512,256]{1,0:T(8,128)(2,1)S(1)}, bf16[512,256]{1,0:T(8,128)(2,1)S(1)}, u32[]{:S(2)}, u32[]{:S(2)}) collective-permute-start(bf16[512,256]{1,0:T(8,128)(2,1)S(1)} %collective-permute-done.7.refs_6_), channel_id=1, source_target_pairs={{56,0},{0,8},{8,16},{16,24},{24,32},{32,40},{40,48},{48,56},{57,1}... | collective-permute-start | bytes 786440 | tf_op jit(solution)/shard_map/ppermute | solution.py:34
  39.2 7.6 %collective-permute-start.6 = (bf16[512,256]{1,0:T(8,128)(2,1)S(1)}, bf16[512,256]{1,0:T(8,128)(2,1)S(1)}, u32[]{:S(2)}, u32[]{:S(2)}) collective-permute-start(bf16[512,256]{1,0:T(8,128)(2,1)S(1)} %collective-permute-done.5.refs_2_), channel_id=1, source_target_pairs={{8,0},{16,8},{24,16},{32,24},{40,32},{48,40},{56,48},{0,56},{9,1},... | collective-permute-start | bytes 786440 | tf_op jit(solution)/shard_map/ppermute | solution.py:34
  43.9 7.9 %collective-permute-start.9 = (bf16[512,256]{1,0:T(8,128)(2,1)S(1)}, bf16[512,256]{1,0:T(8,128)(2,1)S(1)}, u32[]{:S(2)}, u32[]{:S(2)}) collective-permute-start(bf16[512,256]{1,0:T(8,128)(2,1)S(1)} %collective-permute-done.8.refs_5_), channel_id=1, source_target_pairs={{56,0},{0,8},{8,16},{16,24},{24,32},{32,40},{40,48},{48,56},{57,1}... | collective-permute-start | bytes 786440 | tf_op jit(solution)/shard_map/ppermute | solution.py:34
  86.0 7.4 %collective-permute-start.16 = (bf16[16,3584]{1,0:T(8,128)(2,1)S(1)}, bf16[16,3584]{1,0:T(8,128)(2,1)S(1)}, u32[]{:S(2)}, u32[]{:S(2)}) collective-permute-start(bf16[16,3584]{1,0:T(8,128)(2,1)S(1)} %get-tuple-element.32.refs_0_), channel_id=1, source_target_pairs={{192,0},{0,64},{64,128},{128,192},{193,1},{1,65},{65,129},{129,193... | collective-permute-start | bytes 344072 | tf_op jit(solution)/shard_map/ppermute | solution.py:34
  93.4 40.8 %collective-permute-start.20 = (bf16[480,3584]{1,0:T(8,128)(2,1)S(1)}, bf16[480,3584]{1,0:T(8,128)(2,1)S(1)}, u32[]{:S(2)}, u32[]{:S(2)}) collective-permute-start(bf16[480,3584]{1,0:T(8,128)(2,1)S(1)} %collective-permute-done.19.a_any), channel_id=1, source_target_pairs={{1,0},{0,1},{3,2},{2,3},{5,4},{4,5},{7,6},{6,7},{9,8},{8,9},{11,10... | collective-permute-start | bytes 10321928 | tf_op jit(solution)/shard_map/ppermute | solution.py:34
  93.5 12.9 %collective-permute-start.17 = (bf16[64,3584]{1,0:T(8,128)(2,1)S(1)}, bf16[64,3584]{1,0:T(8,128)(2,1)S(1)}, u32[]{:S(2)}, u32[]{:S(2)}) collective-permute-start(bf16[64,3584]{1,0:T(8,128)(2,1)S(1)} %shard_map.112.refs_0_), channel_id=1, source_target_pairs={{8,0},{16,8},{24,16},{32,24},{40,32},{48,40},{56,48},{0,56},{9,1},... | collective-permute-start | bytes 1376264 | tf_op jit(solution)/shard_map/ppermute | solution.py:34
  93.6 14.3 %collective-permute-start.18 = (bf16[64,3584]{1,0:T(8,128)(2,1)S(1)}, bf16[64,3584]{1,0:T(8,128)(2,1)S(1)}, u32[]{:S(2)}, u32[]{:S(2)}) collective-permute-start(bf16[64,3584]{1,0:T(8,128)(2,1)S(1)} %shard_map.112.refs_0_), channel_id=1, source_target_pairs={{56,0},{0,8},{8,16},{16,24},{24,32},{32,40},{40,48},{48,56},{57,1}... | collective-permute-start | bytes 1376264 | tf_op jit(solution)/shard_map/ppermute | solution.py:34
  106.5 12.1 %collective-permute-start.21 = (bf16[64,3584]{1,0:T(8,128)(2,1)S(1)}, bf16[64,3584]{1,0:T(8,128)(2,1)S(1)}, u32[]{:S(2)}, u32[]{:S(2)}) collective-permute-start(bf16[64,3584]{1,0:T(8,128)(2,1)S(1)} %collective-permute-done.17.refs_1_), channel_id=1, source_target_pairs={{8,0},{16,8},{24,16},{32,24},{40,32},{48,40},{56,48},{0,56},{9,1},... | collective-permute-start | bytes 1376264 | tf_op jit(solution)/shard_map/ppermute | solution.py:34
  108.0 13.5 %collective-permute-start.22 = (bf16[64,3584]{1,0:T(8,128)(2,1)S(1)}, bf16[64,3584]{1,0:T(8,128)(2,1)S(1)}, u32[]{:S(2)}, u32[]{:S(2)}) collective-permute-start(bf16[64,3584]{1,0:T(8,128)(2,1)S(1)} %collective-permute-done.18.refs_2_), channel_id=1, source_target_pairs={{56,0},{0,8},{8,16},{16,24},{24,32},{32,40},{40,48},{48,56},{57,1}... | collective-permute-start | bytes 1376264 | tf_op jit(solution)/shard_map/ppermute | solution.py:34
  118.6 11.8 %collective-permute-start.23 = (bf16[64,3584]{1,0:T(8,128)(2,1)S(1)}, bf16[64,3584]{1,0:T(8,128)(2,1)S(1)}, u32[]{:S(2)}, u32[]{:S(2)}) collective-permute-start(bf16[64,3584]{1,0:T(8,128)(2,1)S(1)} %collective-permute-done.21.refs_0_), channel_id=1, source_target_pairs={{8,0},{16,8},{24,16},{32,24},{40,32},{48,40},{56,48},{0,56},{9,1},... | collective-permute-start | bytes 1376264 | tf_op jit(solution)/shard_map/ppermute | solution.py:34
  121.4 12.7 %collective-permute-start.24 = (bf16[64,3584]{1,0:T(8,128)(2,1)S(1)}, bf16[64,3584]{1,0:T(8,128)(2,1)S(1)}, u32[]{:S(2)}, u32[]{:S(2)}) collective-permute-start(bf16[64,3584]{1,0:T(8,128)(2,1)S(1)} %collective-permute-done.22.refs_1_), channel_id=1, source_target_pairs={{56,0},{0,8},{8,16},{16,24},{24,32},{32,40},{40,48},{48,56},{57,1}... | collective-permute-start | bytes 1376264 | tf_op jit(solution)/shard_map/ppermute | solution.py:34
  130.4 8.5 %collective-permute-start.25 = (bf16[32,3584]{1,0:T(8,128)(2,1)S(1)}, bf16[32,3584]{1,0:T(8,128)(2,1)S(1)}, u32[]{:S(2)}, u32[]{:S(2)}) collective-permute-start(bf16[32,3584]{1,0:T(8,128)(2,1)S(1)} %slice.18), channel_id=1, source_target_pairs={{8,0},{16,8},{24,16},{32,24},{40,32},{48,40},{56,48},{0,56},{9,1},... | collective-permute-start | bytes 688136 | tf_op jit(solution)/shard_map/ppermute | solution.py:34
  146.6 8.3 %collective-permute-start.31 = (bf16[32,3584]{1,0:T(8,128)(2,1)S(1)}, bf16[32,3584]{1,0:T(8,128)(2,1)S(1)}, u32[]{:S(2)}, u32[]{:S(2)}) collective-permute-start(bf16[32,3584]{1,0:T(8,128)(2,1)S(1)} %get-tuple-element.44), channel_id=1, source_target_pairs={{8,0},{16,8},{24,16},{32,24},{40,32},{48,40},{56,48},{0,56},{9,1},... | collective-permute-start | bytes 688136 | tf_op jit(solution)/shard_map/ppermute | solution.py:34
  147.3 9.6 %collective-permute-start.27 = (bf16[32,3584]{1,0:T(8,128)(2,1)S(1)}, bf16[32,3584]{1,0:T(8,128)(2,1)S(1)}, u32[]{:S(2)}, u32[]{:S(2)}) collective-permute-start(bf16[32,3584]{1,0:T(8,128)(2,1)S(1)} %get-tuple-element.40), channel_id=1, source_target_pairs={{56,0},{0,8},{8,16},{16,24},{24,32},{32,40},{40,48},{48,56},{57,1}... | collective-permute-start | bytes 688136 | tf_op jit(solution)/shard_map/ppermute | solution.py:34
  155.0 9.6 %collective-permute-start.32 = (bf16[64,3584]{1,0:T(8,128)(2,1)S(1)}, bf16[64,3584]{1,0:T(8,128)(2,1)S(1)}, u32[]{:S(2)}, u32[]{:S(2)}) collective-permute-start(bf16[64,3584]{1,0:T(8,128)(2,1)S(1)} %shard_map.121), channel_id=1, source_target_pairs={{8,0},{16,8},{24,16},{32,24},{40,32},{48,40},{56,48},{0,56},{9,1},... | collective-permute-start | bytes 1376264 | tf_op jit(solution)/shard_map/ppermute | solution.py:34
  156.9 10.7 %collective-permute-start.28 = (bf16[64,3584]{1,0:T(8,128)(2,1)S(1)}, bf16[64,3584]{1,0:T(8,128)(2,1)S(1)}, u32[]{:S(2)}, u32[]{:S(2)}) collective-permute-start(bf16[64,3584]{1,0:T(8,128)(2,1)S(1)} %shard_map.118), channel_id=1, source_target_pairs={{56,0},{0,8},{8,16},{16,24},{24,32},{32,40},{40,48},{48,56},{57,1}... | collective-permute-start | bytes 1376264 | tf_op jit(solution)/shard_map/ppermute | solution.py:34
  164.6 9.6 %collective-permute-start.33 = (bf16[64,3584]{1,0:T(8,128)(2,1)S(1)}, bf16[64,3584]{1,0:T(8,128)(2,1)S(1)}, u32[]{:S(2)}, u32[]{:S(2)}) collective-permute-start(bf16[64,3584]{1,0:T(8,128)(2,1)S(1)} %shard_map.122), channel_id=1, source_target_pairs={{8,0},{16,8},{24,16},{32,24},{40,32},{48,40},{56,48},{0,56},{9,1},... | collective-permute-start | bytes 1376264 | tf_op jit(solution)/shard_map/ppermute | solution.py:34
  167.7 10.7 %collective-permute-start.29 = (bf16[64,3584]{1,0:T(8,128)(2,1)S(1)}, bf16[64,3584]{1,0:T(8,128)(2,1)S(1)}, u32[]{:S(2)}, u32[]{:S(2)}) collective-permute-start(bf16[64,3584]{1,0:T(8,128)(2,1)S(1)} %shard_map.119), channel_id=1, source_target_pairs={{56,0},{0,8},{8,16},{16,24},{24,32},{32,40},{40,48},{48,56},{57,1}... | collective-permute-start | bytes 1376264 | tf_op jit(solution)/shard_map/ppermute | solution.py:34
  174.3 9.7 %collective-permute-start.34 = (bf16[64,3584]{1,0:T(8,128)(2,1)S(1)}, bf16[64,3584]{1,0:T(8,128)(2,1)S(1)}, u32[]{:S(2)}, u32[]{:S(2)}) collective-permute-start(bf16[64,3584]{1,0:T(8,128)(2,1)S(1)} %shard_map.123), channel_id=1, source_target_pairs={{8,0},{16,8},{24,16},{32,24},{40,32},{48,40},{56,48},{0,56},{9,1},... | collective-permute-start | bytes 1376264 | tf_op jit(solution)/shard_map/ppermute | solution.py:34
  178.5 9.8 %collective-permute-start.30 = (bf16[64,3584]{1,0:T(8,128)(2,1)S(1)}, bf16[64,3584]{1,0:T(8,128)(2,1)S(1)}, u32[]{:S(2)}, u32[]{:S(2)}) collective-permute-start(bf16[64,3584]{1,0:T(8,128)(2,1)S(1)} %shard_map.120), channel_id=1, source_target_pairs={{56,0},{0,8},{8,16},{16,24},{24,32},{32,40},{40,48},{48,56},{57,1}... | collective-permute-start | bytes 1376264 | tf_op jit(solution)/shard_map/ppermute | solution.py:34
  (36 other events, 400.4 us)
where the time goes:
time: 199 us; the launch traced here: 197 us
  waiting for transfers between devices  90.1 us (45%)
  starting transfers between devices  55.3 us (28%)
  Pallas kernels  37.2 us (19%)
  local copies, waits for them, and re-layouts  14.4 us (7%)
    ppermute x37, waiting for transfers between devices, fetch(): return lax.ppermute(x, axis, [((i + k) % n, i) for i in range(n)])  90.1 us
    ppermute x37, starting transfers between devices, fetch(): return lax.ppermute(x, axis, [((i + k) % n, i) for i in range(n)])  54.2 us
    pallas_call x3, Pallas kernels, expert(): pl.pallas_call(functools.partial(expert_kernel, len(xs)), out_shape=[jax....  17.4 us
    unnamed x48, local copies, waits for them, and re-layouts  12.3 us
    pallas_call x1, Pallas kernels, per_device(): pl.pallas_call(attention_kernel, out_shape=[jax.ShapeDtypeStruct((half, w...  9.01 us
    pallas_call x1, Pallas kernels, per_device(): pl.pallas_call(assemble_kernel, out_shape=[jax.ShapeDtypeStruct((4 * hidd...  4.53 us
  transfers between devices with their start and end apart: 38, of which 26 were waited for; matrix products, arithmetic and copies ran while one was open for 1% of the time, Pallas kernels for 14%

commit v1 on v0

--- a/solution.py
+++ b/solution.py
@@ -45,9 +45,12 @@
     for k in range(1, h):
         ahead.append(fetch(ahead[-1], axis, 1))
         behind.append(fetch(behind[-1], axis, -1))
-    rows = x.shape[0] // 2
-    far = [fetch(ahead[-1][:rows], axis, 1), fetch(behind[-1][rows:], axis, -1)]
-    return ahead, behind, far
+    return ahead, behind
+
+
+def gather_far(ahead, behind, axis):
+    rows = ahead.shape[0] // 2
+    return [fetch(ahead[:rows], axis, 1), fetch(behind[rows:], axis, -1)]
 
 
 def add_kernel(n_in, first, *refs):
@@ -344,6 +347,10 @@
 
     gate_t, up_t = gate_weight.T, up_weight.T
     piece = hidden // 2
+    kv = jnp.concatenate([keys, values], axis=1)
+    kv = jnp.concatenate([kv, fetch(kv, "xh", 1)], axis=0)
+    core_at, _ = lax.optimization_barrier((core.astype(jnp.int32)[None], kv))
+
     to_send = pl.pallas_call(
         send_kernel,
         out_shape=jax.ShapeDtypeStruct((3 * piece, width), bf16),
@@ -353,13 +360,12 @@
         cost_estimate=pl.CostEstimate(
             flops=0, bytes_accessed=12 * piece * width, transcendentals=0
         ),
-    )(core.astype(jnp.int32)[None], gate_t, up_t, down_weight)
+    )(core_at, gate_t, up_t, down_weight)
     swap_a = lax.ppermute(to_send, ("xh", "xl"), [(0, 3), (3, 0), (1, 2), (2, 1)])
 
-    kv = jnp.concatenate([keys, values], axis=1)
-    kv = jnp.concatenate([kv, fetch(kv, "xh", 1)], axis=0)
     kv = jnp.concatenate(gather_direct(kv, "y"), axis=0)
-    ahead, behind, far = gather_ring(kv, "z")
+    ahead, behind = gather_ring(kv, "z")
+    far = gather_far(ahead[3], behind[3], "z")
     kvs = ahead + behind[:0:-1] + far
     at = jnp.stack([y, z, xh, t]).astype(jnp.int32)
 
@@ -404,8 +410,8 @@
     )(keep, near, beyond, residual, norm_gain[None, :], gate_logit_weight[None, :])
 
     by_y = join(gather_direct(normed, "y"))
-    ahead, behind, far = gather_ring(by_y, "z")
-    swap_a, _ = lax.optimization_barrier((swap_a, by_y))
+    ahead, behind = gather_ring(by_y, "z")
+    swap_a, _ = lax.optimization_barrier((swap_a, ahead[1]))
     swap_b = fetch(swap_a, "core", 1)
     weights = pl.pallas_call(
         assemble_kernel,
@@ -421,8 +427,12 @@
             flops=0, bytes_accessed=12 * hidden * width, transcendentals=0
         ),
     )(gate_t, up_t, down_weight, swap_a, swap_b)
+    ahead_3, behind_3, weights = lax.optimization_barrier((ahead[3], behind[3], weights))
+    far = gather_far(ahead_3, behind_3, "z")
     own, after, before = expert([ahead[0], ahead[1], behind[1]], weights)
-    after_2, before_2, after_3, before_3 = expert([ahead[2], behind[2], ahead[3], behind[3]], weights)
+    after_2, before_2, after_3, before_3 = expert(
+        [ahead[2], behind[2], ahead[3], behind[3]], weights
+    )
     far_parts = expert(far, weights)
     near_parts = [own, after, after_2, after_3, None, before_3, before_2, before]
     by_y = add(scatter_ring(near_parts, far_parts, "z"), pieces=4)

time: 199 us -> 202 us (1.015)
  waiting for transfers between devices: 90.1 us -> 111 us
  local copies, waits for them, and re-layouts: 14.4 us -> 3.12 us
  starting transfers between devices: 55.3 us -> 49.9 us
    ppermute x37, waiting for transfers between devices: 90.1 us -> 111 us  [fetch(): return lax.ppermute(x, axis, [((i + k) % n, i) for i in range(n)])]
    unnamed x48 -> x20, local copies, waits for them, and re-layouts: 12.3 us -> 2.31 us
    ppermute x37, starting transfers between devices: 54.2 us -> 48.8 us  [fetch(): return lax.ppermute(x, axis, [((i + k) % n, i) for i in range(n)])]
  transfers between devices with their start and end apart: 38 -> 38, of which waited for: 26 -> 30; matrix products, arithmetic and copies ran while one was open for 1% -> 0% of each run, Pallas kernels for 14% -> 13%
where the time goes in v1:
time: 202 us; the launch traced here: 201 us
  waiting for transfers between devices  111 us (55%)
  starting transfers between devices  49.9 us (25%)
  Pallas kernels  36.2 us (18%)
  local copies, waits for them, and re-layouts  3.12 us (2%)
    ppermute x37, waiting for transfers between devices, fetch(): return lax.ppermute(x, axis, [((i + k) % n, i) for i in range(n)])  111 us
    ppermute x37, starting transfers between devices, fetch(): return lax.ppermute(x, axis, [((i + k) % n, i) for i in range(n)])  48.8 us
    pallas_call x3, Pallas kernels, expert(): pl.pallas_call(functools.partial(expert_kernel, len(xs)), out_shape=[jax....  17.4 us
    pallas_call x1, Pallas kernels, per_device(): pl.pallas_call(attention_kernel, out_shape=[jax.ShapeDtypeStruct((half, w...  8.12 us
    pallas_call x1, Pallas kernels, per_device(): pl.pallas_call(assemble_kernel, out_shape=[jax.ShapeDtypeStruct((4 * hidd...  4.42 us
  transfers between devices with their start and end apart: 38, of which 30 were waited for; matrix products, arithmetic and copies ran while one was open for 0% of the time, Pallas kernels for 13%

profile of v1, /device:TPU:0, one launch (start us, length us, event | category | flops | bytes accessed | tf_op | source)
XLA Modules:
  0.0 201.0 jit_solution(15605318549337894684)
XLA Ops:
  2.8 4.1 %collective-permute-done = bf16[64,256]{1,0:T(8,128)(2,1)S(1)} collective-permute-done((bf16[64,256]{1,0:T(8,128)(2,1)S(1)}, bf16[64,256]{1,0:T(8,128)(2,1)S(1)}, u32[]{:S(2)}, u32[]{:S(2)}) %collective-permute-start) | collective-permute-done | bytes 32800 | tf_op jit(solution)/shard_map/ppermute | solution.py:34
  7.0 3.7 %shard_map.113 = bf16[480,3584]{1,0:T(8,128)(2,1)} custom-call(s32[1]{0:T(128)} %bitcast.6.core_ref, bf16[320,3584]{1,0:T(8,128)(2,1)} %bitcast.7, bf16[320,3584]{1,0:T(8,128)(2,1)} %bitcast.9, bf16[320,3584]{1,0:T(8,128)(2,1)} %d_any.3), custom_call_target="tpu_custom_call" | custom-call | bytes 6881280 | tf_op jit(solution)/shard_map/pallas_call | solution.py:354
  16.7 3.9 %collective-permute-done.2 = bf16[128,256]{1,0:T(8,128)(2,1)S(1)} collective-permute-done((bf16[128,256]{1,0:T(8,128)(2,1)S(1)}, bf16[128,256]{1,0:T(8,128)(2,1)S(1)}, u32[]{:S(2)}, u32[]{:S(2)}) %collective-permute-start.2) | collective-permute-done | bytes 65568 | tf_op jit(solution)/shard_map/ppermute | solution.py:34
  21.3 5.9 %collective-permute-start.4 = (bf16[512,256]{1,0:T(8,128)(2,1)S(1)}, bf16[512,256]{1,0:T(8,128)(2,1)S(1)}, u32[]{:S(2)}, u32[]{:S(2)}) collective-permute-start(bf16[512,256]{1,0:T(8,128)(2,1)S(1)} %constant_dynamic-update-slice_fusion.2.refs_0_), channel_id=1, source_target_pairs={{8,0},{16,8},{24,16},{32,24},{40,32},{48,40},{56,48},{0,56},{9,1},... | collective-permute-start | bytes 786440 | tf_op jit(solution)/shard_map/ppermute | solution.py:34
  27.1 3.9 %collective-permute-done.4.refs_1_ = bf16[512,256]{1,0:T(8,128)(2,1)S(1)} collective-permute-done((bf16[512,256]{1,0:T(8,128)(2,1)S(1)}, bf16[512,256]{1,0:T(8,128)(2,1)S(1)}, u32[]{:S(2)}, u32[]{:S(2)}) %collective-permute-start.4) | collective-permute-done | bytes 262176 | tf_op jit(solution)/shard_map/ppermute | solution.py:34
  31.0 3.7 %collective-permute-start.5 = (bf16[512,256]{1,0:T(8,128)(2,1)S(1)}, bf16[512,256]{1,0:T(8,128)(2,1)S(1)}, u32[]{:S(2)}, u32[]{:S(2)}) collective-permute-start(bf16[512,256]{1,0:T(8,128)(2,1)S(1)} %collective-permute-done.4.refs_1_), channel_id=1, source_target_pairs={{8,0},{16,8},{24,16},{32,24},{40,32},{48,40},{56,48},{0,56},{9,1},... | collective-permute-start | bytes 786440 | tf_op jit(solution)/shard_map/ppermute | solution.py:34
  34.7 4.1 %collective-permute-done.5.refs_2_ = bf16[512,256]{1,0:T(8,128)(2,1)S(1)} collective-permute-done((bf16[512,256]{1,0:T(8,128)(2,1)S(1)}, bf16[512,256]{1,0:T(8,128)(2,1)S(1)}, u32[]{:S(2)}, u32[]{:S(2)}) %collective-permute-start.5) | collective-permute-done | bytes 262176 | tf_op jit(solution)/shard_map/ppermute | solution.py:34
  38.9 3.7 %collective-permute-start.6 = (bf16[512,256]{1,0:T(8,128)(2,1)S(1)}, bf16[512,256]{1,0:T(8,128)(2,1)S(1)}, u32[]{:S(2)}, u32[]{:S(2)}) collective-permute-start(bf16[512,256]{1,0:T(8,128)(2,1)S(1)} %collective-permute-done.5.refs_2_), channel_id=1, source_target_pairs={{8,0},{16,8},{24,16},{32,24},{40,32},{48,40},{56,48},{0,56},{9,1},... | collective-permute-start | bytes 786440 | tf_op jit(solution)/shard_map/ppermute | solution.py:34
  42.8 4.4 %collective-permute-done.6.refs_3_ = bf16[512,256]{1,0:T(8,128)(2,1)S(1)} collective-permute-done((bf16[512,256]{1,0:T(8,128)(2,1)S(1)}, bf16[512,256]{1,0:T(8,128)(2,1)S(1)}, u32[]{:S(2)}, u32[]{:S(2)}) %collective-permute-start.6) | collective-permute-done | bytes 262176 | tf_op jit(solution)/shard_map/ppermute | solution.py:34
  47.3 3.8 %collective-permute-start.10 = (bf16[256,256]{1,0:T(8,128)(2,1)S(1)}, bf16[256,256]{1,0:T(8,128)(2,1)S(1)}, u32[]{:S(2)}, u32[]{:S(2)}) collective-permute-start(bf16[256,256]{1,0:T(8,128)(2,1)S(1)} %slice.16), channel_id=1, source_target_pairs={{8,0},{16,8},{24,16},{32,24},{40,32},{48,40},{56,48},{0,56},{9,1},... | collective-permute-start | bytes 393224 | tf_op jit(solution)/shard_map/ppermute | solution.py:34
  53.6 4.2 %collective-permute-done.11.refs_8_ = bf16[256,256]{1,0:T(8,128)(2,1)S(1)} collective-permute-done((bf16[256,256]{1,0:T(8,128)(2,1)S(1)}, bf16[256,256]{1,0:T(8,128)(2,1)S(1)}, u32[]{:S(2)}, u32[]{:S(2)}) %collective-permute-start.11) | collective-permute-done | bytes 131104 | tf_op jit(solution)/shard_map/ppermute | solution.py:34
  59.4 8.1 %shard_map.109 = (bf16[32,3584]{1,0:T(8,128)(2,1)S(1)}, bf16[32,3584]{1,0:T(8,128)(2,1)S(1)}) custom-call(s32[4]{0:T(128)S(1)} %pad_add_fusion.at_ref, s32[64]{0:T(128)S(1)} %copy-done.5, bf16[64,896]{1,0:T(8,128)(2,1)S(1)} %copy-done.3, bf16[512,256]{1,0:T(8,128)(2,1)S(1)} %constant_dynamic-update-slice_fusion.2.refs_0_, ...), custom_call_target="tpu_custom_call" | custom-call | flops 1350565888 | bytes 8519680 | tf_op jit(solution)/shard_map/pallas_call | solution.py:374
  85.0 12.4 %collective-permute-done.17.refs_1_ = bf16[64,3584]{1,0:T(8,128)(2,1)S(1)} collective-permute-done((bf16[64,3584]{1,0:T(8,128)(2,1)S(1)}, bf16[64,3584]{1,0:T(8,128)(2,1)S(1)}, u32[]{:S(2)}, u32[]{:S(2)}) %collective-permute-start.17) | collective-permute-done | bytes 458784 | tf_op jit(solution)/shard_map/ppermute | solution.py:34
  100.7 10.9 %collective-permute-done.18.refs_2_ = bf16[64,3584]{1,0:T(8,128)(2,1)S(1)} collective-permute-done((bf16[64,3584]{1,0:T(8,128)(2,1)S(1)}, bf16[64,3584]{1,0:T(8,128)(2,1)S(1)}, u32[]{:S(2)}, u32[]{:S(2)}) %collective-permute-start.18) | collective-permute-done | bytes 458784 | tf_op jit(solution)/shard_map/ppermute | solution.py:34
  114.8 10.1 %collective-permute-done.21.refs_1_ = bf16[64,3584]{1,0:T(8,128)(2,1)S(1)} collective-permute-done((bf16[64,3584]{1,0:T(8,128)(2,1)S(1)}, bf16[64,3584]{1,0:T(8,128)(2,1)S(1)}, u32[]{:S(2)}, u32[]{:S(2)}) %collective-permute-start.21) | collective-permute-done | bytes 458784 | tf_op jit(solution)/shard_map/ppermute | solution.py:34
  125.0 4.4 %shard_map.114 = (bf16[1280,3584]{1,0:T(8,128)(2,1)S(1)}, bf16[640,3584]{1,0:T(8,128)(2,1)S(1)}) custom-call(bf16[320,3584]{1,0:T(8,128)(2,1)S(1)} %bitcast.8, bf16[320,3584]{1,0:T(8,128)(2,1)S(1)} %bitcast.10, bf16[320,3584]{1,0:T(8,128)(2,1)S(1)} %copy-done.2, bf16[480,3584]{1,0:T(8,128)(2,1)} %collective-permute-done.23.a_any, ...), custom_call_target="tpu_custom_call" | custom-call | bytes 13762560 | tf_op jit(solution)/shard_map/pallas_call | solution.py:416
  129.4 8.0 %collective-permute-done.22.refs_3_ = bf16[64,3584]{1,0:T(8,128)(2,1)S(1)} collective-permute-done((bf16[64,3584]{1,0:T(8,128)(2,1)S(1)}, bf16[64,3584]{1,0:T(8,128)(2,1)S(1)}, u32[]{:S(2)}, u32[]{:S(2)}) %collective-permute-start.22) | collective-permute-done | bytes 458784 | tf_op jit(solution)/shard_map/ppermute | solution.py:34
  139.6 3.9 %collective-permute-done.25.refs_0_ = bf16[32,3584]{1,0:T(8,128)(2,1)S(1)} collective-permute-done((bf16[32,3584]{1,0:T(8,128)(2,1)S(1)}, bf16[32,3584]{1,0:T(8,128)(2,1)S(1)}, u32[]{:S(2)}, u32[]{:S(2)}) %collective-permute-start.25) | collective-permute-done | bytes 229408 | tf_op jit(solution)/shard_map/ppermute | solution.py:34
  144.8 5.1 %shard_map.117 = (bf16[32,3584]{1,0:T(8,128)(2,1)S(1)}, bf16[32,3584]{1,0:T(8,128)(2,1)S(1)}) custom-call(bf16[32,3584]{1,0:T(8,128)(2,1)S(1)} %collective-permute-done.25.refs_0_, bf16[32,3584]{1,0:T(8,128)(2,1)S(1)} %collective-permute-done.26.refs_1_, bf16[1280,3584]{1,0:T(8,128)(2,1)S(1)} %get-tuple-element.42.refs_3_.refs_4_.refs_2_, ...), custom_call_target="tpu_custom_call" | custom-call | flops 880803840 | bytes 14680064 | tf_op jit(solution)/shard_map/pallas_call | solution.py:303
  152.1 6.2 %shard_map.116 = (bf16[64,3584]{1,0:T(8,128)(2,1)S(1)}, bf16[64,3584]{1,0:T(8,128)(2,1)S(1)}, bf16[64,3584]{1,0:T(8,128)(2,1)S(1)}, bf16[64,3584]{1,0:T(8,128)(2,1)S(1)}) custom-call(bf16[64,3584]{1,0:T(8,128)(2,1)S(1)} %collective-permute-done.19.refs_0_, bf16[64,3584]{1,0:T(8,128)(2,1)S(1)} %collective-permute-done.21.refs_1_, ...), custom_call_target="tpu_custom_call" | custom-call | flops 3523215360 | bytes 17432576 | tf_op jit(solution)/shard_map/pallas_call | solution.py:303
  160.8 8.1 %collective-permute-done.32.refs_1_ = bf16[64,3584]{1,0:T(8,128)(2,1)S(1)} collective-permute-done((bf16[64,3584]{1,0:T(8,128)(2,1)S(1)}, bf16[64,3584]{1,0:T(8,128)(2,1)S(1)}, u32[]{:S(2)}, u32[]{:S(2)}) %collective-permute-start.32) | collective-permute-done | bytes 458784 | tf_op jit(solution)/shard_map/ppermute | solution.py:34
  171.3 6.2 %shard_map.115 = (bf16[64,3584]{1,0:T(8,128)(2,1)S(1)}, bf16[64,3584]{1,0:T(8,128)(2,1)S(1)}, bf16[64,3584]{1,0:T(8,128)(2,1)S(1)}) custom-call(bf16[64,3584]{1,0:T(8,128)(2,1)S(1)} %shard_map.112.refs_0_, bf16[64,3584]{1,0:T(8,128)(2,1)S(1)} %collective-permute-done.17.refs_1_, bf16[64,3584]{1,0:T(8,128)(2,1)S(1)} %collective-permute-done.18.refs_2_, ...), custom_call_target="tpu_custom_call" | custom-call | flops 2642411520 | bytes 16515072 | tf_op jit(solution)/shard_map/pallas_call | solution.py:303
  182.9 6.3 %collective-permute-done.34.refs_2_ = bf16[64,3584]{1,0:T(8,128)(2,1)S(1)} collective-permute-done((bf16[64,3584]{1,0:T(8,128)(2,1)S(1)}, bf16[64,3584]{1,0:T(8,128)(2,1)S(1)}, u32[]{:S(2)}, u32[]{:S(2)}) %collective-permute-start.34) | collective-permute-done | bytes 458784 | tf_op jit(solution)/shard_map/ppermute | solution.py:34
  195.4 4.0 %collective-permute-done.35.refs_1_ = bf16[16,3584]{1,0:T(8,128)(2,1)S(1)} collective-permute-done((bf16[16,3584]{1,0:T(8,128)(2,1)S(1)}, bf16[16,3584]{1,0:T(8,128)(2,1)S(1)}, u32[]{:S(2)}, u32[]{:S(2)}) %collective-permute-start.35) | collective-permute-done | bytes 114720 | tf_op jit(solution)/shard_map/ppermute | solution.py:34
  (99 shorter events, 61.7 us)
Async XLA Ops:
  10.7 86.7 %collective-permute-start.23 = (bf16[480,3584]{1,0:T(8,128)(2,1)}, bf16[480,3584]{1,0:T(8,128)(2,1)}, u32[]{:S(2)}, u32[]{:S(2)}) collective-permute-start(bf16[480,3584]{1,0:T(8,128)(2,1)} %shard_map.113), channel_id=1, source_target_pairs={{0,6},{6,0},{2,4},{4,2},{1,7},{7,1},{3,5},{5,3},{8,14},{14,8},{10,... | collective-permute-start | bytes 10321928 | tf_op jit(solution)/shard_map/ppermute | solution.py:364
  21.3 9.7 %collective-permute-start.4 = (bf16[512,256]{1,0:T(8,128)(2,1)S(1)}, bf16[512,256]{1,0:T(8,128)(2,1)S(1)}, u32[]{:S(2)}, u32[]{:S(2)}) collective-permute-start(bf16[512,256]{1,0:T(8,128)(2,1)S(1)} %constant_dynamic-update-slice_fusion.2.refs_0_), channel_id=1, source_target_pairs={{8,0},{16,8},{24,16},{32,24},{40,32},{48,40},{56,48},{0,56},{9,1},... | collective-permute-start | bytes 786440 | tf_op jit(solution)/shard_map/ppermute | solution.py:34
  27.1 7.6 %collective-permute-start.7 = (bf16[512,256]{1,0:T(8,128)(2,1)S(1)}, bf16[512,256]{1,0:T(8,128)(2,1)S(1)}, u32[]{:S(2)}, u32[]{:S(2)}) collective-permute-start(bf16[512,256]{1,0:T(8,128)(2,1)S(1)} %constant_dynamic-update-slice_fusion.2.refs_0_), channel_id=1, source_target_pairs={{56,0},{0,8},{8,16},{16,24},{24,32},{32,40},{40,48},{48,56},{57,1}... | collective-permute-start | bytes 786440 | tf_op jit(solution)/shard_map/ppermute | solution.py:34
  31.0 7.8 %collective-permute-start.5 = (bf16[512,256]{1,0:T(8,128)(2,1)S(1)}, bf16[512,256]{1,0:T(8,128)(2,1)S(1)}, u32[]{:S(2)}, u32[]{:S(2)}) collective-permute-start(bf16[512,256]{1,0:T(8,128)(2,1)S(1)} %collective-permute-done.4.refs_1_), channel_id=1, source_target_pairs={{8,0},{16,8},{24,16},{32,24},{40,32},{48,40},{56,48},{0,56},{9,1},... | collective-permute-start | bytes 786440 | tf_op jit(solution)/shard_map/ppermute | solution.py:34
  34.7 8.1 %collective-permute-start.8 = (bf16[512,256]{1,0:T(8,128)(2,1)S(1)}, bf16[512,256]{1,0:T(8,128)(2,1)S(1)}, u32[]{:S(2)}, u32[]{:S(2)}) collective-permute-start(bf16[512,256]{1,0:T(8,128)(2,1)S(1)} %collective-permute-done.7.refs_6_), channel_id=1, source_target_pairs={{56,0},{0,8},{8,16},{16,24},{24,32},{32,40},{40,48},{48,56},{57,1}... | collective-permute-start | bytes 786440 | tf_op jit(solution)/shard_map/ppermute | solution.py:34
  38.9 8.4 %collective-permute-start.6 = (bf16[512,256]{1,0:T(8,128)(2,1)S(1)}, bf16[512,256]{1,0:T(8,128)(2,1)S(1)}, u32[]{:S(2)}, u32[]{:S(2)}) collective-permute-start(bf16[512,256]{1,0:T(8,128)(2,1)S(1)} %collective-permute-done.5.refs_2_), channel_id=1, source_target_pairs={{8,0},{16,8},{24,16},{32,24},{40,32},{48,40},{56,48},{0,56},{9,1},... | collective-permute-start | bytes 786440 | tf_op jit(solution)/shard_map/ppermute | solution.py:34
  42.8 8.7 %collective-permute-start.9 = (bf16[512,256]{1,0:T(8,128)(2,1)S(1)}, bf16[512,256]{1,0:T(8,128)(2,1)S(1)}, u32[]{:S(2)}, u32[]{:S(2)}) collective-permute-start(bf16[512,256]{1,0:T(8,128)(2,1)S(1)} %collective-permute-done.8.refs_5_), channel_id=1, source_target_pairs={{56,0},{0,8},{8,16},{16,24},{24,32},{32,40},{40,48},{48,56},{57,1}... | collective-permute-start | bytes 786440 | tf_op jit(solution)/shard_map/ppermute | solution.py:34
  77.4 7.5 %collective-permute-start.16 = (bf16[16,3584]{1,0:T(8,128)(2,1)S(1)}, bf16[16,3584]{1,0:T(8,128)(2,1)S(1)}, u32[]{:S(2)}, u32[]{:S(2)}) collective-permute-start(bf16[16,3584]{1,0:T(8,128)(2,1)S(1)} %get-tuple-element.37.refs_0_), channel_id=1, source_target_pairs={{192,0},{0,64},{64,128},{128,192},{193,1},{1,65},{65,129},{129,193... | collective-permute-start | bytes 344072 | tf_op jit(solution)/shard_map/ppermute | solution.py:34
  84.9 12.5 %collective-permute-start.17 = (bf16[64,3584]{1,0:T(8,128)(2,1)S(1)}, bf16[64,3584]{1,0:T(8,128)(2,1)S(1)}, u32[]{:S(2)}, u32[]{:S(2)}) collective-permute-start(bf16[64,3584]{1,0:T(8,128)(2,1)S(1)} %shard_map.112.refs_0_), channel_id=1, source_target_pairs={{8,0},{16,8},{24,16},{32,24},{40,32},{48,40},{56,48},{0,56},{9,1},... | collective-permute-start | bytes 1376264 | tf_op jit(solution)/shard_map/ppermute | solution.py:34
  97.4 27.5 %collective-permute-start.24 = (bf16[480,3584]{1,0:T(8,128)(2,1)}, bf16[480,3584]{1,0:T(8,128)(2,1)S(1)}, u32[]{:S(2)}, u32[]{:S(2)}) collective-permute-start(bf16[480,3584]{1,0:T(8,128)(2,1)} %collective-permute-done.23.a_any), channel_id=1, source_target_pairs={{1,0},{0,1},{3,2},{2,3},{5,4},{4,5},{7,6},{6,7},{9,8},{8,9},{11,10... | collective-permute-start | bytes 10321928 | tf_op jit(solution)/shard_map/ppermute | solution.py:34
  97.4 14.1 %collective-permute-start.18 = (bf16[64,3584]{1,0:T(8,128)(2,1)S(1)}, bf16[64,3584]{1,0:T(8,128)(2,1)S(1)}, u32[]{:S(2)}, u32[]{:S(2)}) collective-permute-start(bf16[64,3584]{1,0:T(8,128)(2,1)S(1)} %shard_map.112.refs_0_), channel_id=1, source_target_pairs={{56,0},{0,8},{8,16},{16,24},{24,32},{32,40},{40,48},{48,56},{57,1}... | collective-permute-start | bytes 1376264 | tf_op jit(solution)/shard_map/ppermute | solution.py:34
  97.4 14.1 %collective-permute-start.19 = (bf16[64,3584]{1,0:T(8,128)(2,1)S(1)}, bf16[64,3584]{1,0:T(8,128)(2,1)S(1)}, u32[]{:S(2)}, u32[]{:S(2)}) collective-permute-start(bf16[64,3584]{1,0:T(8,128)(2,1)S(1)} %collective-permute-done.17.refs_1_), channel_id=1, source_target_pairs={{8,0},{16,8},{24,16},{32,24},{40,32},{48,40},{56,48},{0,56},{9,1},... | collective-permute-start | bytes 1376264 | tf_op jit(solution)/shard_map/ppermute | solution.py:34
  111.6 13.4 %collective-permute-start.21 = (bf16[64,3584]{1,0:T(8,128)(2,1)S(1)}, bf16[64,3584]{1,0:T(8,128)(2,1)S(1)}, u32[]{:S(2)}, u32[]{:S(2)}) collective-permute-start(bf16[64,3584]{1,0:T(8,128)(2,1)S(1)} %collective-permute-done.18.refs_2_), channel_id=1, source_target_pairs={{56,0},{0,8},{8,16},{16,24},{24,32},{32,40},{40,48},{48,56},{57,1}... | collective-permute-start | bytes 1376264 | tf_op jit(solution)/shard_map/ppermute | solution.py:34
  111.6 17.8 %collective-permute-start.20 = (bf16[64,3584]{1,0:T(8,128)(2,1)S(1)}, bf16[64,3584]{1,0:T(8,128)(2,1)S(1)}, u32[]{:S(2)}, u32[]{:S(2)}) collective-permute-start(bf16[64,3584]{1,0:T(8,128)(2,1)S(1)} %collective-permute-done.19.refs_0_), channel_id=1, source_target_pairs={{8,0},{16,8},{24,16},{32,24},{40,32},{48,40},{56,48},{0,56},{9,1},... | collective-permute-start | bytes 1376264 | tf_op jit(solution)/shard_map/ppermute | solution.py:34
  124.9 12.5 %collective-permute-start.22 = (bf16[64,3584]{1,0:T(8,128)(2,1)S(1)}, bf16[64,3584]{1,0:T(8,128)(2,1)S(1)}, u32[]{:S(2)}, u32[]{:S(2)}) collective-permute-start(bf16[64,3584]{1,0:T(8,128)(2,1)S(1)} %collective-permute-done.21.refs_1_), channel_id=1, source_target_pairs={{56,0},{0,8},{8,16},{16,24},{24,32},{32,40},{40,48},{48,56},{57,1}... | collective-permute-start | bytes 1376264 | tf_op jit(solution)/shard_map/ppermute | solution.py:34
  137.5 7.3 %collective-permute-start.26 = (bf16[32,3584]{1,0:T(8,128)(2,1)S(1)}, bf16[32,3584]{1,0:T(8,128)(2,1)S(1)}, u32[]{:S(2)}, u32[]{:S(2)}) collective-permute-start(bf16[32,3584]{1,0:T(8,128)(2,1)S(1)} %slice.15), channel_id=1, source_target_pairs={{56,0},{0,8},{8,16},{16,24},{24,32},{32,40},{40,48},{48,56},{57,1}... | collective-permute-start | bytes 688136 | tf_op jit(solution)/shard_map/ppermute | solution.py:34
  150.0 8.3 %collective-permute-start.31 = (bf16[32,3584]{1,0:T(8,128)(2,1)S(1)}, bf16[32,3584]{1,0:T(8,128)(2,1)S(1)}, u32[]{:S(2)}, u32[]{:S(2)}) collective-permute-start(bf16[32,3584]{1,0:T(8,128)(2,1)S(1)} %get-tuple-element.54), channel_id=1, source_target_pairs={{8,0},{16,8},{24,16},{32,24},{40,32},{48,40},{56,48},{0,56},{9,1},... | collective-permute-start | bytes 688136 | tf_op jit(solution)/shard_map/ppermute | solution.py:34
  150.1 9.7 %collective-permute-start.27 = (bf16[32,3584]{1,0:T(8,128)(2,1)S(1)}, bf16[32,3584]{1,0:T(8,128)(2,1)S(1)}, u32[]{:S(2)}, u32[]{:S(2)}) collective-permute-start(bf16[32,3584]{1,0:T(8,128)(2,1)S(1)} %get-tuple-element.50), channel_id=1, source_target_pairs={{56,0},{0,8},{8,16},{16,24},{24,32},{32,40},{40,48},{48,56},{57,1}... | collective-permute-start | bytes 688136 | tf_op jit(solution)/shard_map/ppermute | solution.py:34
  158.3 10.6 %collective-permute-start.32 = (bf16[64,3584]{1,0:T(8,128)(2,1)S(1)}, bf16[64,3584]{1,0:T(8,128)(2,1)S(1)}, u32[]{:S(2)}, u32[]{:S(2)}) collective-permute-start(bf16[64,3584]{1,0:T(8,128)(2,1)S(1)} %shard_map.121), channel_id=1, source_target_pairs={{8,0},{16,8},{24,16},{32,24},{40,32},{48,40},{56,48},{0,56},{9,1},... | collective-permute-start | bytes 1376264 | tf_op jit(solution)/shard_map/ppermute | solution.py:34
  159.8 10.7 %collective-permute-start.28 = (bf16[64,3584]{1,0:T(8,128)(2,1)S(1)}, bf16[64,3584]{1,0:T(8,128)(2,1)S(1)}, u32[]{:S(2)}, u32[]{:S(2)}) collective-permute-start(bf16[64,3584]{1,0:T(8,128)(2,1)S(1)} %shard_map.118), channel_id=1, source_target_pairs={{56,0},{0,8},{8,16},{16,24},{24,32},{32,40},{40,48},{48,56},{57,1}... | collective-permute-start | bytes 1376264 | tf_op jit(solution)/shard_map/ppermute | solution.py:34
  169.0 11.5 %collective-permute-start.33 = (bf16[64,3584]{1,0:T(8,128)(2,1)S(1)}, bf16[64,3584]{1,0:T(8,128)(2,1)S(1)}, u32[]{:S(2)}, u32[]{:S(2)}) collective-permute-start(bf16[64,3584]{1,0:T(8,128)(2,1)S(1)} %shard_map.122), channel_id=1, source_target_pairs={{8,0},{16,8},{24,16},{32,24},{40,32},{48,40},{56,48},{0,56},{9,1},... | collective-permute-start | bytes 1376264 | tf_op jit(solution)/shard_map/ppermute | solution.py:34
  170.6 11.4 %collective-permute-start.29 = (bf16[64,3584]{1,0:T(8,128)(2,1)S(1)}, bf16[64,3584]{1,0:T(8,128)(2,1)S(1)}, u32[]{:S(2)}, u32[]{:S(2)}) collective-permute-start(bf16[64,3584]{1,0:T(8,128)(2,1)S(1)} %shard_map.119), channel_id=1, source_target_pairs={{56,0},{0,8},{8,16},{16,24},{24,32},{32,40},{40,48},{48,56},{57,1}... | collective-permute-start | bytes 1376264 | tf_op jit(solution)/shard_map/ppermute | solution.py:34
  180.6 8.6 %collective-permute-start.34 = (bf16[64,3584]{1,0:T(8,128)(2,1)S(1)}, bf16[64,3584]{1,0:T(8,128)(2,1)S(1)}, u32[]{:S(2)}, u32[]{:S(2)}) collective-permute-start(bf16[64,3584]{1,0:T(8,128)(2,1)S(1)} %shard_map.123), channel_id=1, source_target_pairs={{8,0},{16,8},{24,16},{32,24},{40,32},{48,40},{56,48},{0,56},{9,1},... | collective-permute-start | bytes 1376264 | tf_op jit(solution)/shard_map/ppermute | solution.py:34
  182.1 9.8 %collective-permute-start.30 = (bf16[64,3584]{1,0:T(8,128)(2,1)S(1)}, bf16[64,3584]{1,0:T(8,128)(2,1)S(1)}, u32[]{:S(2)}, u32[]{:S(2)}) collective-permute-start(bf16[64,3584]{1,0:T(8,128)(2,1)S(1)} %shard_map.120), channel_id=1, source_target_pairs={{56,0},{0,8},{8,16},{16,24},{24,32},{32,40},{40,48},{48,56},{57,1}... | collective-permute-start | bytes 1376264 | tf_op jit(solution)/shard_map/ppermute | solution.py:34
  (22 other events, 345.4 us)

commit v2 on v1

--- a/solution.py
+++ b/solution.py
@@ -100,22 +100,12 @@
     return [near[0], up, down]
 
 
-def attention_kernel(at_ref, table_ref, q_ref, *refs):
-    kvs, w_any, keep_ref, send_ref = refs[:9], refs[9], refs[10], refs[11]
-    w_ref, kv_ref, q_all, kp_ref, sems = refs[12:]
-    half_rows = kvs[7].shape[0]
-    places = [kv_ref.at[j] for j in (0, 1, 2, 3, 5, 6, 7)]
-    places += [kv_ref.at[4, pl.ds(i * half_rows, half_rows)] for i in range(2)]
-    copies = [
-        pltpu.make_async_copy(src, dst, sems.at[i]) for i, (src, dst) in enumerate(zip(kvs, places))
-    ]
-    copy = pltpu.make_async_copy(w_any, w_ref, sems.at[9])
-    for one in copies:
-        one.start()
-    copy.start()
+def attend(at_ref, table_ref, q_all, kv_ref, kp_ref, steps, carry):
     y, z, xh, t = (at_ref[i] for i in range(4))
-    tokens = q_ref.shape[0]
+    count = kv_ref.shape[1]
+    tokens = count // 8
     half = tokens // 2
+    quarter = tokens // 4
     mirror = 2 * table_ref.shape[0] - 1
 
     def place(pair, local):
@@ -125,42 +115,28 @@
         slot = ((y + dy) % 4 * 8 + (z + dz) % 8) * 2 + (xh + dx) % 2
         return table_ref[slot]
 
-    lane = lax.broadcasted_iota(jnp.int32, (1, 8 * tokens), 1)
-    for j in range(8):
+    lane = lax.broadcasted_iota(jnp.int32, (1, count), 1)
+    for j, dz in enumerate(steps):
         pair = jnp.zeros_like(lane)
         for b in range(8):
-            pair = jnp.where(lane // tokens == b, pair_of(b // 2, j, b % 2), pair)
+            pair = jnp.where(lane // tokens == b, pair_of(b // 2, dz, b % 2), pair)
         kp_ref[j : j + 1, :] = place(pair, lane % tokens)
-    quarter = tokens // 4
-    parts = [
-        q_ref[pl.ds(pl.multiple_of((t ^ k) * quarter, quarter), quarter), :] for k in (0, 2, 1, 3)
-    ]
-    q = jnp.concatenate(parts, axis=0)
-    q = jnp.concatenate([q[:, g * HEAD_DIM : (g + 1) * HEAD_DIM] for g in range(GROUP)], axis=0)
     row = lax.broadcasted_iota(jnp.int32, (tokens, 1), 0)
     order = row // quarter
     order = (order % 2) * 2 + order // 2
     qp = place(pair_of(0, 0, 0), (order ^ t) * quarter + row % quarter)
-    total_rows = GROUP * tokens
-    top = jnp.full((total_rows, 1), FLOOR, f32)
-    total = jnp.zeros((total_rows, 1), f32)
-    acc = jnp.zeros((total_rows, HEAD_DIM), f32)
-    q_all[...] = q
-    for one in copies:
-        one.wait()
 
     def step(j, carry):
         top, total, acc = carry
         k = kv_ref[j, :, :HEAD_DIM]
         v = kv_ref[j, :, HEAD_DIM:]
-        count = k.shape[0]
         score = lax.dot_general(
             q_all[...], k, (((1,), (1,)), ((), ())), preferred_element_type=f32
         )
         score = score * (HEAD_DIM**-0.5 * EXP2)
         visible = kp_ref[pl.ds(j, 1), :] <= qp
         score = jnp.where(visible[None], score.reshape(GROUP, tokens, count), NEG)
-        score = score.reshape(total_rows, count)
+        score = score.reshape(GROUP * tokens, count)
         new_top = jnp.maximum(top, jnp.max(score, axis=-1, keepdims=True))
         weight = jnp.exp2(score - new_top)
         keep = jnp.exp2(top - new_top)
@@ -168,7 +144,56 @@
         acc = acc * keep + jnp.dot(weight.astype(bf16), v, preferred_element_type=f32)
         return new_top, total, acc
 
-    top, total, acc = lax.fori_loop(0, 8, step, (top, total, acc))
+    return lax.fori_loop(0, len(steps), step, carry)
+
+
+def attention_kernel(steps, at_ref, table_ref, q_ref, *refs):
+    n = len(steps)
+    kvs, (q_all, top_ref, total_ref, acc_ref) = refs[:n], refs[n : n + 4]
+    kv_ref, kp_ref, sems = refs[n + 4 :]
+    copies = [pltpu.make_async_copy(kvs[i], kv_ref.at[i], sems.at[i]) for i in range(n)]
+    for one in copies:
+        one.start()
+    t = at_ref[3]
+    tokens = q_ref.shape[0]
+    quarter = tokens // 4
+    parts = [
+        q_ref[pl.ds(pl.multiple_of((t ^ k) * quarter, quarter), quarter), :] for k in (0, 2, 1, 3)
+    ]
+    q = jnp.concatenate(parts, axis=0)
+    for g in range(GROUP):
+        q_all[g * tokens : (g + 1) * tokens, :] = q[:, g * HEAD_DIM : (g + 1) * HEAD_DIM]
+    rows = GROUP * tokens
+    carry = (
+        jnp.full((rows, 1), FLOOR, f32),
+        jnp.zeros((rows, 1), f32),
+        jnp.zeros((rows, HEAD_DIM), f32),
+    )
+    for one in copies:
+        one.wait()
+    top, total, acc = attend(at_ref, table_ref, q_all, kv_ref, kp_ref, steps, carry)
+    top_ref[...] = jnp.broadcast_to(top, top_ref.shape)
+    total_ref[...] = jnp.broadcast_to(total, total_ref.shape)
+    acc_ref[...] = acc
+
+
+def project_kernel(steps, at_ref, table_ref, q_all, top_ref, total_ref, acc_ref, *refs):
+    kvs, w_any, keep_ref, send_ref = refs[:4], refs[4], refs[5], refs[6]
+    w_ref, kv_ref, kp_ref, sems = refs[7:]
+    rows = kvs[2].shape[0]
+    places = [kv_ref.at[0], kv_ref.at[1]]
+    places += [kv_ref.at[2, pl.ds(i * rows, rows)] for i in range(2)]
+    copies = [pltpu.make_async_copy(kvs[i], places[i], sems.at[i]) for i in range(4)]
+    copy = pltpu.make_async_copy(w_any, w_ref, sems.at[4])
+    for one in copies:
+        one.start()
+    copy.start()
+    carry = top_ref[:, :1], total_ref[:, :1], acc_ref[...]
+    for one in copies:
+        one.wait()
+    top, total, acc = attend(at_ref, table_ref, q_all, kv_ref, kp_ref, steps, carry)
+    tokens = kv_ref.shape[1] // 8
+    half = tokens // 2
     summed = (acc / total).astype(bf16)
     heads = jnp.concatenate([summed[g * tokens : (g + 1) * tokens] for g in range(GROUP)], axis=1)
     copy.wait()
@@ -366,30 +391,48 @@
     kv = jnp.concatenate(gather_direct(kv, "y"), axis=0)
     ahead, behind = gather_ring(kv, "z")
     far = gather_far(ahead[3], behind[3], "z")
-    kvs = ahead + behind[:0:-1] + far
     at = jnp.stack([y, z, xh, t]).astype(jnp.int32)
 
     rows = GROUP * tokens
-    span = 64 * tokens
+    piece_rows = kv.shape[0]
+    steps = (0, 1, 7, 2, 6)
+    state = pl.pallas_call(
+        functools.partial(attention_kernel, steps),
+        out_shape=[jax.ShapeDtypeStruct((rows, HEAD_DIM), bf16)]
+        + [jax.ShapeDtypeStruct((rows, HEAD_DIM), f32)] * 3,
+        in_specs=[SMEM, SMEM, VMEM] + [HBM] * 5,
+        out_specs=[VMEM] * 4,
+        scratch_shapes=[
+            pltpu.VMEM((5,) + kv.shape, bf16),
+            pltpu.VMEM((8, piece_rows), jnp.int32),
+            pltpu.SemaphoreType.DMA((5,)),
+        ],
+        compiler_params=pltpu.CompilerParams(vmem_limit_bytes=16 << 20),
+        cost_estimate=pl.CostEstimate(
+            flops=20 * rows * piece_rows * HEAD_DIM,
+            bytes_accessed=20 * piece_rows * HEAD_DIM,
+            transcendentals=5 * rows * piece_rows,
+        ),
+    )(at, block_table, queries, ahead[0], ahead[1], behind[1], ahead[2], behind[2])
+    steps = (3, 5, 4)
     keep, send = pl.pallas_call(
-        attention_kernel,
+        functools.partial(project_kernel, steps),
         out_shape=[jax.ShapeDtypeStruct((half, width), bf16)] * 2,
-        in_specs=[SMEM, SMEM, VMEM] + [HBM] * 10,
+        in_specs=[SMEM, SMEM] + [VMEM] * 4 + [HBM] * 5,
         out_specs=[VMEM] * 2,
         scratch_shapes=[
             pltpu.VMEM(out_weight.shape, bf16),
-            pltpu.VMEM((8, 8 * tokens, 2 * HEAD_DIM), bf16),
-            pltpu.VMEM((GROUP * tokens, HEAD_DIM), bf16),
-            pltpu.VMEM((8, 8 * tokens), jnp.int32),
-            pltpu.SemaphoreType.DMA((10,)),
+            pltpu.VMEM((3,) + kv.shape, bf16),
+            pltpu.VMEM((8, piece_rows), jnp.int32),
+            pltpu.SemaphoreType.DMA((5,)),
         ],
         compiler_params=pltpu.CompilerParams(vmem_limit_bytes=46 << 20),
         cost_estimate=pl.CostEstimate(
-            flops=4 * rows * span * HEAD_DIM + 2 * tokens * out_weight.size,
-            bytes_accessed=2 * out_weight.size + 4 * span * HEAD_DIM,
-            transcendentals=rows * span,
-        ),
-    )(at, block_table, queries, *kvs, out_weight)
+            flops=12 * rows * piece_rows * HEAD_DIM + 2 * tokens * out_weight.size,
+            bytes_accessed=2 * out_weight.size + 12 * piece_rows * HEAD_DIM,
+            transcendentals=3 * rows * piece_rows,
+        ),
+    )(at, block_table, *state, ahead[3], behind[3], *far, out_weight)
 
     near = fetch(send, "core", 1)
     _, beyond = add([keep, near], pieces=2)
@@ -411,7 +454,7 @@
 
     by_y = join(gather_direct(normed, "y"))
     ahead, behind = gather_ring(by_y, "z")
-    swap_a, _ = lax.optimization_barrier((swap_a, ahead[1]))
+    swap_a, _ = lax.optimization_barrier((swap_a, (ahead[1], behind[1])))
     swap_b = fetch(swap_a, "core", 1)
     weights = pl.pallas_call(
         assemble_kernel,

time: 202 us -> 188 us (0.931)
  waiting for transfers between devices: 111 us -> 96.8 us
  Pallas kernels: 36.2 us -> 38.5 us
    ppermute x37, waiting for transfers between devices: 111 us -> 96.8 us  [fetch(): return lax.ppermute(x, axis, [((i + k) % n, i) for i in range(n)])]
    pallas_call x1 -> x2, Pallas kernels: 8.12 us -> 10.4 us  [the longest x1 6.5 us: per_device(): pl.pallas_call(functools.partial(project_kernel, steps), out_shape=[jax.S...]
  transfers between devices with their start and end apart: 38 -> 38, of which waited for: 30 -> 28; matrix products, arithmetic and copies ran while one was open for 0% -> 0% of each run, Pallas kernels for 13% -> 15%
where the time goes in v2:
time: 188 us; the launch traced here: 187 us
  waiting for transfers between devices  96.8 us (51%)
  starting transfers between devices  49.8 us (26%)
  Pallas kernels  38.5 us (20%)
    ppermute x37, waiting for transfers between devices, fetch(): return lax.ppermute(x, axis, [((i + k) % n, i) for i in range(n)])  96.8 us
    ppermute x37, starting transfers between devices, fetch(): return lax.ppermute(x, axis, [((i + k) % n, i) for i in range(n)])  48.7 us
    pallas_call x3, Pallas kernels, expert(): pl.pallas_call(functools.partial(expert_kernel, len(xs)), out_shape=[jax....  17.4 us
    pallas_call x1, Pallas kernels, per_device(): pl.pallas_call(functools.partial(project_kernel, steps), out_shape=[jax.S...  6.5 us
    pallas_call x1, Pallas kernels, per_device(): pl.pallas_call(assemble_kernel, out_shape=[jax.ShapeDtypeStruct((4 * hidd...  4.42 us
    pallas_call x1, Pallas kernels, per_device(): pl.pallas_call(functools.partial(attention_kernel, steps), out_shape=[jax...  3.89 us
  transfers between devices with their start and end apart: 38, of which 28 were waited for; matrix products, arithmetic and copies ran while one was open for 0% of the time, Pallas kernels for 15%

profile of v2, /device:TPU:0, one launch (start us, length us, event | category | flops | bytes accessed | tf_op | source)
XLA Modules:
  0.0 187.1 jit_solution(9650941857646589159)
XLA Ops:
  2.8 4.1 %collective-permute-done = bf16[64,256]{1,0:T(8,128)(2,1)S(1)} collective-permute-done((bf16[64,256]{1,0:T(8,128)(2,1)S(1)}, bf16[64,256]{1,0:T(8,128)(2,1)S(1)}, u32[]{:S(2)}, u32[]{:S(2)}) %collective-permute-start) | collective-permute-done | bytes 32800 | tf_op jit(solution)/shard_map/ppermute | solution.py:34
  7.0 3.7 %shard_map.114 = bf16[480,3584]{1,0:T(8,128)(2,1)} custom-call(s32[1]{0:T(128)} %bitcast.6.core_ref, bf16[320,3584]{1,0:T(8,128)(2,1)} %bitcast.7, bf16[320,3584]{1,0:T(8,128)(2,1)} %bitcast.9, bf16[320,3584]{1,0:T(8,128)(2,1)} %d_any.3), custom_call_target="tpu_custom_call" | custom-call | bytes 6881280 | tf_op jit(solution)/shard_map/pallas_call | solution.py:379
  16.8 3.9 %collective-permute-done.2 = bf16[128,256]{1,0:T(8,128)(2,1)S(1)} collective-permute-done((bf16[128,256]{1,0:T(8,128)(2,1)S(1)}, bf16[128,256]{1,0:T(8,128)(2,1)S(1)}, u32[]{:S(2)}, u32[]{:S(2)}) %collective-permute-start.2) | collective-permute-done | bytes 65568 | tf_op jit(solution)/shard_map/ppermute | solution.py:34
  21.3 5.9 %collective-permute-start.4 = (bf16[512,256]{1,0:T(8,128)(2,1)S(1)}, bf16[512,256]{1,0:T(8,128)(2,1)S(1)}, u32[]{:S(2)}, u32[]{:S(2)}) collective-permute-start(bf16[512,256]{1,0:T(8,128)(2,1)S(1)} %constant_dynamic-update-slice_fusion.2.refs_0_), channel_id=1, source_target_pairs={{8,0},{16,8},{24,16},{32,24},{40,32},{48,40},{56,48},{0,56},{9,1},... | collective-permute-start | bytes 786440 | tf_op jit(solution)/shard_map/ppermute | solution.py:34
  27.2 3.9 %collective-permute-done.4.refs_1_ = bf16[512,256]{1,0:T(8,128)(2,1)S(1)} collective-permute-done((bf16[512,256]{1,0:T(8,128)(2,1)S(1)}, bf16[512,256]{1,0:T(8,128)(2,1)S(1)}, u32[]{:S(2)}, u32[]{:S(2)}) %collective-permute-start.4) | collective-permute-done | bytes 262176 | tf_op jit(solution)/shard_map/ppermute | solution.py:34
  31.1 3.7 %collective-permute-start.6 = (bf16[512,256]{1,0:T(8,128)(2,1)S(1)}, bf16[512,256]{1,0:T(8,128)(2,1)S(1)}, u32[]{:S(2)}, u32[]{:S(2)}) collective-permute-start(bf16[512,256]{1,0:T(8,128)(2,1)S(1)} %collective-permute-done.4.refs_1_), channel_id=1, source_target_pairs={{8,0},{16,8},{24,16},{32,24},{40,32},{48,40},{56,48},{0,56},{9,1},... | collective-permute-start | bytes 786440 | tf_op jit(solution)/shard_map/ppermute | solution.py:34
  34.8 4.1 %collective-permute-done.6.refs_3_ = bf16[512,256]{1,0:T(8,128)(2,1)S(1)} collective-permute-done((bf16[512,256]{1,0:T(8,128)(2,1)S(1)}, bf16[512,256]{1,0:T(8,128)(2,1)S(1)}, u32[]{:S(2)}, u32[]{:S(2)}) %collective-permute-start.6) | collective-permute-done | bytes 262176 | tf_op jit(solution)/shard_map/ppermute | solution.py:34
  38.9 3.7 %collective-permute-start.8 = (bf16[512,256]{1,0:T(8,128)(2,1)S(1)}, bf16[512,256]{1,0:T(8,128)(2,1)S(1)}, u32[]{:S(2)}, u32[]{:S(2)}) collective-permute-start(bf16[512,256]{1,0:T(8,128)(2,1)S(1)} %collective-permute-done.6.refs_3_), channel_id=1, source_target_pairs={{8,0},{16,8},{24,16},{32,24},{40,32},{48,40},{56,48},{0,56},{9,1},... | collective-permute-start | bytes 786440 | tf_op jit(solution)/shard_map/ppermute | solution.py:34
  42.9 4.4 %collective-permute-done.8.refs_0_ = bf16[512,256]{1,0:T(8,128)(2,1)S(1)} collective-permute-done((bf16[512,256]{1,0:T(8,128)(2,1)S(1)}, bf16[512,256]{1,0:T(8,128)(2,1)S(1)}, u32[]{:S(2)}, u32[]{:S(2)}) %collective-permute-start.8) | collective-permute-done | bytes 262176 | tf_op jit(solution)/shard_map/ppermute | solution.py:34
  47.4 3.8 %collective-permute-start.10 = (bf16[256,256]{1,0:T(8,128)(2,1)S(1)}, bf16[256,256]{1,0:T(8,128)(2,1)S(1)}, u32[]{:S(2)}, u32[]{:S(2)}) collective-permute-start(bf16[256,256]{1,0:T(8,128)(2,1)S(1)} %slice.16), channel_id=1, source_target_pairs={{8,0},{16,8},{24,16},{32,24},{40,32},{48,40},{56,48},{0,56},{9,1},... | collective-permute-start | bytes 393224 | tf_op jit(solution)/shard_map/ppermute | solution.py:34
  51.8 3.9 %shard_map.109 = (bf16[448,128]{1,0:T(8,128)(2,1)S(1)}, f32[448,128]{1,0:T(8,128)S(1)}, f32[448,128]{1,0:T(8,128)S(1)}, f32[448,128]{1,0:T(8,128)S(1)}) custom-call(s32[4]{0:T(128)S(1)} %pad_add_fusion.at_ref, s32[64]{0:T(128)S(1)} %copy-done.4, bf16[64,896]{1,0:T(8,128)(2,1)S(1)} %copy-done.5, ...), custom_call_target="tpu_custom_call" | custom-call | flops 587202560 | bytes 1310720 | tf_op jit(solution)/shard_map/pallas_call | solution.py:399
  57.9 6.5 %shard_map.110 = (bf16[32,3584]{1,0:T(8,128)(2,1)S(1)}, bf16[32,3584]{1,0:T(8,128)(2,1)S(1)}) custom-call(s32[4]{0:T(128)S(1)} %pad_add_fusion.at_ref, s32[64]{0:T(128)S(1)} %copy-done.4, bf16[448,128]{1,0:T(8,128)(2,1)S(1)} %get-tuple-element.36.q_all, f32[448,128]{1,0:T(8,128)S(1)} %get-tuple-element.37.top_ref, ...), custom_call_target="tpu_custom_call" | custom-call | flops 763363328 | bytes 7208960 | tf_op jit(solution)/shard_map/pallas_call | solution.py:418
  83.9 10.4 %collective-permute-done.17.refs_1_ = bf16[64,3584]{1,0:T(8,128)(2,1)S(1)} collective-permute-done((bf16[64,3584]{1,0:T(8,128)(2,1)S(1)}, bf16[64,3584]{1,0:T(8,128)(2,1)S(1)}, u32[]{:S(2)}, u32[]{:S(2)}) %collective-permute-start.17) | collective-permute-done | bytes 458784 | tf_op jit(solution)/shard_map/ppermute | solution.py:34
  98.4 10.9 %collective-permute-done.19.refs_0_ = bf16[64,3584]{1,0:T(8,128)(2,1)S(1)} collective-permute-done((bf16[64,3584]{1,0:T(8,128)(2,1)S(1)}, bf16[64,3584]{1,0:T(8,128)(2,1)S(1)}, u32[]{:S(2)}, u32[]{:S(2)}) %collective-permute-start.19) | collective-permute-done | bytes 458784 | tf_op jit(solution)/shard_map/ppermute | solution.py:34
  111.3 4.4 %shard_map.115 = (bf16[1280,3584]{1,0:T(8,128)(2,1)S(1)}, bf16[640,3584]{1,0:T(8,128)(2,1)S(1)}) custom-call(bf16[320,3584]{1,0:T(8,128)(2,1)S(1)} %bitcast.8, bf16[320,3584]{1,0:T(8,128)(2,1)S(1)} %bitcast.10, bf16[320,3584]{1,0:T(8,128)(2,1)S(1)} %copy-done.2, bf16[480,3584]{1,0:T(8,128)(2,1)} %collective-permute-done.23.a_any, ...), custom_call_target="tpu_custom_call" | custom-call | bytes 13762560 | tf_op jit(solution)/shard_map/pallas_call | solution.py:459
  115.8 5.7 %collective-permute-done.20.refs_2_ = bf16[64,3584]{1,0:T(8,128)(2,1)S(1)} collective-permute-done((bf16[64,3584]{1,0:T(8,128)(2,1)S(1)}, bf16[64,3584]{1,0:T(8,128)(2,1)S(1)}, u32[]{:S(2)}, u32[]{:S(2)}) %collective-permute-start.20) | collective-permute-done | bytes 458784 | tf_op jit(solution)/shard_map/ppermute | solution.py:34
  126.0 3.9 %collective-permute-done.25.refs_0_ = bf16[32,3584]{1,0:T(8,128)(2,1)S(1)} collective-permute-done((bf16[32,3584]{1,0:T(8,128)(2,1)S(1)}, bf16[32,3584]{1,0:T(8,128)(2,1)S(1)}, u32[]{:S(2)}, u32[]{:S(2)}) %collective-permute-start.25) | collective-permute-done | bytes 229408 | tf_op jit(solution)/shard_map/ppermute | solution.py:34
  131.5 5.1 %shard_map.118 = (bf16[32,3584]{1,0:T(8,128)(2,1)S(1)}, bf16[32,3584]{1,0:T(8,128)(2,1)S(1)}) custom-call(bf16[32,3584]{1,0:T(8,128)(2,1)S(1)} %collective-permute-done.25.refs_0_, bf16[32,3584]{1,0:T(8,128)(2,1)S(1)} %collective-permute-done.26.refs_1_, bf16[1280,3584]{1,0:T(8,128)(2,1)S(1)} %get-tuple-element.50.refs_3_.refs_4_.refs_2_, ...), custom_call_target="tpu_custom_call" | custom-call | flops 880803840 | bytes 14680064 | tf_op jit(solution)/shard_map/pallas_call | solution.py:328
  138.7 6.2 %shard_map.117 = (bf16[64,3584]{1,0:T(8,128)(2,1)S(1)}, bf16[64,3584]{1,0:T(8,128)(2,1)S(1)}, bf16[64,3584]{1,0:T(8,128)(2,1)S(1)}, bf16[64,3584]{1,0:T(8,128)(2,1)S(1)}) custom-call(bf16[64,3584]{1,0:T(8,128)(2,1)S(1)} %collective-permute-done.19.refs_0_, bf16[64,3584]{1,0:T(8,128)(2,1)S(1)} %collective-permute-done.21.refs_1_, ...), custom_call_target="tpu_custom_call" | custom-call | flops 3523215360 | bytes 17432576 | tf_op jit(solution)/shard_map/pallas_call | solution.py:328
  147.3 8.3 %collective-permute-done.32.refs_1_ = bf16[64,3584]{1,0:T(8,128)(2,1)S(1)} collective-permute-done((bf16[64,3584]{1,0:T(8,128)(2,1)S(1)}, bf16[64,3584]{1,0:T(8,128)(2,1)S(1)}, u32[]{:S(2)}, u32[]{:S(2)}) %collective-permute-start.32) | collective-permute-done | bytes 458784 | tf_op jit(solution)/shard_map/ppermute | solution.py:34
  158.0 6.2 %shard_map.116 = (bf16[64,3584]{1,0:T(8,128)(2,1)S(1)}, bf16[64,3584]{1,0:T(8,128)(2,1)S(1)}, bf16[64,3584]{1,0:T(8,128)(2,1)S(1)}) custom-call(bf16[64,3584]{1,0:T(8,128)(2,1)S(1)} %shard_map.113.refs_0_, bf16[64,3584]{1,0:T(8,128)(2,1)S(1)} %collective-permute-done.17.refs_1_, bf16[64,3584]{1,0:T(8,128)(2,1)S(1)} %collective-permute-done.18.refs_2_, ...), custom_call_target="tpu_custom_call" | custom-call | flops 2642411520 | bytes 16515072 | tf_op jit(solution)/shard_map/pallas_call | solution.py:328
  168.3 6.2 %collective-permute-done.34.refs_2_ = bf16[64,3584]{1,0:T(8,128)(2,1)S(1)} collective-permute-done((bf16[64,3584]{1,0:T(8,128)(2,1)S(1)}, bf16[64,3584]{1,0:T(8,128)(2,1)S(1)}, u32[]{:S(2)}, u32[]{:S(2)}) %collective-permute-start.34) | collective-permute-done | bytes 458784 | tf_op jit(solution)/shard_map/ppermute | solution.py:34
  174.5 3.5 %collective-permute-done.30.refs_1_ = bf16[64,3584]{1,0:T(8,128)(2,1)S(1)} collective-permute-done((bf16[64,3584]{1,0:T(8,128)(2,1)S(1)}, bf16[64,3584]{1,0:T(8,128)(2,1)S(1)}, u32[]{:S(2)}, u32[]{:S(2)}) %collective-permute-start.30) | collective-permute-done | bytes 458784 | tf_op jit(solution)/shard_map/ppermute | solution.py:34
  181.4 4.0 %collective-permute-done.35.refs_1_ = bf16[16,3584]{1,0:T(8,128)(2,1)S(1)} collective-permute-done((bf16[16,3584]{1,0:T(8,128)(2,1)S(1)}, bf16[16,3584]{1,0:T(8,128)(2,1)S(1)}, u32[]{:S(2)}, u32[]{:S(2)}) %collective-permute-start.35) | collective-permute-done | bytes 114720 | tf_op jit(solution)/shard_map/ppermute | solution.py:34
  (100 shorter events, 60.5 us)
Async XLA Ops:
  10.7 85.6 %collective-permute-start.23 = (bf16[480,3584]{1,0:T(8,128)(2,1)}, bf16[480,3584]{1,0:T(8,128)(2,1)}, u32[]{:S(2)}, u32[]{:S(2)}) collective-permute-start(bf16[480,3584]{1,0:T(8,128)(2,1)} %shard_map.114), channel_id=1, source_target_pairs={{0,6},{6,0},{2,4},{4,2},{1,7},{7,1},{3,5},{5,3},{8,14},{14,8},{10,... | collective-permute-start | bytes 10321928 | tf_op jit(solution)/shard_map/ppermute | solution.py:389
  21.3 9.7 %collective-permute-start.4 = (bf16[512,256]{1,0:T(8,128)(2,1)S(1)}, bf16[512,256]{1,0:T(8,128)(2,1)S(1)}, u32[]{:S(2)}, u32[]{:S(2)}) collective-permute-start(bf16[512,256]{1,0:T(8,128)(2,1)S(1)} %constant_dynamic-update-slice_fusion.2.refs_0_), channel_id=1, source_target_pairs={{8,0},{16,8},{24,16},{32,24},{40,32},{48,40},{56,48},{0,56},{9,1},... | collective-permute-start | bytes 786440 | tf_op jit(solution)/shard_map/ppermute | solution.py:34
  27.2 7.6 %collective-permute-start.5 = (bf16[512,256]{1,0:T(8,128)(2,1)S(1)}, bf16[512,256]{1,0:T(8,128)(2,1)S(1)}, u32[]{:S(2)}, u32[]{:S(2)}) collective-permute-start(bf16[512,256]{1,0:T(8,128)(2,1)S(1)} %constant_dynamic-update-slice_fusion.2.refs_0_), channel_id=1, source_target_pairs={{56,0},{0,8},{8,16},{16,24},{24,32},{32,40},{40,48},{48,56},{57,1}... | collective-permute-start | bytes 786440 | tf_op jit(solution)/shard_map/ppermute | solution.py:34
  31.1 7.8 %collective-permute-start.6 = (bf16[512,256]{1,0:T(8,128)(2,1)S(1)}, bf16[512,256]{1,0:T(8,128)(2,1)S(1)}, u32[]{:S(2)}, u32[]{:S(2)}) collective-permute-start(bf16[512,256]{1,0:T(8,128)(2,1)S(1)} %collective-permute-done.4.refs_1_), channel_id=1, source_target_pairs={{8,0},{16,8},{24,16},{32,24},{40,32},{48,40},{56,48},{0,56},{9,1},... | collective-permute-start | bytes 786440 | tf_op jit(solution)/shard_map/ppermute | solution.py:34
  34.8 8.1 %collective-permute-start.7 = (bf16[512,256]{1,0:T(8,128)(2,1)S(1)}, bf16[512,256]{1,0:T(8,128)(2,1)S(1)}, u32[]{:S(2)}, u32[]{:S(2)}) collective-permute-start(bf16[512,256]{1,0:T(8,128)(2,1)S(1)} %collective-permute-done.5.refs_2_), channel_id=1, source_target_pairs={{56,0},{0,8},{8,16},{16,24},{24,32},{32,40},{40,48},{48,56},{57,1}... | collective-permute-start | bytes 786440 | tf_op jit(solution)/shard_map/ppermute | solution.py:34
  38.9 8.4 %collective-permute-start.8 = (bf16[512,256]{1,0:T(8,128)(2,1)S(1)}, bf16[512,256]{1,0:T(8,128)(2,1)S(1)}, u32[]{:S(2)}, u32[]{:S(2)}) collective-permute-start(bf16[512,256]{1,0:T(8,128)(2,1)S(1)} %collective-permute-done.6.refs_3_), channel_id=1, source_target_pairs={{8,0},{16,8},{24,16},{32,24},{40,32},{48,40},{56,48},{0,56},{9,1},... | collective-permute-start | bytes 786440 | tf_op jit(solution)/shard_map/ppermute | solution.py:34
  42.9 8.7 %collective-permute-start.9 = (bf16[512,256]{1,0:T(8,128)(2,1)S(1)}, bf16[512,256]{1,0:T(8,128)(2,1)S(1)}, u32[]{:S(2)}, u32[]{:S(2)}) collective-permute-start(bf16[512,256]{1,0:T(8,128)(2,1)S(1)} %collective-permute-done.7.refs_4_), channel_id=1, source_target_pairs={{56,0},{0,8},{8,16},{16,24},{24,32},{32,40},{40,48},{48,56},{57,1}... | collective-permute-start | bytes 786440 | tf_op jit(solution)/shard_map/ppermute | solution.py:34
  47.4 8.3 %collective-permute-start.10 = (bf16[256,256]{1,0:T(8,128)(2,1)S(1)}, bf16[256,256]{1,0:T(8,128)(2,1)S(1)}, u32[]{:S(2)}, u32[]{:S(2)}) collective-permute-start(bf16[256,256]{1,0:T(8,128)(2,1)S(1)} %slice.16), channel_id=1, source_target_pairs={{8,0},{16,8},{24,16},{32,24},{40,32},{48,40},{56,48},{0,56},{9,1},... | collective-permute-start | bytes 393224 | tf_op jit(solution)/shard_map/ppermute | solution.py:34
  74.3 7.5 %collective-permute-start.16 = (bf16[16,3584]{1,0:T(8,128)(2,1)S(1)}, bf16[16,3584]{1,0:T(8,128)(2,1)S(1)}, u32[]{:S(2)}, u32[]{:S(2)}) collective-permute-start(bf16[16,3584]{1,0:T(8,128)(2,1)S(1)} %get-tuple-element.45.refs_0_), channel_id=1, source_target_pairs={{192,0},{0,64},{64,128},{128,192},{193,1},{1,65},{65,129},{129,193... | collective-permute-start | bytes 344072 | tf_op jit(solution)/shard_map/ppermute | solution.py:34
  81.8 12.5 %collective-permute-start.17 = (bf16[64,3584]{1,0:T(8,128)(2,1)S(1)}, bf16[64,3584]{1,0:T(8,128)(2,1)S(1)}, u32[]{:S(2)}, u32[]{:S(2)}) collective-permute-start(bf16[64,3584]{1,0:T(8,128)(2,1)S(1)} %shard_map.113.refs_0_), channel_id=1, source_target_pairs={{8,0},{16,8},{24,16},{32,24},{40,32},{48,40},{56,48},{0,56},{9,1},... | collective-permute-start | bytes 1376264 | tf_op jit(solution)/shard_map/ppermute | solution.py:34
  83.0 13.4 %collective-permute-start.18 = (bf16[64,3584]{1,0:T(8,128)(2,1)S(1)}, bf16[64,3584]{1,0:T(8,128)(2,1)S(1)}, u32[]{:S(2)}, u32[]{:S(2)}) collective-permute-start(bf16[64,3584]{1,0:T(8,128)(2,1)S(1)} %shard_map.113.refs_0_), channel_id=1, source_target_pairs={{56,0},{0,8},{8,16},{16,24},{24,32},{32,40},{40,48},{48,56},{57,1}... | collective-permute-start | bytes 1376264 | tf_op jit(solution)/shard_map/ppermute | solution.py:34
  96.3 15.0 %collective-permute-start.24 = (bf16[480,3584]{1,0:T(8,128)(2,1)}, bf16[480,3584]{1,0:T(8,128)(2,1)S(1)}, u32[]{:S(2)}, u32[]{:S(2)}) collective-permute-start(bf16[480,3584]{1,0:T(8,128)(2,1)} %collective-permute-done.23.a_any), channel_id=1, source_target_pairs={{1,0},{0,1},{3,2},{2,3},{5,4},{4,5},{7,6},{6,7},{9,8},{8,9},{11,10... | collective-permute-start | bytes 10321928 | tf_op jit(solution)/shard_map/ppermute | solution.py:34
  96.3 12.9 %collective-permute-start.19 = (bf16[64,3584]{1,0:T(8,128)(2,1)S(1)}, bf16[64,3584]{1,0:T(8,128)(2,1)S(1)}, u32[]{:S(2)}, u32[]{:S(2)}) collective-permute-start(bf16[64,3584]{1,0:T(8,128)(2,1)S(1)} %collective-permute-done.17.refs_1_), channel_id=1, source_target_pairs={{8,0},{16,8},{24,16},{32,24},{40,32},{48,40},{56,48},{0,56},{9,1},... | collective-permute-start | bytes 1376264 | tf_op jit(solution)/shard_map/ppermute | solution.py:34
  96.7 14.1 %collective-permute-start.21 = (bf16[64,3584]{1,0:T(8,128)(2,1)S(1)}, bf16[64,3584]{1,0:T(8,128)(2,1)S(1)}, u32[]{:S(2)}, u32[]{:S(2)}) collective-permute-start(bf16[64,3584]{1,0:T(8,128)(2,1)S(1)} %collective-permute-done.18.refs_2_), channel_id=1, source_target_pairs={{56,0},{0,8},{8,16},{16,24},{24,32},{32,40},{40,48},{48,56},{57,1}... | collective-permute-start | bytes 1376264 | tf_op jit(solution)/shard_map/ppermute | solution.py:34
  109.3 12.2 %collective-permute-start.20 = (bf16[64,3584]{1,0:T(8,128)(2,1)S(1)}, bf16[64,3584]{1,0:T(8,128)(2,1)S(1)}, u32[]{:S(2)}, u32[]{:S(2)}) collective-permute-start(bf16[64,3584]{1,0:T(8,128)(2,1)S(1)} %collective-permute-done.19.refs_0_), channel_id=1, source_target_pairs={{8,0},{16,8},{24,16},{32,24},{40,32},{48,40},{56,48},{0,56},{9,1},... | collective-permute-start | bytes 1376264 | tf_op jit(solution)/shard_map/ppermute | solution.py:34
  110.8 13.0 %collective-permute-start.22 = (bf16[64,3584]{1,0:T(8,128)(2,1)S(1)}, bf16[64,3584]{1,0:T(8,128)(2,1)S(1)}, u32[]{:S(2)}, u32[]{:S(2)}) collective-permute-start(bf16[64,3584]{1,0:T(8,128)(2,1)S(1)} %collective-permute-done.21.refs_1_), channel_id=1, source_target_pairs={{56,0},{0,8},{8,16},{16,24},{24,32},{32,40},{40,48},{48,56},{57,1}... | collective-permute-start | bytes 1376264 | tf_op jit(solution)/shard_map/ppermute | solution.py:34
  136.6 8.3 %collective-permute-start.31 = (bf16[32,3584]{1,0:T(8,128)(2,1)S(1)}, bf16[32,3584]{1,0:T(8,128)(2,1)S(1)}, u32[]{:S(2)}, u32[]{:S(2)}) collective-permute-start(bf16[32,3584]{1,0:T(8,128)(2,1)S(1)} %get-tuple-element.62), channel_id=1, source_target_pairs={{8,0},{16,8},{24,16},{32,24},{40,32},{48,40},{56,48},{0,56},{9,1},... | collective-permute-start | bytes 688136 | tf_op jit(solution)/shard_map/ppermute | solution.py:34
  136.9 9.7 %collective-permute-start.27 = (bf16[32,3584]{1,0:T(8,128)(2,1)S(1)}, bf16[32,3584]{1,0:T(8,128)(2,1)S(1)}, u32[]{:S(2)}, u32[]{:S(2)}) collective-permute-start(bf16[32,3584]{1,0:T(8,128)(2,1)S(1)} %get-tuple-element.58), channel_id=1, source_target_pairs={{56,0},{0,8},{8,16},{16,24},{24,32},{32,40},{40,48},{48,56},{57,1}... | collective-permute-start | bytes 688136 | tf_op jit(solution)/shard_map/ppermute | solution.py:34
  145.0 10.6 %collective-permute-start.32 = (bf16[64,3584]{1,0:T(8,128)(2,1)S(1)}, bf16[64,3584]{1,0:T(8,128)(2,1)S(1)}, u32[]{:S(2)}, u32[]{:S(2)}) collective-permute-start(bf16[64,3584]{1,0:T(8,128)(2,1)S(1)} %shard_map.122), channel_id=1, source_target_pairs={{8,0},{16,8},{24,16},{32,24},{40,32},{48,40},{56,48},{0,56},{9,1},... | collective-permute-start | bytes 1376264 | tf_op jit(solution)/shard_map/ppermute | solution.py:34
  146.7 10.9 %collective-permute-start.28 = (bf16[64,3584]{1,0:T(8,128)(2,1)S(1)}, bf16[64,3584]{1,0:T(8,128)(2,1)S(1)}, u32[]{:S(2)}, u32[]{:S(2)}) collective-permute-start(bf16[64,3584]{1,0:T(8,128)(2,1)S(1)} %shard_map.119), channel_id=1, source_target_pairs={{56,0},{0,8},{8,16},{16,24},{24,32},{32,40},{40,48},{48,56},{57,1}... | collective-permute-start | bytes 1376264 | tf_op jit(solution)/shard_map/ppermute | solution.py:34
  155.7 10.1 %collective-permute-start.33 = (bf16[64,3584]{1,0:T(8,128)(2,1)S(1)}, bf16[64,3584]{1,0:T(8,128)(2,1)S(1)}, u32[]{:S(2)}, u32[]{:S(2)}) collective-permute-start(bf16[64,3584]{1,0:T(8,128)(2,1)S(1)} %shard_map.123), channel_id=1, source_target_pairs={{8,0},{16,8},{24,16},{32,24},{40,32},{48,40},{56,48},{0,56},{9,1},... | collective-permute-start | bytes 1376264 | tf_op jit(solution)/shard_map/ppermute | solution.py:34
  157.6 10.4 %collective-permute-start.29 = (bf16[64,3584]{1,0:T(8,128)(2,1)S(1)}, bf16[64,3584]{1,0:T(8,128)(2,1)S(1)}, u32[]{:S(2)}, u32[]{:S(2)}) collective-permute-start(bf16[64,3584]{1,0:T(8,128)(2,1)S(1)} %shard_map.120), channel_id=1, source_target_pairs={{56,0},{0,8},{8,16},{16,24},{24,32},{32,40},{40,48},{48,56},{57,1}... | collective-permute-start | bytes 1376264 | tf_op jit(solution)/shard_map/ppermute | solution.py:34
  165.9 8.6 %collective-permute-start.34 = (bf16[64,3584]{1,0:T(8,128)(2,1)S(1)}, bf16[64,3584]{1,0:T(8,128)(2,1)S(1)}, u32[]{:S(2)}, u32[]{:S(2)}) collective-permute-start(bf16[64,3584]{1,0:T(8,128)(2,1)S(1)} %shard_map.124), channel_id=1, source_target_pairs={{8,0},{16,8},{24,16},{32,24},{40,32},{48,40},{56,48},{0,56},{9,1},... | collective-permute-start | bytes 1376264 | tf_op jit(solution)/shard_map/ppermute | solution.py:34
  168.2 9.8 %collective-permute-start.30 = (bf16[64,3584]{1,0:T(8,128)(2,1)S(1)}, bf16[64,3584]{1,0:T(8,128)(2,1)S(1)}, u32[]{:S(2)}, u32[]{:S(2)}) collective-permute-start(bf16[64,3584]{1,0:T(8,128)(2,1)S(1)} %shard_map.121), channel_id=1, source_target_pairs={{56,0},{0,8},{8,16},{16,24},{24,32},{32,40},{40,48},{48,56},{57,1}... | collective-permute-start | bytes 1376264 | tf_op jit(solution)/shard_map/ppermute | solution.py:34
  (22 other events, 370.9 us)

commit v3 on v2

--- a/solution.py
+++ b/solution.py
@@ -220,17 +220,21 @@
     prob[...] = jnp.broadcast_to(1.0 / (1.0 + jnp.exp(-logit)), prob.shape)
 
 
-def send_kernel(core_ref, g_any, u_any, d_any, out_any, sems):
+def send_kernel(core_ref, g_any, u_any, d_any, out_any, buf, in_sems, out_sems):
     n = out_any.shape[0] // 3
     at = pl.multiple_of(core_ref[0] * n, n)
-    copies = [
-        pltpu.make_async_copy(w.at[pl.ds(at, n)], out_any.at[pl.ds(i * n, n)], sems.at[i])
-        for i, w in enumerate((g_any, u_any, d_any))
-    ]
-    for copy in copies:
+    ins, outs = [], []
+    for i, w in enumerate((g_any, u_any, d_any)):
+        here = buf.at[pl.ds(i * n, n)]
+        ins.append(pltpu.make_async_copy(w.at[pl.ds(at, n)], here, in_sems.at[i]))
+        outs.append(pltpu.make_async_copy(here, out_any.at[pl.ds(i * n, n)], out_sems.at[i]))
+    for copy in ins:
         copy.start()
-    for copy in copies:
+    for copy, out in zip(ins, outs):
         copy.wait()
+        out.start()
+    for out in outs:
+        out.wait()
 
 
 def assemble_kernel(g_any, u_any, d_any, a_any, b_any, w_ref, d_ref, sems):
@@ -380,8 +384,12 @@
         send_kernel,
         out_shape=jax.ShapeDtypeStruct((3 * piece, width), bf16),
         in_specs=[SMEM, HBM, HBM, HBM],
-        out_specs=VMEM,
-        scratch_shapes=[pltpu.SemaphoreType.DMA((3,))],
+        out_specs=HBM,
+        scratch_shapes=[
+            pltpu.VMEM((3 * piece, width), bf16),
+            pltpu.SemaphoreType.DMA((3,)),
+            pltpu.SemaphoreType.DMA((3,)),
+        ],
         cost_estimate=pl.CostEstimate(
             flops=0, bytes_accessed=12 * piece * width, transcendentals=0
         ),
@@ -472,11 +480,12 @@
     )(gate_t, up_t, down_weight, swap_a, swap_b)
     ahead_3, behind_3, weights = lax.optimization_barrier((ahead[3], behind[3], weights))
     far = gather_far(ahead_3, behind_3, "z")
-    own, after, before = expert([ahead[0], ahead[1], behind[1]], weights)
     after_2, before_2, after_3, before_3 = expert(
         [ahead[2], behind[2], ahead[3], behind[3]], weights
     )
+    weights, after_3 = lax.optimization_barrier((weights, after_3))
     far_parts = expert(far, weights)
+    own, after, before = expert([ahead[0], ahead[1], behind[1]], weights)
     near_parts = [own, after, after_2, after_3, None, before_3, before_2, before]
     by_y = add(scatter_ring(near_parts, far_parts, "z"), pieces=4)
     terms = scatter_direct(by_y, "y")

time: 188 us -> 187 us (level)
  waiting for transfers between devices: 96.8 us -> 94.3 us
  starting transfers between devices: 49.8 us -> 52.1 us
    ppermute x37, waiting for transfers between devices: 96.8 us -> 94.3 us  [fetch(): return lax.ppermute(x, axis, [((i + k) % n, i) for i in range(n)])]
    ppermute x37, starting transfers between devices: 48.7 us -> 51 us  [fetch(): return lax.ppermute(x, axis, [((i + k) % n, i) for i in range(n)])]
where the time goes in v3:
time: 187 us; the launch traced here: 186 us
  waiting for transfers between devices  94.3 us (50%)
  starting transfers between devices  52.1 us (28%)
  Pallas kernels  37.8 us (20%)
    ppermute x37, waiting for transfers between devices, fetch(): return lax.ppermute(x, axis, [((i + k) % n, i) for i in range(n)])  94.3 us
    ppermute x37, starting transfers between devices, fetch(): return lax.ppermute(x, axis, [((i + k) % n, i) for i in range(n)])  51 us
    pallas_call x3, Pallas kernels, expert(): pl.pallas_call(functools.partial(expert_kernel, len(xs)), out_shape=[jax....  17.4 us
    pallas_call x1, Pallas kernels, per_device(): pl.pallas_call(functools.partial(project_kernel, steps), out_shape=[jax.S...  6.5 us
    pallas_call x1, Pallas kernels, per_device(): pl.pallas_call(assemble_kernel, out_shape=[jax.ShapeDtypeStruct((4 * hidd...  4.42 us
    pallas_call x1, Pallas kernels, per_device(): pl.pallas_call(functools.partial(attention_kernel, steps), out_shape=[jax...  3.89 us
  transfers between devices with their start and end apart: 38, of which 28 were waited for; matrix products, arithmetic and copies ran while one was open for 0% of the time, Pallas kernels for 15%

profile of v3, /device:TPU:0, one launch (start us, length us, event | category | flops | bytes accessed | tf_op | source)
XLA Modules:
  0.0 186.1 jit_solution(1857238468524222090)
XLA Ops:
  2.8 4.1 %collective-permute-done = bf16[64,256]{1,0:T(8,128)(2,1)S(1)} collective-permute-done((bf16[64,256]{1,0:T(8,128)(2,1)S(1)}, bf16[64,256]{1,0:T(8,128)(2,1)S(1)}, u32[]{:S(2)}, u32[]{:S(2)}) %collective-permute-start) | collective-permute-done | bytes 32800 | tf_op jit(solution)/shard_map/ppermute | solution.py:34
  16.1 3.9 %collective-permute-done.2 = bf16[128,256]{1,0:T(8,128)(2,1)S(1)} collective-permute-done((bf16[128,256]{1,0:T(8,128)(2,1)S(1)}, bf16[128,256]{1,0:T(8,128)(2,1)S(1)}, u32[]{:S(2)}, u32[]{:S(2)}) %collective-permute-start.2) | collective-permute-done | bytes 65568 | tf_op jit(solution)/shard_map/ppermute | solution.py:34
  20.7 5.9 %collective-permute-start.4 = (bf16[512,256]{1,0:T(8,128)(2,1)S(1)}, bf16[512,256]{1,0:T(8,128)(2,1)S(1)}, u32[]{:S(2)}, u32[]{:S(2)}) collective-permute-start(bf16[512,256]{1,0:T(8,128)(2,1)S(1)} %constant_dynamic-update-slice_fusion.2.refs_0_), channel_id=1, source_target_pairs={{8,0},{16,8},{24,16},{32,24},{40,32},{48,40},{56,48},{0,56},{9,1},... | collective-permute-start | bytes 786440 | tf_op jit(solution)/shard_map/ppermute | solution.py:34
  26.5 3.9 %collective-permute-done.4.refs_1_ = bf16[512,256]{1,0:T(8,128)(2,1)S(1)} collective-permute-done((bf16[512,256]{1,0:T(8,128)(2,1)S(1)}, bf16[512,256]{1,0:T(8,128)(2,1)S(1)}, u32[]{:S(2)}, u32[]{:S(2)}) %collective-permute-start.4) | collective-permute-done | bytes 262176 | tf_op jit(solution)/shard_map/ppermute | solution.py:34
  30.4 3.7 %collective-permute-start.6 = (bf16[512,256]{1,0:T(8,128)(2,1)S(1)}, bf16[512,256]{1,0:T(8,128)(2,1)S(1)}, u32[]{:S(2)}, u32[]{:S(2)}) collective-permute-start(bf16[512,256]{1,0:T(8,128)(2,1)S(1)} %collective-permute-done.4.refs_1_), channel_id=1, source_target_pairs={{8,0},{16,8},{24,16},{32,24},{40,32},{48,40},{56,48},{0,56},{9,1},... | collective-permute-start | bytes 786440 | tf_op jit(solution)/shard_map/ppermute | solution.py:34
  34.1 4.1 %collective-permute-done.6.refs_3_ = bf16[512,256]{1,0:T(8,128)(2,1)S(1)} collective-permute-done((bf16[512,256]{1,0:T(8,128)(2,1)S(1)}, bf16[512,256]{1,0:T(8,128)(2,1)S(1)}, u32[]{:S(2)}, u32[]{:S(2)}) %collective-permute-start.6) | collective-permute-done | bytes 262176 | tf_op jit(solution)/shard_map/ppermute | solution.py:34
  38.3 3.7 %collective-permute-start.8 = (bf16[512,256]{1,0:T(8,128)(2,1)S(1)}, bf16[512,256]{1,0:T(8,128)(2,1)S(1)}, u32[]{:S(2)}, u32[]{:S(2)}) collective-permute-start(bf16[512,256]{1,0:T(8,128)(2,1)S(1)} %collective-permute-done.6.refs_3_), channel_id=1, source_target_pairs={{8,0},{16,8},{24,16},{32,24},{40,32},{48,40},{56,48},{0,56},{9,1},... | collective-permute-start | bytes 786440 | tf_op jit(solution)/shard_map/ppermute | solution.py:34
  42.2 4.4 %collective-permute-done.8.refs_0_ = bf16[512,256]{1,0:T(8,128)(2,1)S(1)} collective-permute-done((bf16[512,256]{1,0:T(8,128)(2,1)S(1)}, bf16[512,256]{1,0:T(8,128)(2,1)S(1)}, u32[]{:S(2)}, u32[]{:S(2)}) %collective-permute-start.8) | collective-permute-done | bytes 262176 | tf_op jit(solution)/shard_map/ppermute | solution.py:34
  46.7 3.8 %collective-permute-start.10 = (bf16[256,256]{1,0:T(8,128)(2,1)S(1)}, bf16[256,256]{1,0:T(8,128)(2,1)S(1)}, u32[]{:S(2)}, u32[]{:S(2)}) collective-permute-start(bf16[256,256]{1,0:T(8,128)(2,1)S(1)} %slice.16), channel_id=1, source_target_pairs={{8,0},{16,8},{24,16},{32,24},{40,32},{48,40},{56,48},{0,56},{9,1},... | collective-permute-start | bytes 393224 | tf_op jit(solution)/shard_map/ppermute | solution.py:34
  51.1 3.9 %shard_map.109 = (bf16[448,128]{1,0:T(8,128)(2,1)S(1)}, f32[448,128]{1,0:T(8,128)S(1)}, f32[448,128]{1,0:T(8,128)S(1)}, f32[448,128]{1,0:T(8,128)S(1)}) custom-call(s32[4]{0:T(128)S(1)} %pad_add_fusion.at_ref, s32[64]{0:T(128)S(1)} %copy-done.4, bf16[64,896]{1,0:T(8,128)(2,1)S(1)} %copy-done.5, ...), custom_call_target="tpu_custom_call" | custom-call | flops 587202560 | bytes 1310720 | tf_op jit(solution)/shard_map/pallas_call | solution.py:407
  57.2 6.5 %shard_map.110 = (bf16[32,3584]{1,0:T(8,128)(2,1)S(1)}, bf16[32,3584]{1,0:T(8,128)(2,1)S(1)}) custom-call(s32[4]{0:T(128)S(1)} %pad_add_fusion.at_ref, s32[64]{0:T(128)S(1)} %copy-done.4, bf16[448,128]{1,0:T(8,128)(2,1)S(1)} %get-tuple-element.39.q_all, f32[448,128]{1,0:T(8,128)S(1)} %get-tuple-element.40.top_ref, ...), custom_call_target="tpu_custom_call" | custom-call | flops 763363328 | bytes 7208960 | tf_op jit(solution)/shard_map/pallas_call | solution.py:426
  83.2 10.4 %collective-permute-done.17.refs_1_ = bf16[64,3584]{1,0:T(8,128)(2,1)S(1)} collective-permute-done((bf16[64,3584]{1,0:T(8,128)(2,1)S(1)}, bf16[64,3584]{1,0:T(8,128)(2,1)S(1)}, u32[]{:S(2)}, u32[]{:S(2)}) %collective-permute-start.17) | collective-permute-done | bytes 458784 | tf_op jit(solution)/shard_map/ppermute | solution.py:34
  97.7 10.9 %collective-permute-done.19.refs_0_ = bf16[64,3584]{1,0:T(8,128)(2,1)S(1)} collective-permute-done((bf16[64,3584]{1,0:T(8,128)(2,1)S(1)}, bf16[64,3584]{1,0:T(8,128)(2,1)S(1)}, u32[]{:S(2)}, u32[]{:S(2)}) %collective-permute-start.19) | collective-permute-done | bytes 458784 | tf_op jit(solution)/shard_map/ppermute | solution.py:34
  110.7 4.4 %shard_map.115 = (bf16[1280,3584]{1,0:T(8,128)(2,1)S(1)}, bf16[640,3584]{1,0:T(8,128)(2,1)S(1)}) custom-call(bf16[320,3584]{1,0:T(8,128)(2,1)S(1)} %bitcast.8, bf16[320,3584]{1,0:T(8,128)(2,1)S(1)} %bitcast.10, bf16[320,3584]{1,0:T(8,128)(2,1)S(1)} %copy-done.2, bf16[480,3584]{1,0:T(8,128)(2,1)} %collective-permute-done.23.a_any, ...), custom_call_target="tpu_custom_call" | custom-call | bytes 13762560 | tf_op jit(solution)/shard_map/pallas_call | solution.py:467
  115.1 5.7 %collective-permute-done.20.refs_2_ = bf16[64,3584]{1,0:T(8,128)(2,1)S(1)} collective-permute-done((bf16[64,3584]{1,0:T(8,128)(2,1)S(1)}, bf16[64,3584]{1,0:T(8,128)(2,1)S(1)}, u32[]{:S(2)}, u32[]{:S(2)}) %collective-permute-start.20) | collective-permute-done | bytes 458784 | tf_op jit(solution)/shard_map/ppermute | solution.py:34
  125.4 6.2 %shard_map.116 = (bf16[64,3584]{1,0:T(8,128)(2,1)S(1)}, bf16[64,3584]{1,0:T(8,128)(2,1)S(1)}, bf16[64,3584]{1,0:T(8,128)(2,1)S(1)}, bf16[64,3584]{1,0:T(8,128)(2,1)S(1)}) custom-call(bf16[64,3584]{1,0:T(8,128)(2,1)S(1)} %collective-permute-done.19.refs_0_, bf16[64,3584]{1,0:T(8,128)(2,1)S(1)} %collective-permute-done.21.refs_1_, ...), custom_call_target="tpu_custom_call" | custom-call | flops 3523215360 | bytes 17432576 | tf_op jit(solution)/shard_map/pallas_call | solution.py:332
  131.5 5.1 %shard_map.118 = (bf16[32,3584]{1,0:T(8,128)(2,1)S(1)}, bf16[32,3584]{1,0:T(8,128)(2,1)S(1)}) custom-call(bf16[32,3584]{1,0:T(8,128)(2,1)S(1)} %collective-permute-done.25.refs_0_, bf16[32,3584]{1,0:T(8,128)(2,1)S(1)} %collective-permute-done.26.refs_1_, bf16[1280,3584]{1,0:T(8,128)(2,1)S(1)} %get-tuple-element.56.refs_4_.refs_3_.refs_2_, ...), custom_call_target="tpu_custom_call" | custom-call | flops 880803840 | bytes 14680064 | tf_op jit(solution)/shard_map/pallas_call | solution.py:332
  138.8 4.4 %collective-permute-done.31.refs_1_ = bf16[32,3584]{1,0:T(8,128)(2,1)S(1)} collective-permute-done((bf16[32,3584]{1,0:T(8,128)(2,1)S(1)}, bf16[32,3584]{1,0:T(8,128)(2,1)S(1)}, u32[]{:S(2)}, u32[]{:S(2)}) %collective-permute-start.31) | collective-permute-done | bytes 229408 | tf_op jit(solution)/shard_map/ppermute | solution.py:34
  145.8 7.8 %collective-permute-done.32.refs_1_ = bf16[64,3584]{1,0:T(8,128)(2,1)S(1)} collective-permute-done((bf16[64,3584]{1,0:T(8,128)(2,1)S(1)}, bf16[64,3584]{1,0:T(8,128)(2,1)S(1)}, u32[]{:S(2)}, u32[]{:S(2)}) %collective-permute-start.32) | collective-permute-done | bytes 458784 | tf_op jit(solution)/shard_map/ppermute | solution.py:34
  156.7 6.2 %shard_map.117 = (bf16[64,3584]{1,0:T(8,128)(2,1)S(1)}, bf16[64,3584]{1,0:T(8,128)(2,1)S(1)}, bf16[64,3584]{1,0:T(8,128)(2,1)S(1)}) custom-call(bf16[64,3584]{1,0:T(8,128)(2,1)S(1)} %shard_map.113.refs_0_, bf16[64,3584]{1,0:T(8,128)(2,1)S(1)} %collective-permute-done.17.refs_1_, bf16[64,3584]{1,0:T(8,128)(2,1)S(1)} %collective-permute-done.18.refs_2_, ...), custom_call_target="tpu_custom_call" | custom-call | flops 2642411520 | bytes 16515072 | tf_op jit(solution)/shard_map/pallas_call | solution.py:332
  163.4 3.5 %collective-permute-start.34 = (bf16[64,3584]{1,0:T(8,128)(2,1)S(1)}, bf16[64,3584]{1,0:T(8,128)(2,1)S(1)}, u32[]{:S(2)}, u32[]{:S(2)}) collective-permute-start(bf16[64,3584]{1,0:T(8,128)(2,1)S(1)} %shard_map.124), channel_id=1, source_target_pairs={{8,0},{16,8},{24,16},{32,24},{40,32},{48,40},{56,48},{0,56},{9,1},... | collective-permute-start | bytes 1376264 | tf_op jit(solution)/shard_map/ppermute | solution.py:34
  167.3 5.6 %collective-permute-done.34.refs_2_ = bf16[64,3584]{1,0:T(8,128)(2,1)S(1)} collective-permute-done((bf16[64,3584]{1,0:T(8,128)(2,1)S(1)}, bf16[64,3584]{1,0:T(8,128)(2,1)S(1)}, u32[]{:S(2)}, u32[]{:S(2)}) %collective-permute-start.34) | collective-permute-done | bytes 458784 | tf_op jit(solution)/shard_map/ppermute | solution.py:34
  173.0 4.1 %collective-permute-done.30.refs_1_ = bf16[64,3584]{1,0:T(8,128)(2,1)S(1)} collective-permute-done((bf16[64,3584]{1,0:T(8,128)(2,1)S(1)}, bf16[64,3584]{1,0:T(8,128)(2,1)S(1)}, u32[]{:S(2)}, u32[]{:S(2)}) %collective-permute-start.30) | collective-permute-done | bytes 458784 | tf_op jit(solution)/shard_map/ppermute | solution.py:34
  180.5 4.0 %collective-permute-done.35.refs_1_ = bf16[16,3584]{1,0:T(8,128)(2,1)S(1)} collective-permute-done((bf16[16,3584]{1,0:T(8,128)(2,1)S(1)}, bf16[16,3584]{1,0:T(8,128)(2,1)S(1)}, u32[]{:S(2)}, u32[]{:S(2)}) %collective-permute-start.35) | collective-permute-done | bytes 114720 | tf_op jit(solution)/shard_map/ppermute | solution.py:34
  (100 shorter events, 59.7 us)
Async XLA Ops:
  10.1 85.6 %collective-permute-start.23 = (bf16[480,3584]{1,0:T(8,128)(2,1)}, bf16[480,3584]{1,0:T(8,128)(2,1)}, u32[]{:S(2)}, u32[]{:S(2)}) collective-permute-start(bf16[480,3584]{1,0:T(8,128)(2,1)} %shard_map.114), channel_id=1, source_target_pairs={{0,6},{6,0},{2,4},{4,2},{1,7},{7,1},{3,5},{5,3},{8,14},{14,8},{10,... | collective-permute-start | bytes 10321928 | tf_op jit(solution)/shard_map/ppermute | solution.py:397
  20.7 9.7 %collective-permute-start.4 = (bf16[512,256]{1,0:T(8,128)(2,1)S(1)}, bf16[512,256]{1,0:T(8,128)(2,1)S(1)}, u32[]{:S(2)}, u32[]{:S(2)}) collective-permute-start(bf16[512,256]{1,0:T(8,128)(2,1)S(1)} %constant_dynamic-update-slice_fusion.2.refs_0_), channel_id=1, source_target_pairs={{8,0},{16,8},{24,16},{32,24},{40,32},{48,40},{56,48},{0,56},{9,1},... | collective-permute-start | bytes 786440 | tf_op jit(solution)/shard_map/ppermute | solution.py:34
  26.5 7.6 %collective-permute-start.5 = (bf16[512,256]{1,0:T(8,128)(2,1)S(1)}, bf16[512,256]{1,0:T(8,128)(2,1)S(1)}, u32[]{:S(2)}, u32[]{:S(2)}) collective-permute-start(bf16[512,256]{1,0:T(8,128)(2,1)S(1)} %constant_dynamic-update-slice_fusion.2.refs_0_), channel_id=1, source_target_pairs={{56,0},{0,8},{8,16},{16,24},{24,32},{32,40},{40,48},{48,56},{57,1}... | collective-permute-start | bytes 786440 | tf_op jit(solution)/shard_map/ppermute | solution.py:34
  30.4 7.8 %collective-permute-start.6 = (bf16[512,256]{1,0:T(8,128)(2,1)S(1)}, bf16[512,256]{1,0:T(8,128)(2,1)S(1)}, u32[]{:S(2)}, u32[]{:S(2)}) collective-permute-start(bf16[512,256]{1,0:T(8,128)(2,1)S(1)} %collective-permute-done.4.refs_1_), channel_id=1, source_target_pairs={{8,0},{16,8},{24,16},{32,24},{40,32},{48,40},{56,48},{0,56},{9,1},... | collective-permute-start | bytes 786440 | tf_op jit(solution)/shard_map/ppermute | solution.py:34
  34.1 8.1 %collective-permute-start.7 = (bf16[512,256]{1,0:T(8,128)(2,1)S(1)}, bf16[512,256]{1,0:T(8,128)(2,1)S(1)}, u32[]{:S(2)}, u32[]{:S(2)}) collective-permute-start(bf16[512,256]{1,0:T(8,128)(2,1)S(1)} %collective-permute-done.5.refs_2_), channel_id=1, source_target_pairs={{56,0},{0,8},{8,16},{16,24},{24,32},{32,40},{40,48},{48,56},{57,1}... | collective-permute-start | bytes 786440 | tf_op jit(solution)/shard_map/ppermute | solution.py:34
  38.3 8.4 %collective-permute-start.8 = (bf16[512,256]{1,0:T(8,128)(2,1)S(1)}, bf16[512,256]{1,0:T(8,128)(2,1)S(1)}, u32[]{:S(2)}, u32[]{:S(2)}) collective-permute-start(bf16[512,256]{1,0:T(8,128)(2,1)S(1)} %collective-permute-done.6.refs_3_), channel_id=1, source_target_pairs={{8,0},{16,8},{24,16},{32,24},{40,32},{48,40},{56,48},{0,56},{9,1},... | collective-permute-start | bytes 786440 | tf_op jit(solution)/shard_map/ppermute | solution.py:34
  42.2 8.7 %collective-permute-start.9 = (bf16[512,256]{1,0:T(8,128)(2,1)S(1)}, bf16[512,256]{1,0:T(8,128)(2,1)S(1)}, u32[]{:S(2)}, u32[]{:S(2)}) collective-permute-start(bf16[512,256]{1,0:T(8,128)(2,1)S(1)} %collective-permute-done.7.refs_4_), channel_id=1, source_target_pairs={{56,0},{0,8},{8,16},{16,24},{24,32},{32,40},{40,48},{48,56},{57,1}... | collective-permute-start | bytes 786440 | tf_op jit(solution)/shard_map/ppermute | solution.py:34
  46.7 8.3 %collective-permute-start.10 = (bf16[256,256]{1,0:T(8,128)(2,1)S(1)}, bf16[256,256]{1,0:T(8,128)(2,1)S(1)}, u32[]{:S(2)}, u32[]{:S(2)}) collective-permute-start(bf16[256,256]{1,0:T(8,128)(2,1)S(1)} %slice.16), channel_id=1, source_target_pairs={{8,0},{16,8},{24,16},{32,24},{40,32},{48,40},{56,48},{0,56},{9,1},... | collective-permute-start | bytes 393224 | tf_op jit(solution)/shard_map/ppermute | solution.py:34
  73.6 7.5 %collective-permute-start.16 = (bf16[16,3584]{1,0:T(8,128)(2,1)S(1)}, bf16[16,3584]{1,0:T(8,128)(2,1)S(1)}, u32[]{:S(2)}, u32[]{:S(2)}) collective-permute-start(bf16[16,3584]{1,0:T(8,128)(2,1)S(1)} %get-tuple-element.48.refs_0_), channel_id=1, source_target_pairs={{192,0},{0,64},{64,128},{128,192},{193,1},{1,65},{65,129},{129,193... | collective-permute-start | bytes 344072 | tf_op jit(solution)/shard_map/ppermute | solution.py:34
  81.1 12.5 %collective-permute-start.17 = (bf16[64,3584]{1,0:T(8,128)(2,1)S(1)}, bf16[64,3584]{1,0:T(8,128)(2,1)S(1)}, u32[]{:S(2)}, u32[]{:S(2)}) collective-permute-start(bf16[64,3584]{1,0:T(8,128)(2,1)S(1)} %shard_map.113.refs_0_), channel_id=1, source_target_pairs={{8,0},{16,8},{24,16},{32,24},{40,32},{48,40},{56,48},{0,56},{9,1},... | collective-permute-start | bytes 1376264 | tf_op jit(solution)/shard_map/ppermute | solution.py:34
  82.3 13.4 %collective-permute-start.18 = (bf16[64,3584]{1,0:T(8,128)(2,1)S(1)}, bf16[64,3584]{1,0:T(8,128)(2,1)S(1)}, u32[]{:S(2)}, u32[]{:S(2)}) collective-permute-start(bf16[64,3584]{1,0:T(8,128)(2,1)S(1)} %shard_map.113.refs_0_), channel_id=1, source_target_pairs={{56,0},{0,8},{8,16},{16,24},{24,32},{32,40},{40,48},{48,56},{57,1}... | collective-permute-start | bytes 1376264 | tf_op jit(solution)/shard_map/ppermute | solution.py:34
  95.7 15.0 %collective-permute-start.24 = (bf16[480,3584]{1,0:T(8,128)(2,1)}, bf16[480,3584]{1,0:T(8,128)(2,1)S(1)}, u32[]{:S(2)}, u32[]{:S(2)}) collective-permute-start(bf16[480,3584]{1,0:T(8,128)(2,1)} %collective-permute-done.23.a_any), channel_id=1, source_target_pairs={{1,0},{0,1},{3,2},{2,3},{5,4},{4,5},{7,6},{6,7},{9,8},{8,9},{11,10... | collective-permute-start | bytes 10321928 | tf_op jit(solution)/shard_map/ppermute | solution.py:34
  95.7 12.9 %collective-permute-start.19 = (bf16[64,3584]{1,0:T(8,128)(2,1)S(1)}, bf16[64,3584]{1,0:T(8,128)(2,1)S(1)}, u32[]{:S(2)}, u32[]{:S(2)}) collective-permute-start(bf16[64,3584]{1,0:T(8,128)(2,1)S(1)} %collective-permute-done.17.refs_1_), channel_id=1, source_target_pairs={{8,0},{16,8},{24,16},{32,24},{40,32},{48,40},{56,48},{0,56},{9,1},... | collective-permute-start | bytes 1376264 | tf_op jit(solution)/shard_map/ppermute | solution.py:34
  96.1 14.1 %collective-permute-start.21 = (bf16[64,3584]{1,0:T(8,128)(2,1)S(1)}, bf16[64,3584]{1,0:T(8,128)(2,1)S(1)}, u32[]{:S(2)}, u32[]{:S(2)}) collective-permute-start(bf16[64,3584]{1,0:T(8,128)(2,1)S(1)} %collective-permute-done.18.refs_2_), channel_id=1, source_target_pairs={{56,0},{0,8},{8,16},{16,24},{24,32},{32,40},{40,48},{48,56},{57,1}... | collective-permute-start | bytes 1376264 | tf_op jit(solution)/shard_map/ppermute | solution.py:34
  108.6 12.2 %collective-permute-start.20 = (bf16[64,3584]{1,0:T(8,128)(2,1)S(1)}, bf16[64,3584]{1,0:T(8,128)(2,1)S(1)}, u32[]{:S(2)}, u32[]{:S(2)}) collective-permute-start(bf16[64,3584]{1,0:T(8,128)(2,1)S(1)} %collective-permute-done.19.refs_0_), channel_id=1, source_target_pairs={{8,0},{16,8},{24,16},{32,24},{40,32},{48,40},{56,48},{0,56},{9,1},... | collective-permute-start | bytes 1376264 | tf_op jit(solution)/shard_map/ppermute | solution.py:34
  110.1 13.0 %collective-permute-start.22 = (bf16[64,3584]{1,0:T(8,128)(2,1)S(1)}, bf16[64,3584]{1,0:T(8,128)(2,1)S(1)}, u32[]{:S(2)}, u32[]{:S(2)}) collective-permute-start(bf16[64,3584]{1,0:T(8,128)(2,1)S(1)} %collective-permute-done.21.refs_1_), channel_id=1, source_target_pairs={{56,0},{0,8},{8,16},{16,24},{24,32},{32,40},{40,48},{48,56},{57,1}... | collective-permute-start | bytes 1376264 | tf_op jit(solution)/shard_map/ppermute | solution.py:34
  123.2 8.4 %collective-permute-start.25 = (bf16[32,3584]{1,0:T(8,128)(2,1)S(1)}, bf16[32,3584]{1,0:T(8,128)(2,1)S(1)}, u32[]{:S(2)}, u32[]{:S(2)}) collective-permute-start(bf16[32,3584]{1,0:T(8,128)(2,1)S(1)} %slice.14), channel_id=1, source_target_pairs={{8,0},{16,8},{24,16},{32,24},{40,32},{48,40},{56,48},{0,56},{9,1},... | collective-permute-start | bytes 688136 | tf_op jit(solution)/shard_map/ppermute | solution.py:34
  123.5 8.0 %collective-permute-start.26 = (bf16[32,3584]{1,0:T(8,128)(2,1)S(1)}, bf16[32,3584]{1,0:T(8,128)(2,1)S(1)}, u32[]{:S(2)}, u32[]{:S(2)}) collective-permute-start(bf16[32,3584]{1,0:T(8,128)(2,1)S(1)} %slice.15), channel_id=1, source_target_pairs={{56,0},{0,8},{8,16},{16,24},{24,32},{32,40},{40,48},{48,56},{57,1}... | collective-permute-start | bytes 688136 | tf_op jit(solution)/shard_map/ppermute | solution.py:34
  143.3 10.4 %collective-permute-start.32 = (bf16[64,3584]{1,0:T(8,128)(2,1)S(1)}, bf16[64,3584]{1,0:T(8,128)(2,1)S(1)}, u32[]{:S(2)}, u32[]{:S(2)}) collective-permute-start(bf16[64,3584]{1,0:T(8,128)(2,1)S(1)} %shard_map.122), channel_id=1, source_target_pairs={{8,0},{16,8},{24,16},{32,24},{40,32},{48,40},{56,48},{0,56},{9,1},... | collective-permute-start | bytes 1376264 | tf_op jit(solution)/shard_map/ppermute | solution.py:34
  145.7 10.8 %collective-permute-start.28 = (bf16[64,3584]{1,0:T(8,128)(2,1)S(1)}, bf16[64,3584]{1,0:T(8,128)(2,1)S(1)}, u32[]{:S(2)}, u32[]{:S(2)}) collective-permute-start(bf16[64,3584]{1,0:T(8,128)(2,1)S(1)} %shard_map.119), channel_id=1, source_target_pairs={{56,0},{0,8},{8,16},{16,24},{24,32},{32,40},{40,48},{48,56},{57,1}... | collective-permute-start | bytes 1376264 | tf_op jit(solution)/shard_map/ppermute | solution.py:34
  153.8 9.6 %collective-permute-start.33 = (bf16[64,3584]{1,0:T(8,128)(2,1)S(1)}, bf16[64,3584]{1,0:T(8,128)(2,1)S(1)}, u32[]{:S(2)}, u32[]{:S(2)}) collective-permute-start(bf16[64,3584]{1,0:T(8,128)(2,1)S(1)} %shard_map.123), channel_id=1, source_target_pairs={{8,0},{16,8},{24,16},{32,24},{40,32},{48,40},{56,48},{0,56},{9,1},... | collective-permute-start | bytes 1376264 | tf_op jit(solution)/shard_map/ppermute | solution.py:34
  156.6 10.5 %collective-permute-start.29 = (bf16[64,3584]{1,0:T(8,128)(2,1)S(1)}, bf16[64,3584]{1,0:T(8,128)(2,1)S(1)}, u32[]{:S(2)}, u32[]{:S(2)}) collective-permute-start(bf16[64,3584]{1,0:T(8,128)(2,1)S(1)} %shard_map.120), channel_id=1, source_target_pairs={{56,0},{0,8},{8,16},{16,24},{24,32},{32,40},{40,48},{48,56},{57,1}... | collective-permute-start | bytes 1376264 | tf_op jit(solution)/shard_map/ppermute | solution.py:34
  163.4 9.5 %collective-permute-start.34 = (bf16[64,3584]{1,0:T(8,128)(2,1)S(1)}, bf16[64,3584]{1,0:T(8,128)(2,1)S(1)}, u32[]{:S(2)}, u32[]{:S(2)}) collective-permute-start(bf16[64,3584]{1,0:T(8,128)(2,1)S(1)} %shard_map.124), channel_id=1, source_target_pairs={{8,0},{16,8},{24,16},{32,24},{40,32},{48,40},{56,48},{0,56},{9,1},... | collective-permute-start | bytes 1376264 | tf_op jit(solution)/shard_map/ppermute | solution.py:34
  167.2 9.8 %collective-permute-start.30 = (bf16[64,3584]{1,0:T(8,128)(2,1)S(1)}, bf16[64,3584]{1,0:T(8,128)(2,1)S(1)}, u32[]{:S(2)}, u32[]{:S(2)}) collective-permute-start(bf16[64,3584]{1,0:T(8,128)(2,1)S(1)} %shard_map.121), channel_id=1, source_target_pairs={{56,0},{0,8},{8,16},{16,24},{24,32},{32,40},{40,48},{48,56},{57,1}... | collective-permute-start | bytes 1376264 | tf_op jit(solution)/shard_map/ppermute | solution.py:34
  (22 other events, 370.1 us)

commit v4 on v3

--- a/solution.py
+++ b/solution.py
@@ -53,35 +53,50 @@
     return [fetch(ahead[:rows], axis, 1), fetch(behind[rows:], axis, -1)]
 
 
-def add_kernel(n_in, first, *refs):
+def add_kernel(n_in, *refs):
     ins, outs = refs[:n_in], refs[n_in:]
     rows = outs[0].shape[0]
     for i, out in enumerate(outs):
         part = ins[0][i * rows : (i + 1) * rows, :].astype(f32)
         for other in ins[1:]:
-            if other.shape[0] == ins[0].shape[0]:
-                part += other[i * rows : (i + 1) * rows, :].astype(f32)
+            part += other[i * rows : (i + 1) * rows, :].astype(f32)
         out[...] = part.astype(out.dtype)
-    last = ins[-1]
-    if last.shape[0] < ins[0].shape[0]:
-        mine = slice(first, first + last.shape[0])
-        outs[0][mine, :] = (ins[0][mine, :].astype(f32) + last[...].astype(f32)).astype(bf16)
-
-
-def add(xs, pieces=1, first=0):
+
+
+def halves_kernel(x, low, high, out):
+    rows = low.shape[0]
+    out[:rows, :] = (x[:rows, :].astype(f32) + low[...].astype(f32)).astype(bf16)
+    out[rows:, :] = (x[rows:, :].astype(f32) + high[...].astype(f32)).astype(bf16)
+
+
+def cost_of_add(size, terms):
+    return pl.CostEstimate(
+        flops=size * terms, bytes_accessed=2 * size * (terms + 1), transcendentals=0
+    )
+
+
+def add(xs, pieces=1):
     rows, width = xs[0].shape
-    size = rows * width
     out = pl.pallas_call(
-        functools.partial(add_kernel, len(xs), first),
+        functools.partial(add_kernel, len(xs)),
         out_shape=[jax.ShapeDtypeStruct((rows // pieces, width), bf16)] * pieces,
         in_specs=[VMEM] * len(xs),
         out_specs=[VMEM] * pieces,
         compiler_params=SMALL,
-        cost_estimate=pl.CostEstimate(
-            flops=size * len(xs), bytes_accessed=2 * size * (len(xs) + 1), transcendentals=0
-        ),
+        cost_estimate=cost_of_add(rows * width, len(xs)),
     )(*xs)
     return out[0] if pieces == 1 else out
+
+
+def add_halves(x, low, high):
+    return pl.pallas_call(
+        halves_kernel,
+        out_shape=jax.ShapeDtypeStruct(x.shape, bf16),
+        in_specs=[VMEM] * 3,
+        out_specs=VMEM,
+        compiler_params=SMALL,
+        cost_estimate=cost_of_add(x.size, 2),
+    )(x, low, high)
 
 
 def scatter_direct(chunks, axis):
@@ -91,12 +106,17 @@
 def scatter_ring(near, far, axis):
     n = SIZES[axis]
     h = n // 2
-    up = fetch(far[0], axis, -1)
-    down = fetch(far[1], axis, 1)
-    for k in range(h - 1, 0, -1):
-        first = near[k].shape[0] - down.shape[0]
+    low, up_high = near[h - 1]
+    down_low, high = near[h + 1]
+    early = fetch(up_high, axis, -1), fetch(down_low, axis, 1)
+    far, (up_high, down_low) = lax.optimization_barrier((list(far), early))
+    up_low = fetch(add([low, fetch(far[0], axis, -1)]), axis, -1)
+    down_high = fetch(add([high, fetch(far[1], axis, 1)]), axis, 1)
+    up = fetch(add_halves(near[h - 2], up_low, up_high), axis, -1)
+    down = fetch(add_halves(near[h + 2], down_low, down_high), axis, 1)
+    for k in range(h - 3, 0, -1):
         up = fetch(add([near[k], up]), axis, -1)
-        down = fetch(add([near[n - k], down], first=first), axis, 1)
+        down = fetch(add([near[n - k], down]), axis, 1)
     return [near[0], up, down]
 
 
@@ -325,15 +345,16 @@
     )(*xs)
 
 
-def expert(xs, weights):
+def expert(xs, weights, parts=None):
     w, d = weights
     rows, width = sum(x.shape[0] for x in xs), xs[0].shape[1]
     units = d.shape[0]
+    parts = parts or [x.shape[0] for x in xs]
     return pl.pallas_call(
         functools.partial(expert_kernel, len(xs)),
-        out_shape=[jax.ShapeDtypeStruct(x.shape, bf16) for x in xs],
+        out_shape=[jax.ShapeDtypeStruct((n, width), bf16) for n in parts],
         in_specs=[VMEM] * (len(xs) + 2),
-        out_specs=[VMEM] * len(xs),
+        out_specs=[VMEM] * len(parts),
         scratch_shapes=[pltpu.VMEM((rows, width), bf16), pltpu.VMEM((rows, units), bf16)],
         compiler_params=pltpu.CompilerParams(vmem_limit_bytes=30 << 20),
         cost_estimate=pl.CostEstimate(
@@ -480,13 +501,13 @@
     )(gate_t, up_t, down_weight, swap_a, swap_b)
     ahead_3, behind_3, weights = lax.optimization_barrier((ahead[3], behind[3], weights))
     far = gather_far(ahead_3, behind_3, "z")
-    after_2, before_2, after_3, before_3 = expert(
-        [ahead[2], behind[2], ahead[3], behind[3]], weights
+    after_2, before_2, *third = expert(
+        [ahead[2], behind[2], ahead[3], behind[3]], weights, [tokens] * 2 + [half] * 4
     )
-    weights, after_3 = lax.optimization_barrier((weights, after_3))
+    weights, third = lax.optimization_barrier((weights, third))
     far_parts = expert(far, weights)
     own, after, before = expert([ahead[0], ahead[1], behind[1]], weights)
-    near_parts = [own, after, after_2, after_3, None, before_3, before_2, before]
+    near_parts = [own, after, after_2, third[:2], None, third[2:], before_2, before]
     by_y = add(scatter_ring(near_parts, far_parts, "z"), pieces=4)
     terms = scatter_direct(by_y, "y")
     return pl.pallas_call(

time: 187 us -> 193 us (1.032)
  starting transfers between devices: 52.1 us -> 57.3 us
    ppermute x37 -> x39, starting transfers between devices: 51 us -> 56.2 us  [fetch(): return lax.ppermute(x, axis, [((i + k) % n, i) for i in range(n)])]
    ppermute x37 -> x39, waiting for transfers between devices: 94.3 us -> 94.4 us  [fetch(): return lax.ppermute(x, axis, [((i + k) % n, i) for i in range(n)])]
  transfers between devices with their start and end apart: 38 -> 40, of which waited for: 28 -> 29; matrix products, arithmetic and copies ran while one was open for 0% -> 0% of each run, Pallas kernels for 15% -> 18%
where the time goes in v4:
time: 193 us; the launch traced here: 191 us
  waiting for transfers between devices  94.4 us (49%)
  starting transfers between devices  57.3 us (30%)
  Pallas kernels  37.8 us (20%)
    ppermute x39, waiting for transfers between devices, fetch(): return lax.ppermute(x, axis, [((i + k) % n, i) for i in range(n)])  94.4 us
    ppermute x39, starting transfers between devices, fetch(): return lax.ppermute(x, axis, [((i + k) % n, i) for i in range(n)])  56.2 us
    pallas_call x3, Pallas kernels, expert(): pl.pallas_call(functools.partial(expert_kernel, len(xs)), out_shape=[jax....  17.4 us
    pallas_call x1, Pallas kernels, per_device(): pl.pallas_call(functools.partial(project_kernel, steps), out_shape=[jax.S...  6.5 us
    pallas_call x1, Pallas kernels, per_device(): pl.pallas_call(assemble_kernel, out_shape=[jax.ShapeDtypeStruct((4 * hidd...  4.42 us
    pallas_call x1, Pallas kernels, per_device(): pl.pallas_call(functools.partial(attention_kernel, steps), out_shape=[jax...  3.89 us
  transfers between devices with their start and end apart: 40, of which 29 were waited for; matrix products, arithmetic and copies ran while one was open for 0% of the time, Pallas kernels for 18%

profile of v4, /device:TPU:0, one launch (start us, length us, event | category | flops | bytes accessed | tf_op | source)
XLA Modules:
  0.0 191.4 jit_solution(15321612493419372567)
XLA Ops:
  2.8 4.1 %collective-permute-done = bf16[64,256]{1,0:T(8,128)(2,1)S(1)} collective-permute-done((bf16[64,256]{1,0:T(8,128)(2,1)S(1)}, bf16[64,256]{1,0:T(8,128)(2,1)S(1)}, u32[]{:S(2)}, u32[]{:S(2)}) %collective-permute-start) | collective-permute-done | bytes 32800 | tf_op jit(solution)/shard_map/ppermute | solution.py:34
  16.1 3.9 %collective-permute-done.2 = bf16[128,256]{1,0:T(8,128)(2,1)S(1)} collective-permute-done((bf16[128,256]{1,0:T(8,128)(2,1)S(1)}, bf16[128,256]{1,0:T(8,128)(2,1)S(1)}, u32[]{:S(2)}, u32[]{:S(2)}) %collective-permute-start.2) | collective-permute-done | bytes 65568 | tf_op jit(solution)/shard_map/ppermute | solution.py:34
  20.7 5.9 %collective-permute-start.4 = (bf16[512,256]{1,0:T(8,128)(2,1)S(1)}, bf16[512,256]{1,0:T(8,128)(2,1)S(1)}, u32[]{:S(2)}, u32[]{:S(2)}) collective-permute-start(bf16[512,256]{1,0:T(8,128)(2,1)S(1)} %constant_dynamic-update-slice_fusion.2.refs_0_), channel_id=1, source_target_pairs={{8,0},{16,8},{24,16},{32,24},{40,32},{48,40},{56,48},{0,56},{9,1},... | collective-permute-start | bytes 786440 | tf_op jit(solution)/shard_map/ppermute | solution.py:34
  26.5 3.9 %collective-permute-done.4.refs_1_ = bf16[512,256]{1,0:T(8,128)(2,1)S(1)} collective-permute-done((bf16[512,256]{1,0:T(8,128)(2,1)S(1)}, bf16[512,256]{1,0:T(8,128)(2,1)S(1)}, u32[]{:S(2)}, u32[]{:S(2)}) %collective-permute-start.4) | collective-permute-done | bytes 262176 | tf_op jit(solution)/shard_map/ppermute | solution.py:34
  30.4 3.7 %collective-permute-start.6 = (bf16[512,256]{1,0:T(8,128)(2,1)S(1)}, bf16[512,256]{1,0:T(8,128)(2,1)S(1)}, u32[]{:S(2)}, u32[]{:S(2)}) collective-permute-start(bf16[512,256]{1,0:T(8,128)(2,1)S(1)} %collective-permute-done.4.refs_1_), channel_id=1, source_target_pairs={{8,0},{16,8},{24,16},{32,24},{40,32},{48,40},{56,48},{0,56},{9,1},... | collective-permute-start | bytes 786440 | tf_op jit(solution)/shard_map/ppermute | solution.py:34
  34.1 4.1 %collective-permute-done.6.refs_3_ = bf16[512,256]{1,0:T(8,128)(2,1)S(1)} collective-permute-done((bf16[512,256]{1,0:T(8,128)(2,1)S(1)}, bf16[512,256]{1,0:T(8,128)(2,1)S(1)}, u32[]{:S(2)}, u32[]{:S(2)}) %collective-permute-start.6) | collective-permute-done | bytes 262176 | tf_op jit(solution)/shard_map/ppermute | solution.py:34
  42.2 4.4 %collective-permute-done.8.refs_0_ = bf16[512,256]{1,0:T(8,128)(2,1)S(1)} collective-permute-done((bf16[512,256]{1,0:T(8,128)(2,1)S(1)}, bf16[512,256]{1,0:T(8,128)(2,1)S(1)}, u32[]{:S(2)}, u32[]{:S(2)}) %collective-permute-start.8) | collective-permute-done | bytes 262176 | tf_op jit(solution)/shard_map/ppermute | solution.py:34
  46.7 3.8 %collective-permute-start.10 = (bf16[256,256]{1,0:T(8,128)(2,1)S(1)}, bf16[256,256]{1,0:T(8,128)(2,1)S(1)}, u32[]{:S(2)}, u32[]{:S(2)}) collective-permute-start(bf16[256,256]{1,0:T(8,128)(2,1)S(1)} %slice.16), channel_id=1, source_target_pairs={{8,0},{16,8},{24,16},{32,24},{40,32},{48,40},{56,48},{0,56},{9,1},... | collective-permute-start | bytes 393224 | tf_op jit(solution)/shard_map/ppermute | solution.py:34
  51.1 3.9 %shard_map.109 = (bf16[448,128]{1,0:T(8,128)(2,1)S(1)}, f32[448,128]{1,0:T(8,128)S(1)}, f32[448,128]{1,0:T(8,128)S(1)}, f32[448,128]{1,0:T(8,128)S(1)}) custom-call(s32[4]{0:T(128)S(1)} %pad_add_fusion.at_ref, s32[64]{0:T(128)S(1)} %copy-done.4, bf16[64,896]{1,0:T(8,128)(2,1)S(1)} %copy-done.5, ...), custom_call_target="tpu_custom_call" | custom-call | flops 587202560 | bytes 1310720 | tf_op jit(solution)/shard_map/pallas_call | solution.py:428
  57.2 6.5 %shard_map.110 = (bf16[32,3584]{1,0:T(8,128)(2,1)S(1)}, bf16[32,3584]{1,0:T(8,128)(2,1)S(1)}) custom-call(s32[4]{0:T(128)S(1)} %pad_add_fusion.at_ref, s32[64]{0:T(128)S(1)} %copy-done.4, bf16[448,128]{1,0:T(8,128)(2,1)S(1)} %get-tuple-element.48.q_all, f32[448,128]{1,0:T(8,128)S(1)} %get-tuple-element.49.top_ref, ...), custom_call_target="tpu_custom_call" | custom-call | flops 763363328 | bytes 7208960 | tf_op jit(solution)/shard_map/pallas_call | solution.py:447
  83.2 10.4 %collective-permute-done.17.refs_1_ = bf16[64,3584]{1,0:T(8,128)(2,1)S(1)} collective-permute-done((bf16[64,3584]{1,0:T(8,128)(2,1)S(1)}, bf16[64,3584]{1,0:T(8,128)(2,1)S(1)}, u32[]{:S(2)}, u32[]{:S(2)}) %collective-permute-start.17) | collective-permute-done | bytes 458784 | tf_op jit(solution)/shard_map/ppermute | solution.py:34
  97.7 10.9 %collective-permute-done.19.refs_0_ = bf16[64,3584]{1,0:T(8,128)(2,1)S(1)} collective-permute-done((bf16[64,3584]{1,0:T(8,128)(2,1)S(1)}, bf16[64,3584]{1,0:T(8,128)(2,1)S(1)}, u32[]{:S(2)}, u32[]{:S(2)}) %collective-permute-start.19) | collective-permute-done | bytes 458784 | tf_op jit(solution)/shard_map/ppermute | solution.py:34
  110.7 4.4 %shard_map.115 = (bf16[1280,3584]{1,0:T(8,128)(2,1)S(1)}, bf16[640,3584]{1,0:T(8,128)(2,1)S(1)}) custom-call(bf16[320,3584]{1,0:T(8,128)(2,1)S(1)} %bitcast.8, bf16[320,3584]{1,0:T(8,128)(2,1)S(1)} %bitcast.10, bf16[320,3584]{1,0:T(8,128)(2,1)S(1)} %copy-done.2, bf16[480,3584]{1,0:T(8,128)(2,1)} %collective-permute-done.23.a_any, ...), custom_call_target="tpu_custom_call" | custom-call | bytes 13762560 | tf_op jit(solution)/shard_map/pallas_call | solution.py:488
  115.1 5.7 %collective-permute-done.20.refs_2_ = bf16[64,3584]{1,0:T(8,128)(2,1)S(1)} collective-permute-done((bf16[64,3584]{1,0:T(8,128)(2,1)S(1)}, bf16[64,3584]{1,0:T(8,128)(2,1)S(1)}, u32[]{:S(2)}, u32[]{:S(2)}) %collective-permute-start.20) | collective-permute-done | bytes 458784 | tf_op jit(solution)/shard_map/ppermute | solution.py:34
  125.4 6.2 %shard_map.116 = (bf16[64,3584]{1,0:T(8,128)(2,1)S(1)}, bf16[64,3584]{1,0:T(8,128)(2,1)S(1)}, bf16[32,3584]{1,0:T(8,128)(2,1)S(1)}, bf16[32,3584]{1,0:T(8,128)(2...) custom-call(bf16[64,3584]{1,0:T(8,128)(2,1)S(1)} %collective-permute-done.19.refs_0_, ...), custom_call_target="tpu_custom_call" | custom-call | flops 3523215360 | bytes 17432576 | tf_op jit(solution)/shard_map/pallas_call | solution.py:353
  134.8 5.1 %shard_map.118 = (bf16[32,3584]{1,0:T(8,128)(2,1)S(1)}, bf16[32,3584]{1,0:T(8,128)(2,1)S(1)}) custom-call(bf16[32,3584]{1,0:T(8,128)(2,1)S(1)} %collective-permute-done.25.refs_0_, bf16[32,3584]{1,0:T(8,128)(2,1)S(1)} %collective-permute-done.26.refs_1_, bf16[1280,3584]{1,0:T(8,128)(2,1)S(1)} %get-tuple-element.68.refs_4_.refs_3_.refs_2_, ...), custom_call_target="tpu_custom_call" | custom-call | flops 880803840 | bytes 14680064 | tf_op jit(solution)/shard_map/pallas_call | solution.py:353
  142.1 5.0 %collective-permute-done.33.refs_1_ = bf16[32,3584]{1,0:T(8,128)(2,1)S(1)} collective-permute-done((bf16[32,3584]{1,0:T(8,128)(2,1)S(1)}, bf16[32,3584]{1,0:T(8,128)(2,1)S(1)}, u32[]{:S(2)}, u32[]{:S(2)}) %collective-permute-start.33) | collective-permute-done | bytes 229408 | tf_op jit(solution)/shard_map/ppermute | solution.py:34
  150.3 5.2 %collective-permute-done.34.high = bf16[32,3584]{1,0:T(8,128)(2,1)S(1)} collective-permute-done((bf16[32,3584]{1,0:T(8,128)(2,1)S(1)}, bf16[32,3584]{1,0:T(8,128)(2,1)S(1)}, u32[]{:S(2)}, u32[]{:S(2)}) %collective-permute-start.34) | collective-permute-done | bytes 229408 | tf_op jit(solution)/shard_map/ppermute | solution.py:34
  155.6 3.8 %collective-permute-start.35 = (bf16[64,3584]{1,0:T(8,128)(2,1)S(1)}, bf16[64,3584]{1,0:T(8,128)(2,1)S(1)}, u32[]{:S(2)}, u32[]{:S(2)}) collective-permute-start(bf16[64,3584]{1,0:T(8,128)(2,1)S(1)} %shard_map.123), channel_id=1, source_target_pairs={{8,0},{16,8},{24,16},{32,24},{40,32},{48,40},{56,48},{0,56},{9,1},... | collective-permute-start | bytes 1376264 | tf_op jit(solution)/shard_map/ppermute | solution.py:34
  159.7 6.2 %shard_map.117 = (bf16[64,3584]{1,0:T(8,128)(2,1)S(1)}, bf16[64,3584]{1,0:T(8,128)(2,1)S(1)}, bf16[64,3584]{1,0:T(8,128)(2,1)S(1)}) custom-call(bf16[64,3584]{1,0:T(8,128)(2,1)S(1)} %shard_map.113.refs_0_, bf16[64,3584]{1,0:T(8,128)(2,1)S(1)} %collective-permute-done.17.refs_1_, bf16[64,3584]{1,0:T(8,128)(2,1)S(1)} %collective-permute-done.18.refs_2_, ...), custom_call_target="tpu_custom_call" | custom-call | flops 2642411520 | bytes 16515072 | tf_op jit(solution)/shard_map/pallas_call | solution.py:353
  168.3 3.8 %collective-permute-start.36 = (bf16[64,3584]{1,0:T(8,128)(2,1)S(1)}, bf16[64,3584]{1,0:T(8,128)(2,1)S(1)}, u32[]{:S(2)}, u32[]{:S(2)}) collective-permute-start(bf16[64,3584]{1,0:T(8,128)(2,1)S(1)} %shard_map.124), channel_id=1, source_target_pairs={{8,0},{16,8},{24,16},{32,24},{40,32},{48,40},{56,48},{0,56},{9,1},... | collective-permute-start | bytes 1376264 | tf_op jit(solution)/shard_map/ppermute | solution.py:34
  172.6 5.5 %collective-permute-done.36.refs_2_ = bf16[64,3584]{1,0:T(8,128)(2,1)S(1)} collective-permute-done((bf16[64,3584]{1,0:T(8,128)(2,1)S(1)}, bf16[64,3584]{1,0:T(8,128)(2,1)S(1)}, u32[]{:S(2)}, u32[]{:S(2)}) %collective-permute-start.36) | collective-permute-done | bytes 458784 | tf_op jit(solution)/shard_map/ppermute | solution.py:34
  178.1 4.2 %collective-permute-done.32.refs_1_ = bf16[64,3584]{1,0:T(8,128)(2,1)S(1)} collective-permute-done((bf16[64,3584]{1,0:T(8,128)(2,1)S(1)}, bf16[64,3584]{1,0:T(8,128)(2,1)S(1)}, u32[]{:S(2)}, u32[]{:S(2)}) %collective-permute-start.32) | collective-permute-done | bytes 458784 | tf_op jit(solution)/shard_map/ppermute | solution.py:34
  185.8 4.0 %collective-permute-done.37.refs_1_ = bf16[16,3584]{1,0:T(8,128)(2,1)S(1)} collective-permute-done((bf16[16,3584]{1,0:T(8,128)(2,1)S(1)}, bf16[16,3584]{1,0:T(8,128)(2,1)S(1)}, u32[]{:S(2)}, u32[]{:S(2)}) %collective-permute-start.37) | collective-permute-done | bytes 114720 | tf_op jit(solution)/shard_map/ppermute | solution.py:34
  (104 shorter events, 66.6 us)
Async XLA Ops:
  10.1 85.6 %collective-permute-start.23 = (bf16[480,3584]{1,0:T(8,128)(2,1)}, bf16[480,3584]{1,0:T(8,128)(2,1)}, u32[]{:S(2)}, u32[]{:S(2)}) collective-permute-start(bf16[480,3584]{1,0:T(8,128)(2,1)} %shard_map.114), channel_id=1, source_target_pairs={{0,6},{6,0},{2,4},{4,2},{1,7},{7,1},{3,5},{5,3},{8,14},{14,8},{10,... | collective-permute-start | bytes 10321928 | tf_op jit(solution)/shard_map/ppermute | solution.py:418
  20.7 9.7 %collective-permute-start.4 = (bf16[512,256]{1,0:T(8,128)(2,1)S(1)}, bf16[512,256]{1,0:T(8,128)(2,1)S(1)}, u32[]{:S(2)}, u32[]{:S(2)}) collective-permute-start(bf16[512,256]{1,0:T(8,128)(2,1)S(1)} %constant_dynamic-update-slice_fusion.2.refs_0_), channel_id=1, source_target_pairs={{8,0},{16,8},{24,16},{32,24},{40,32},{48,40},{56,48},{0,56},{9,1},... | collective-permute-start | bytes 786440 | tf_op jit(solution)/shard_map/ppermute | solution.py:34
  34.1 8.1 %collective-permute-start.7 = (bf16[512,256]{1,0:T(8,128)(2,1)S(1)}, bf16[512,256]{1,0:T(8,128)(2,1)S(1)}, u32[]{:S(2)}, u32[]{:S(2)}) collective-permute-start(bf16[512,256]{1,0:T(8,128)(2,1)S(1)} %collective-permute-done.5.refs_2_), channel_id=1, source_target_pairs={{56,0},{0,8},{8,16},{16,24},{24,32},{32,40},{40,48},{48,56},{57,1}... | collective-permute-start | bytes 786440 | tf_op jit(solution)/shard_map/ppermute | solution.py:34
  38.3 8.4 %collective-permute-start.8 = (bf16[512,256]{1,0:T(8,128)(2,1)S(1)}, bf16[512,256]{1,0:T(8,128)(2,1)S(1)}, u32[]{:S(2)}, u32[]{:S(2)}) collective-permute-start(bf16[512,256]{1,0:T(8,128)(2,1)S(1)} %collective-permute-done.6.refs_3_), channel_id=1, source_target_pairs={{8,0},{16,8},{24,16},{32,24},{40,32},{48,40},{56,48},{0,56},{9,1},... | collective-permute-start | bytes 786440 | tf_op jit(solution)/shard_map/ppermute | solution.py:34
  42.2 8.7 %collective-permute-start.9 = (bf16[512,256]{1,0:T(8,128)(2,1)S(1)}, bf16[512,256]{1,0:T(8,128)(2,1)S(1)}, u32[]{:S(2)}, u32[]{:S(2)}) collective-permute-start(bf16[512,256]{1,0:T(8,128)(2,1)S(1)} %collective-permute-done.7.refs_4_), channel_id=1, source_target_pairs={{56,0},{0,8},{8,16},{16,24},{24,32},{32,40},{40,48},{48,56},{57,1}... | collective-permute-start | bytes 786440 | tf_op jit(solution)/shard_map/ppermute | solution.py:34
  46.7 8.3 %collective-permute-start.10 = (bf16[256,256]{1,0:T(8,128)(2,1)S(1)}, bf16[256,256]{1,0:T(8,128)(2,1)S(1)}, u32[]{:S(2)}, u32[]{:S(2)}) collective-permute-start(bf16[256,256]{1,0:T(8,128)(2,1)S(1)} %slice.16), channel_id=1, source_target_pairs={{8,0},{16,8},{24,16},{32,24},{40,32},{48,40},{56,48},{0,56},{9,1},... | collective-permute-start | bytes 393224 | tf_op jit(solution)/shard_map/ppermute | solution.py:34
  81.1 12.5 %collective-permute-start.17 = (bf16[64,3584]{1,0:T(8,128)(2,1)S(1)}, bf16[64,3584]{1,0:T(8,128)(2,1)S(1)}, u32[]{:S(2)}, u32[]{:S(2)}) collective-permute-start(bf16[64,3584]{1,0:T(8,128)(2,1)S(1)} %shard_map.113.refs_0_), channel_id=1, source_target_pairs={{8,0},{16,8},{24,16},{32,24},{40,32},{48,40},{56,48},{0,56},{9,1},... | collective-permute-start | bytes 1376264 | tf_op jit(solution)/shard_map/ppermute | solution.py:34
  82.3 13.4 %collective-permute-start.18 = (bf16[64,3584]{1,0:T(8,128)(2,1)S(1)}, bf16[64,3584]{1,0:T(8,128)(2,1)S(1)}, u32[]{:S(2)}, u32[]{:S(2)}) collective-permute-start(bf16[64,3584]{1,0:T(8,128)(2,1)S(1)} %shard_map.113.refs_0_), channel_id=1, source_target_pairs={{56,0},{0,8},{8,16},{16,24},{24,32},{32,40},{40,48},{48,56},{57,1}... | collective-permute-start | bytes 1376264 | tf_op jit(solution)/shard_map/ppermute | solution.py:34
  95.7 15.0 %collective-permute-start.24 = (bf16[480,3584]{1,0:T(8,128)(2,1)}, bf16[480,3584]{1,0:T(8,128)(2,1)S(1)}, u32[]{:S(2)}, u32[]{:S(2)}) collective-permute-start(bf16[480,3584]{1,0:T(8,128)(2,1)} %collective-permute-done.23.a_any), channel_id=1, source_target_pairs={{1,0},{0,1},{3,2},{2,3},{5,4},{4,5},{7,6},{6,7},{9,8},{8,9},{11,10... | collective-permute-start | bytes 10321928 | tf_op jit(solution)/shard_map/ppermute | solution.py:34
  95.7 12.9 %collective-permute-start.19 = (bf16[64,3584]{1,0:T(8,128)(2,1)S(1)}, bf16[64,3584]{1,0:T(8,128)(2,1)S(1)}, u32[]{:S(2)}, u32[]{:S(2)}) collective-permute-start(bf16[64,3584]{1,0:T(8,128)(2,1)S(1)} %collective-permute-done.17.refs_1_), channel_id=1, source_target_pairs={{8,0},{16,8},{24,16},{32,24},{40,32},{48,40},{56,48},{0,56},{9,1},... | collective-permute-start | bytes 1376264 | tf_op jit(solution)/shard_map/ppermute | solution.py:34
  96.1 14.1 %collective-permute-start.21 = (bf16[64,3584]{1,0:T(8,128)(2,1)S(1)}, bf16[64,3584]{1,0:T(8,128)(2,1)S(1)}, u32[]{:S(2)}, u32[]{:S(2)}) collective-permute-start(bf16[64,3584]{1,0:T(8,128)(2,1)S(1)} %collective-permute-done.18.refs_2_), channel_id=1, source_target_pairs={{56,0},{0,8},{8,16},{16,24},{24,32},{32,40},{40,48},{48,56},{57,1}... | collective-permute-start | bytes 1376264 | tf_op jit(solution)/shard_map/ppermute | solution.py:34
  108.6 12.2 %collective-permute-start.20 = (bf16[64,3584]{1,0:T(8,128)(2,1)S(1)}, bf16[64,3584]{1,0:T(8,128)(2,1)S(1)}, u32[]{:S(2)}, u32[]{:S(2)}) collective-permute-start(bf16[64,3584]{1,0:T(8,128)(2,1)S(1)} %collective-permute-done.19.refs_0_), channel_id=1, source_target_pairs={{8,0},{16,8},{24,16},{32,24},{40,32},{48,40},{56,48},{0,56},{9,1},... | collective-permute-start | bytes 1376264 | tf_op jit(solution)/shard_map/ppermute | solution.py:34
  110.1 13.0 %collective-permute-start.22 = (bf16[64,3584]{1,0:T(8,128)(2,1)S(1)}, bf16[64,3584]{1,0:T(8,128)(2,1)S(1)}, u32[]{:S(2)}, u32[]{:S(2)}) collective-permute-start(bf16[64,3584]{1,0:T(8,128)(2,1)S(1)} %collective-permute-done.21.refs_1_), channel_id=1, source_target_pairs={{56,0},{0,8},{8,16},{16,24},{24,32},{32,40},{40,48},{48,56},{57,1}... | collective-permute-start | bytes 1376264 | tf_op jit(solution)/shard_map/ppermute | solution.py:34
  123.2 11.7 %collective-permute-start.25 = (bf16[32,3584]{1,0:T(8,128)(2,1)S(1)}, bf16[32,3584]{1,0:T(8,128)(2,1)S(1)}, u32[]{:S(2)}, u32[]{:S(2)}) collective-permute-start(bf16[32,3584]{1,0:T(8,128)(2,1)S(1)} %slice.14), channel_id=1, source_target_pairs={{8,0},{16,8},{24,16},{32,24},{40,32},{48,40},{56,48},{0,56},{9,1},... | collective-permute-start | bytes 688136 | tf_op jit(solution)/shard_map/ppermute | solution.py:34
  123.5 11.3 %collective-permute-start.26 = (bf16[32,3584]{1,0:T(8,128)(2,1)S(1)}, bf16[32,3584]{1,0:T(8,128)(2,1)S(1)}, u32[]{:S(2)}, u32[]{:S(2)}) collective-permute-start(bf16[32,3584]{1,0:T(8,128)(2,1)S(1)} %slice.15), channel_id=1, source_target_pairs={{56,0},{0,8},{8,16},{16,24},{24,32},{32,40},{40,48},{48,56},{57,1}... | collective-permute-start | bytes 688136 | tf_op jit(solution)/shard_map/ppermute | solution.py:34
  131.5 8.5 %collective-permute-start.27 = (bf16[32,3584]{1,0:T(8,128)(2,1)S(1)}, bf16[32,3584]{1,0:T(8,128)(2,1)S(1)}, u32[]{:S(2)}, u32[]{:S(2)}) collective-permute-start(bf16[32,3584]{1,0:T(8,128)(2,1)S(1)} %get-tuple-element.78), channel_id=1, source_target_pairs={{56,0},{0,8},{8,16},{16,24},{24,32},{32,40},{40,48},{48,56},{57,1}... | collective-permute-start | bytes 688136 | tf_op jit(solution)/shard_map/ppermute | solution.py:34
  131.6 8.4 %collective-permute-start.28 = (bf16[32,3584]{1,0:T(8,128)(2,1)S(1)}, bf16[32,3584]{1,0:T(8,128)(2,1)S(1)}, u32[]{:S(2)}, u32[]{:S(2)}) collective-permute-start(bf16[32,3584]{1,0:T(8,128)(2,1)S(1)} %get-tuple-element.79), channel_id=1, source_target_pairs={{8,0},{16,8},{24,16},{32,24},{40,32},{48,40},{56,48},{0,56},{9,1},... | collective-permute-start | bytes 688136 | tf_op jit(solution)/shard_map/ppermute | solution.py:34
  142.1 8.0 %collective-permute-start.29 = (bf16[32,3584]{1,0:T(8,128)(2,1)S(1)}, bf16[32,3584]{1,0:T(8,128)(2,1)S(1)}, u32[]{:S(2)}, u32[]{:S(2)}) collective-permute-start(bf16[32,3584]{1,0:T(8,128)(2,1)S(1)} %get-tuple-element.80), channel_id=1, source_target_pairs={{56,0},{0,8},{8,16},{16,24},{24,32},{32,40},{40,48},{48,56},{57,1}... | collective-permute-start | bytes 688136 | tf_op jit(solution)/shard_map/ppermute | solution.py:34
  147.2 8.3 %collective-permute-start.34 = (bf16[32,3584]{1,0:T(8,128)(2,1)S(1)}, bf16[32,3584]{1,0:T(8,128)(2,1)S(1)}, u32[]{:S(2)}, u32[]{:S(2)}) collective-permute-start(bf16[32,3584]{1,0:T(8,128)(2,1)S(1)} %shard_map.122), channel_id=1, source_target_pairs={{8,0},{16,8},{24,16},{32,24},{40,32},{48,40},{56,48},{0,56},{9,1},... | collective-permute-start | bytes 688136 | tf_op jit(solution)/shard_map/ppermute | solution.py:34
  150.2 9.3 %collective-permute-start.30 = (bf16[32,3584]{1,0:T(8,128)(2,1)S(1)}, bf16[32,3584]{1,0:T(8,128)(2,1)S(1)}, u32[]{:S(2)}, u32[]{:S(2)}) collective-permute-start(bf16[32,3584]{1,0:T(8,128)(2,1)S(1)} %shard_map.119), channel_id=1, source_target_pairs={{56,0},{0,8},{8,16},{16,24},{24,32},{32,40},{40,48},{48,56},{57,1}... | collective-permute-start | bytes 688136 | tf_op jit(solution)/shard_map/ppermute | solution.py:34
  155.6 12.7 %collective-permute-start.35 = (bf16[64,3584]{1,0:T(8,128)(2,1)S(1)}, bf16[64,3584]{1,0:T(8,128)(2,1)S(1)}, u32[]{:S(2)}, u32[]{:S(2)}) collective-permute-start(bf16[64,3584]{1,0:T(8,128)(2,1)S(1)} %shard_map.123), channel_id=1, source_target_pairs={{8,0},{16,8},{24,16},{32,24},{40,32},{48,40},{56,48},{0,56},{9,1},... | collective-permute-start | bytes 1376264 | tf_op jit(solution)/shard_map/ppermute | solution.py:34
  159.6 12.8 %collective-permute-start.31 = (bf16[64,3584]{1,0:T(8,128)(2,1)S(1)}, bf16[64,3584]{1,0:T(8,128)(2,1)S(1)}, u32[]{:S(2)}, u32[]{:S(2)}) collective-permute-start(bf16[64,3584]{1,0:T(8,128)(2,1)S(1)} %shard_map.120), channel_id=1, source_target_pairs={{56,0},{0,8},{8,16},{16,24},{24,32},{32,40},{40,48},{48,56},{57,1}... | collective-permute-start | bytes 1376264 | tf_op jit(solution)/shard_map/ppermute | solution.py:34
  168.3 9.8 %collective-permute-start.36 = (bf16[64,3584]{1,0:T(8,128)(2,1)S(1)}, bf16[64,3584]{1,0:T(8,128)(2,1)S(1)}, u32[]{:S(2)}, u32[]{:S(2)}) collective-permute-start(bf16[64,3584]{1,0:T(8,128)(2,1)S(1)} %shard_map.124), channel_id=1, source_target_pairs={{8,0},{16,8},{24,16},{32,24},{40,32},{48,40},{56,48},{0,56},{9,1},... | collective-permute-start | bytes 1376264 | tf_op jit(solution)/shard_map/ppermute | solution.py:34
  172.5 9.8 %collective-permute-start.32 = (bf16[64,3584]{1,0:T(8,128)(2,1)S(1)}, bf16[64,3584]{1,0:T(8,128)(2,1)S(1)}, u32[]{:S(2)}, u32[]{:S(2)}) collective-permute-start(bf16[64,3584]{1,0:T(8,128)(2,1)S(1)} %shard_map.121), channel_id=1, source_target_pairs={{56,0},{0,8},{8,16},{16,24},{24,32},{32,40},{40,48},{48,56},{57,1}... | collective-permute-start | bytes 1376264 | tf_op jit(solution)/shard_map/ppermute | solution.py:34
  (24 other events, 386.1 us)

commit v5 on v3

--- a/solution.py
+++ b/solution.py
@@ -100,7 +100,7 @@
     return [near[0], up, down]
 
 
-def attend(at_ref, table_ref, q_all, kv_ref, kp_ref, steps, carry):
+def attend(at_ref, table_ref, q_all, kv_ref, kp_ref, steps, carry, unroll):
     y, z, xh, t = (at_ref[i] for i in range(4))
     count = kv_ref.shape[1]
     tokens = count // 8
@@ -144,7 +144,7 @@
         acc = acc * keep + jnp.dot(weight.astype(bf16), v, preferred_element_type=f32)
         return new_top, total, acc
 
-    return lax.fori_loop(0, len(steps), step, carry)
+    return lax.fori_loop(0, len(steps), step, carry, unroll=unroll)
 
 
 def attention_kernel(steps, at_ref, table_ref, q_ref, *refs):
@@ -171,7 +171,7 @@
     )
     for one in copies:
         one.wait()
-    top, total, acc = attend(at_ref, table_ref, q_all, kv_ref, kp_ref, steps, carry)
+    top, total, acc = attend(at_ref, table_ref, q_all, kv_ref, kp_ref, steps, carry, False)
     top_ref[...] = jnp.broadcast_to(top, top_ref.shape)
     total_ref[...] = jnp.broadcast_to(total, total_ref.shape)
     acc_ref[...] = acc
@@ -191,17 +191,15 @@
     carry = top_ref[:, :1], total_ref[:, :1], acc_ref[...]
     for one in copies:
         one.wait()
-    top, total, acc = attend(at_ref, table_ref, q_all, kv_ref, kp_ref, steps, carry)
+    top, total, acc = attend(at_ref, table_ref, q_all, kv_ref, kp_ref, steps, carry, False)
     tokens = kv_ref.shape[1] // 8
     half = tokens // 2
     summed = (acc / total).astype(bf16)
     heads = jnp.concatenate([summed[g * tokens : (g + 1) * tokens] for g in range(GROUP)], axis=1)
     copy.wait()
     width = 512
-
-    @pl.loop(0, w_ref.shape[1] // width)
-    def _(n):
-        cols = pl.ds(pl.multiple_of(n * width, width), width)
+    for n in range(w_ref.shape[1] // width):
+        cols = slice(n * width, (n + 1) * width)
         part = jnp.dot(heads, w_ref[:, cols], preferred_element_type=f32).astype(bf16)
         keep_ref[:, cols] = part[:half]
         send_ref[:, cols] = part[half:]
@@ -271,7 +269,19 @@
         copy.wait()
 
 
-def expert_kernel(count, *refs):
+def aligned(i, step):
+    return i * step if isinstance(i, int) else pl.multiple_of(i * step, step)
+
+
+def repeat(count, unroll, body):
+    if unroll:
+        for i in range(count):
+            body(i)
+    else:
+        pl.loop(0, count)(body)
+
+
+def expert_kernel(count, unroll, *refs):
     xs, w_ref, d_ref, outs = refs[:count], refs[count], refs[count + 1], refs[count + 2 : -2]
     x_ref, h_ref = refs[-2:]
     at = 0
@@ -280,28 +290,29 @@
         at += x.shape[0]
     block = 128
 
-    @pl.loop(0, w_ref.shape[0] // (2 * block))
-    def _(b):
+    def gate_and_up(b):
         both = lax.dot_general(
             x_ref[...],
-            w_ref[pl.ds(pl.multiple_of(b * 2 * block, 2 * block), 2 * block), :],
+            w_ref[pl.ds(aligned(b, 2 * block), 2 * block), :],
             (((1,), (1,)), ((), ())),
             preferred_element_type=f32,
         )
         gate, up = both[:, :block], both[:, block:]
         value = (gate / (1.0 + jnp.exp(-gate)) * up).astype(bf16)
-        h_ref[:, pl.ds(pl.multiple_of(b * block, block), block)] = value
-
-    width = 512
-
-    @pl.loop(0, d_ref.shape[1] // width)
-    def _(c):
-        cols = pl.ds(pl.multiple_of(c * width, width), width)
+        h_ref[:, pl.ds(aligned(b, block), block)] = value
+
+    repeat(w_ref.shape[0] // (2 * block), unroll, gate_and_up)
+    width = 256 if unroll else 512
+
+    def down(c):
+        cols = pl.ds(aligned(c, width), width)
         part = jnp.dot(h_ref[...], d_ref[:, cols], preferred_element_type=f32).astype(bf16)
         at = 0
         for out in outs:
             out[:, cols] = part[at : at + out.shape[0]]
             at += out.shape[0]
+
+    repeat(d_ref.shape[1] // width, unroll, down)
 
 
 def join_kernel(*refs):
@@ -325,12 +336,12 @@
     )(*xs)
 
 
-def expert(xs, weights):
+def expert(xs, weights, unroll):
     w, d = weights
     rows, width = sum(x.shape[0] for x in xs), xs[0].shape[1]
     units = d.shape[0]
     return pl.pallas_call(
-        functools.partial(expert_kernel, len(xs)),
+        functools.partial(expert_kernel, len(xs), unroll),
         out_shape=[jax.ShapeDtypeStruct(x.shape, bf16) for x in xs],
         in_specs=[VMEM] * (len(xs) + 2),
         out_specs=[VMEM] * len(xs),
@@ -481,11 +492,11 @@
     ahead_3, behind_3, weights = lax.optimization_barrier((ahead[3], behind[3], weights))
     far = gather_far(ahead_3, behind_3, "z")
     after_2, before_2, after_3, before_3 = expert(
-        [ahead[2], behind[2], ahead[3], behind[3]], weights
+        [ahead[2], behind[2], ahead[3], behind[3]], weights, False
     )
     weights, after_3 = lax.optimization_barrier((weights, after_3))
-    far_parts = expert(far, weights)
-    own, after, before = expert([ahead[0], ahead[1], behind[1]], weights)
+    far_parts = expert(far, weights, True)
+    own, after, before = expert([ahead[0], ahead[1], behind[1]], weights, False)
     near_parts = [own, after, after_2, after_3, None, before_3, before_2, before]
     by_y = add(scatter_ring(near_parts, far_parts, "z"), pieces=4)
     terms = scatter_direct(by_y, "y")

time: 187 us -> 186 us (level)
  no operation moved by 1% of the time
where the time goes in v5:
time: 186 us; the launch traced here: 185 us
  waiting for transfers between devices  94.3 us (51%)
  starting transfers between devices  52.3 us (28%)
  Pallas kernels  36.5 us (20%)
    ppermute x37, waiting for transfers between devices, fetch(): return lax.ppermute(x, axis, [((i + k) % n, i) for i in range(n)])  94.3 us
    ppermute x37, starting transfers between devices, fetch(): return lax.ppermute(x, axis, [((i + k) % n, i) for i in range(n)])  51.2 us
    pallas_call x3, Pallas kernels, expert(): pl.pallas_call(functools.partial(expert_kernel, len(xs), unroll), out_sha...  16.8 us
    pallas_call x1, Pallas kernels, per_device(): pl.pallas_call(functools.partial(project_kernel, steps), out_shape=[jax.S...  5.78 us
    pallas_call x1, Pallas kernels, per_device(): pl.pallas_call(assemble_kernel, out_shape=[jax.ShapeDtypeStruct((4 * hidd...  4.42 us
    pallas_call x1, Pallas kernels, per_device(): pl.pallas_call(functools.partial(attention_kernel, steps), out_shape=[jax...  3.89 us
  transfers between devices with their start and end apart: 38, of which 28 were waited for; matrix products, arithmetic and copies ran while one was open for 0% of the time, Pallas kernels for 15%

profile of v5, /device:TPU:0, one launch (start us, length us, event | category | flops | bytes accessed | tf_op | source)
XLA Modules:
  0.0 185.0 jit_solution(8823638409264533449)
XLA Ops:
  2.8 4.1 %collective-permute-done = bf16[64,256]{1,0:T(8,128)(2,1)S(1)} collective-permute-done((bf16[64,256]{1,0:T(8,128)(2,1)S(1)}, bf16[64,256]{1,0:T(8,128)(2,1)S(1)}, u32[]{:S(2)}, u32[]{:S(2)}) %collective-permute-start) | collective-permute-done | bytes 32800 | tf_op jit(solution)/shard_map/ppermute | solution.py:34
  16.1 3.9 %collective-permute-done.2 = bf16[128,256]{1,0:T(8,128)(2,1)S(1)} collective-permute-done((bf16[128,256]{1,0:T(8,128)(2,1)S(1)}, bf16[128,256]{1,0:T(8,128)(2,1)S(1)}, u32[]{:S(2)}, u32[]{:S(2)}) %collective-permute-start.2) | collective-permute-done | bytes 65568 | tf_op jit(solution)/shard_map/ppermute | solution.py:34
  20.7 5.9 %collective-permute-start.4 = (bf16[512,256]{1,0:T(8,128)(2,1)S(1)}, bf16[512,256]{1,0:T(8,128)(2,1)S(1)}, u32[]{:S(2)}, u32[]{:S(2)}) collective-permute-start(bf16[512,256]{1,0:T(8,128)(2,1)S(1)} %constant_dynamic-update-slice_fusion.2.refs_0_), channel_id=1, source_target_pairs={{8,0},{16,8},{24,16},{32,24},{40,32},{48,40},{56,48},{0,56},{9,1},... | collective-permute-start | bytes 786440 | tf_op jit(solution)/shard_map/ppermute | solution.py:34
  26.5 3.9 %collective-permute-done.4.refs_1_ = bf16[512,256]{1,0:T(8,128)(2,1)S(1)} collective-permute-done((bf16[512,256]{1,0:T(8,128)(2,1)S(1)}, bf16[512,256]{1,0:T(8,128)(2,1)S(1)}, u32[]{:S(2)}, u32[]{:S(2)}) %collective-permute-start.4) | collective-permute-done | bytes 262176 | tf_op jit(solution)/shard_map/ppermute | solution.py:34
  30.4 3.7 %collective-permute-start.6 = (bf16[512,256]{1,0:T(8,128)(2,1)S(1)}, bf16[512,256]{1,0:T(8,128)(2,1)S(1)}, u32[]{:S(2)}, u32[]{:S(2)}) collective-permute-start(bf16[512,256]{1,0:T(8,128)(2,1)S(1)} %collective-permute-done.4.refs_1_), channel_id=1, source_target_pairs={{8,0},{16,8},{24,16},{32,24},{40,32},{48,40},{56,48},{0,56},{9,1},... | collective-permute-start | bytes 786440 | tf_op jit(solution)/shard_map/ppermute | solution.py:34
  34.1 4.1 %collective-permute-done.6.refs_3_ = bf16[512,256]{1,0:T(8,128)(2,1)S(1)} collective-permute-done((bf16[512,256]{1,0:T(8,128)(2,1)S(1)}, bf16[512,256]{1,0:T(8,128)(2,1)S(1)}, u32[]{:S(2)}, u32[]{:S(2)}) %collective-permute-start.6) | collective-permute-done | bytes 262176 | tf_op jit(solution)/shard_map/ppermute | solution.py:34
  38.3 3.7 %collective-permute-start.8 = (bf16[512,256]{1,0:T(8,128)(2,1)S(1)}, bf16[512,256]{1,0:T(8,128)(2,1)S(1)}, u32[]{:S(2)}, u32[]{:S(2)}) collective-permute-start(bf16[512,256]{1,0:T(8,128)(2,1)S(1)} %collective-permute-done.6.refs_3_), channel_id=1, source_target_pairs={{8,0},{16,8},{24,16},{32,24},{40,32},{48,40},{56,48},{0,56},{9,1},... | collective-permute-start | bytes 786440 | tf_op jit(solution)/shard_map/ppermute | solution.py:34
  42.2 4.4 %collective-permute-done.8.refs_0_ = bf16[512,256]{1,0:T(8,128)(2,1)S(1)} collective-permute-done((bf16[512,256]{1,0:T(8,128)(2,1)S(1)}, bf16[512,256]{1,0:T(8,128)(2,1)S(1)}, u32[]{:S(2)}, u32[]{:S(2)}) %collective-permute-start.8) | collective-permute-done | bytes 262176 | tf_op jit(solution)/shard_map/ppermute | solution.py:34
  46.7 3.8 %collective-permute-start.10 = (bf16[256,256]{1,0:T(8,128)(2,1)S(1)}, bf16[256,256]{1,0:T(8,128)(2,1)S(1)}, u32[]{:S(2)}, u32[]{:S(2)}) collective-permute-start(bf16[256,256]{1,0:T(8,128)(2,1)S(1)} %slice.16), channel_id=1, source_target_pairs={{8,0},{16,8},{24,16},{32,24},{40,32},{48,40},{56,48},{0,56},{9,1},... | collective-permute-start | bytes 393224 | tf_op jit(solution)/shard_map/ppermute | solution.py:34
  51.1 3.9 %shard_map.109 = (bf16[448,128]{1,0:T(8,128)(2,1)S(1)}, f32[448,128]{1,0:T(8,128)S(1)}, f32[448,128]{1,0:T(8,128)S(1)}, f32[448,128]{1,0:T(8,128)S(1)}) custom-call(s32[4]{0:T(128)S(1)} %pad_add_fusion.at_ref, s32[64]{0:T(128)S(1)} %copy-done.4, bf16[64,896]{1,0:T(8,128)(2,1)S(1)} %copy-done.5, ...), custom_call_target="tpu_custom_call" | custom-call | flops 587202560 | bytes 1310720 | tf_op jit(solution)/shard_map/pallas_call | solution.py:418
  57.2 5.8 %shard_map.110 = (bf16[32,3584]{1,0:T(8,128)(2,1)S(1)}, bf16[32,3584]{1,0:T(8,128)(2,1)S(1)}) custom-call(s32[4]{0:T(128)S(1)} %pad_add_fusion.at_ref, s32[64]{0:T(128)S(1)} %copy-done.4, bf16[448,128]{1,0:T(8,128)(2,1)S(1)} %get-tuple-element.39.q_all, f32[448,128]{1,0:T(8,128)S(1)} %get-tuple-element.40.top_ref, ...), custom_call_target="tpu_custom_call" | custom-call | flops 763363328 | bytes 7208960 | tf_op jit(solution)/shard_map/pallas_call | solution.py:437
  74.0 3.5 %collective-permute-done.14.refs_1_ = bf16[16,3584]{1,0:T(8,128)(2,1)S(1)} collective-permute-done((bf16[16,3584]{1,0:T(8,128)(2,1)S(1)}, bf16[16,3584]{1,0:T(8,128)(2,1)S(1)}, u32[]{:S(2)}, u32[]{:S(2)}) %collective-permute-start.14) | collective-permute-done | bytes 114720 | tf_op jit(solution)/shard_map/ppermute | solution.py:34
  82.5 10.4 %collective-permute-done.17.refs_1_ = bf16[64,3584]{1,0:T(8,128)(2,1)S(1)} collective-permute-done((bf16[64,3584]{1,0:T(8,128)(2,1)S(1)}, bf16[64,3584]{1,0:T(8,128)(2,1)S(1)}, u32[]{:S(2)}, u32[]{:S(2)}) %collective-permute-start.17) | collective-permute-done | bytes 458784 | tf_op jit(solution)/shard_map/ppermute | solution.py:34
  97.0 10.9 %collective-permute-done.19.refs_0_ = bf16[64,3584]{1,0:T(8,128)(2,1)S(1)} collective-permute-done((bf16[64,3584]{1,0:T(8,128)(2,1)S(1)}, bf16[64,3584]{1,0:T(8,128)(2,1)S(1)}, u32[]{:S(2)}, u32[]{:S(2)}) %collective-permute-start.19) | collective-permute-done | bytes 458784 | tf_op jit(solution)/shard_map/ppermute | solution.py:34
  109.9 4.4 %shard_map.115 = (bf16[1280,3584]{1,0:T(8,128)(2,1)S(1)}, bf16[640,3584]{1,0:T(8,128)(2,1)S(1)}) custom-call(bf16[320,3584]{1,0:T(8,128)(2,1)S(1)} %bitcast.8, bf16[320,3584]{1,0:T(8,128)(2,1)S(1)} %bitcast.10, bf16[320,3584]{1,0:T(8,128)(2,1)S(1)} %copy-done.2, bf16[480,3584]{1,0:T(8,128)(2,1)} %collective-permute-done.23.a_any, ...), custom_call_target="tpu_custom_call" | custom-call | bytes 13762560 | tf_op jit(solution)/shard_map/pallas_call | solution.py:478
  114.4 5.7 %collective-permute-done.20.refs_2_ = bf16[64,3584]{1,0:T(8,128)(2,1)S(1)} collective-permute-done((bf16[64,3584]{1,0:T(8,128)(2,1)S(1)}, bf16[64,3584]{1,0:T(8,128)(2,1)S(1)}, u32[]{:S(2)}, u32[]{:S(2)}) %collective-permute-start.20) | collective-permute-done | bytes 458784 | tf_op jit(solution)/shard_map/ppermute | solution.py:34
  124.8 6.2 %shard_map.116 = (bf16[64,3584]{1,0:T(8,128)(2,1)S(1)}, bf16[64,3584]{1,0:T(8,128)(2,1)S(1)}, bf16[64,3584]{1,0:T(8,128)(2,1)S(1)}, bf16[64,3584]{1,0:T(8,128)(2,1)S(1)}) custom-call(bf16[64,3584]{1,0:T(8,128)(2,1)S(1)} %collective-permute-done.19.refs_0_, bf16[64,3584]{1,0:T(8,128)(2,1)S(1)} %collective-permute-done.21.refs_1_, ...), custom_call_target="tpu_custom_call" | custom-call | flops 3523215360 | bytes 17432576 | tf_op jit(solution)/shard_map/pallas_call | solution.py:343
  131.0 4.5 %shard_map.118 = (bf16[32,3584]{1,0:T(8,128)(2,1)S(1)}, bf16[32,3584]{1,0:T(8,128)(2,1)S(1)}) custom-call(bf16[32,3584]{1,0:T(8,128)(2,1)S(1)} %collective-permute-done.25.refs_0_, bf16[32,3584]{1,0:T(8,128)(2,1)S(1)} %collective-permute-done.26.refs_1_, bf16[1280,3584]{1,0:T(8,128)(2,1)S(1)} %get-tuple-element.56.refs_4_.refs_3_.refs_2_, ...), custom_call_target="tpu_custom_call" | custom-call | flops 880803840 | bytes 14680064 | tf_op jit(solution)/shard_map/pallas_call | solution.py:343
  137.7 4.4 %collective-permute-done.31.refs_1_ = bf16[32,3584]{1,0:T(8,128)(2,1)S(1)} collective-permute-done((bf16[32,3584]{1,0:T(8,128)(2,1)S(1)}, bf16[32,3584]{1,0:T(8,128)(2,1)S(1)}, u32[]{:S(2)}, u32[]{:S(2)}) %collective-permute-start.31) | collective-permute-done | bytes 229408 | tf_op jit(solution)/shard_map/ppermute | solution.py:34
  144.7 7.8 %collective-permute-done.32.refs_1_ = bf16[64,3584]{1,0:T(8,128)(2,1)S(1)} collective-permute-done((bf16[64,3584]{1,0:T(8,128)(2,1)S(1)}, bf16[64,3584]{1,0:T(8,128)(2,1)S(1)}, u32[]{:S(2)}, u32[]{:S(2)}) %collective-permute-start.32) | collective-permute-done | bytes 458784 | tf_op jit(solution)/shard_map/ppermute | solution.py:34
  155.6 6.2 %shard_map.117 = (bf16[64,3584]{1,0:T(8,128)(2,1)S(1)}, bf16[64,3584]{1,0:T(8,128)(2,1)S(1)}, bf16[64,3584]{1,0:T(8,128)(2,1)S(1)}) custom-call(bf16[64,3584]{1,0:T(8,128)(2,1)S(1)} %shard_map.113.refs_0_, bf16[64,3584]{1,0:T(8,128)(2,1)S(1)} %collective-permute-done.17.refs_1_, bf16[64,3584]{1,0:T(8,128)(2,1)S(1)} %collective-permute-done.18.refs_2_, ...), custom_call_target="tpu_custom_call" | custom-call | flops 2642411520 | bytes 16515072 | tf_op jit(solution)/shard_map/pallas_call | solution.py:343
  166.2 5.6 %collective-permute-done.34.refs_2_ = bf16[64,3584]{1,0:T(8,128)(2,1)S(1)} collective-permute-done((bf16[64,3584]{1,0:T(8,128)(2,1)S(1)}, bf16[64,3584]{1,0:T(8,128)(2,1)S(1)}, u32[]{:S(2)}, u32[]{:S(2)}) %collective-permute-start.34) | collective-permute-done | bytes 458784 | tf_op jit(solution)/shard_map/ppermute | solution.py:34
  171.8 4.1 %collective-permute-done.30.refs_1_ = bf16[64,3584]{1,0:T(8,128)(2,1)S(1)} collective-permute-done((bf16[64,3584]{1,0:T(8,128)(2,1)S(1)}, bf16[64,3584]{1,0:T(8,128)(2,1)S(1)}, u32[]{:S(2)}, u32[]{:S(2)}) %collective-permute-start.30) | collective-permute-done | bytes 458784 | tf_op jit(solution)/shard_map/ppermute | solution.py:34
  179.4 4.0 %collective-permute-done.35.refs_1_ = bf16[16,3584]{1,0:T(8,128)(2,1)S(1)} collective-permute-done((bf16[16,3584]{1,0:T(8,128)(2,1)S(1)}, bf16[16,3584]{1,0:T(8,128)(2,1)S(1)}, u32[]{:S(2)}, u32[]{:S(2)}) %collective-permute-start.35) | collective-permute-done | bytes 114720 | tf_op jit(solution)/shard_map/ppermute | solution.py:34
  (100 shorter events, 59.9 us)
Async XLA Ops:
  10.1 84.9 %collective-permute-start.23 = (bf16[480,3584]{1,0:T(8,128)(2,1)}, bf16[480,3584]{1,0:T(8,128)(2,1)}, u32[]{:S(2)}, u32[]{:S(2)}) collective-permute-start(bf16[480,3584]{1,0:T(8,128)(2,1)} %shard_map.114), channel_id=1, source_target_pairs={{0,6},{6,0},{2,4},{4,2},{1,7},{7,1},{3,5},{5,3},{8,14},{14,8},{10,... | collective-permute-start | bytes 10321928 | tf_op jit(solution)/shard_map/ppermute | solution.py:408
  20.7 9.7 %collective-permute-start.4 = (bf16[512,256]{1,0:T(8,128)(2,1)S(1)}, bf16[512,256]{1,0:T(8,128)(2,1)S(1)}, u32[]{:S(2)}, u32[]{:S(2)}) collective-permute-start(bf16[512,256]{1,0:T(8,128)(2,1)S(1)} %constant_dynamic-update-slice_fusion.2.refs_0_), channel_id=1, source_target_pairs={{8,0},{16,8},{24,16},{32,24},{40,32},{48,40},{56,48},{0,56},{9,1},... | collective-permute-start | bytes 786440 | tf_op jit(solution)/shard_map/ppermute | solution.py:34
  26.5 7.6 %collective-permute-start.5 = (bf16[512,256]{1,0:T(8,128)(2,1)S(1)}, bf16[512,256]{1,0:T(8,128)(2,1)S(1)}, u32[]{:S(2)}, u32[]{:S(2)}) collective-permute-start(bf16[512,256]{1,0:T(8,128)(2,1)S(1)} %constant_dynamic-update-slice_fusion.2.refs_0_), channel_id=1, source_target_pairs={{56,0},{0,8},{8,16},{16,24},{24,32},{32,40},{40,48},{48,56},{57,1}... | collective-permute-start | bytes 786440 | tf_op jit(solution)/shard_map/ppermute | solution.py:34
  30.4 7.8 %collective-permute-start.6 = (bf16[512,256]{1,0:T(8,128)(2,1)S(1)}, bf16[512,256]{1,0:T(8,128)(2,1)S(1)}, u32[]{:S(2)}, u32[]{:S(2)}) collective-permute-start(bf16[512,256]{1,0:T(8,128)(2,1)S(1)} %collective-permute-done.4.refs_1_), channel_id=1, source_target_pairs={{8,0},{16,8},{24,16},{32,24},{40,32},{48,40},{56,48},{0,56},{9,1},... | collective-permute-start | bytes 786440 | tf_op jit(solution)/shard_map/ppermute | solution.py:34
  34.1 8.1 %collective-permute-start.7 = (bf16[512,256]{1,0:T(8,128)(2,1)S(1)}, bf16[512,256]{1,0:T(8,128)(2,1)S(1)}, u32[]{:S(2)}, u32[]{:S(2)}) collective-permute-start(bf16[512,256]{1,0:T(8,128)(2,1)S(1)} %collective-permute-done.5.refs_2_), channel_id=1, source_target_pairs={{56,0},{0,8},{8,16},{16,24},{24,32},{32,40},{40,48},{48,56},{57,1}... | collective-permute-start | bytes 786440 | tf_op jit(solution)/shard_map/ppermute | solution.py:34
  38.3 8.4 %collective-permute-start.8 = (bf16[512,256]{1,0:T(8,128)(2,1)S(1)}, bf16[512,256]{1,0:T(8,128)(2,1)S(1)}, u32[]{:S(2)}, u32[]{:S(2)}) collective-permute-start(bf16[512,256]{1,0:T(8,128)(2,1)S(1)} %collective-permute-done.6.refs_3_), channel_id=1, source_target_pairs={{8,0},{16,8},{24,16},{32,24},{40,32},{48,40},{56,48},{0,56},{9,1},... | collective-permute-start | bytes 786440 | tf_op jit(solution)/shard_map/ppermute | solution.py:34
  42.2 8.5 %collective-permute-start.9 = (bf16[512,256]{1,0:T(8,128)(2,1)S(1)}, bf16[512,256]{1,0:T(8,128)(2,1)S(1)}, u32[]{:S(2)}, u32[]{:S(2)}) collective-permute-start(bf16[512,256]{1,0:T(8,128)(2,1)S(1)} %collective-permute-done.7.refs_4_), channel_id=1, source_target_pairs={{56,0},{0,8},{8,16},{16,24},{24,32},{32,40},{40,48},{48,56},{57,1}... | collective-permute-start | bytes 786440 | tf_op jit(solution)/shard_map/ppermute | solution.py:34
  46.7 8.3 %collective-permute-start.10 = (bf16[256,256]{1,0:T(8,128)(2,1)S(1)}, bf16[256,256]{1,0:T(8,128)(2,1)S(1)}, u32[]{:S(2)}, u32[]{:S(2)}) collective-permute-start(bf16[256,256]{1,0:T(8,128)(2,1)S(1)} %slice.16), channel_id=1, source_target_pairs={{8,0},{16,8},{24,16},{32,24},{40,32},{48,40},{56,48},{0,56},{9,1},... | collective-permute-start | bytes 393224 | tf_op jit(solution)/shard_map/ppermute | solution.py:34
  72.7 7.7 %collective-permute-start.16 = (bf16[16,3584]{1,0:T(8,128)(2,1)S(1)}, bf16[16,3584]{1,0:T(8,128)(2,1)S(1)}, u32[]{:S(2)}, u32[]{:S(2)}) collective-permute-start(bf16[16,3584]{1,0:T(8,128)(2,1)S(1)} %get-tuple-element.48.refs_0_), channel_id=1, source_target_pairs={{192,0},{0,64},{64,128},{128,192},{193,1},{1,65},{65,129},{129,193... | collective-permute-start | bytes 344072 | tf_op jit(solution)/shard_map/ppermute | solution.py:34
  80.4 12.5 %collective-permute-start.17 = (bf16[64,3584]{1,0:T(8,128)(2,1)S(1)}, bf16[64,3584]{1,0:T(8,128)(2,1)S(1)}, u32[]{:S(2)}, u32[]{:S(2)}) collective-permute-start(bf16[64,3584]{1,0:T(8,128)(2,1)S(1)} %shard_map.113.refs_0_), channel_id=1, source_target_pairs={{8,0},{16,8},{24,16},{32,24},{40,32},{48,40},{56,48},{0,56},{9,1},... | collective-permute-start | bytes 1376264 | tf_op jit(solution)/shard_map/ppermute | solution.py:34
  81.6 13.4 %collective-permute-start.18 = (bf16[64,3584]{1,0:T(8,128)(2,1)S(1)}, bf16[64,3584]{1,0:T(8,128)(2,1)S(1)}, u32[]{:S(2)}, u32[]{:S(2)}) collective-permute-start(bf16[64,3584]{1,0:T(8,128)(2,1)S(1)} %shard_map.113.refs_0_), channel_id=1, source_target_pairs={{56,0},{0,8},{8,16},{16,24},{24,32},{32,40},{40,48},{48,56},{57,1}... | collective-permute-start | bytes 1376264 | tf_op jit(solution)/shard_map/ppermute | solution.py:34
  95.0 15.0 %collective-permute-start.24 = (bf16[480,3584]{1,0:T(8,128)(2,1)}, bf16[480,3584]{1,0:T(8,128)(2,1)S(1)}, u32[]{:S(2)}, u32[]{:S(2)}) collective-permute-start(bf16[480,3584]{1,0:T(8,128)(2,1)} %collective-permute-done.23.a_any), channel_id=1, source_target_pairs={{1,0},{0,1},{3,2},{2,3},{5,4},{4,5},{7,6},{6,7},{9,8},{8,9},{11,10... | collective-permute-start | bytes 10321928 | tf_op jit(solution)/shard_map/ppermute | solution.py:34
  95.0 12.9 %collective-permute-start.19 = (bf16[64,3584]{1,0:T(8,128)(2,1)S(1)}, bf16[64,3584]{1,0:T(8,128)(2,1)S(1)}, u32[]{:S(2)}, u32[]{:S(2)}) collective-permute-start(bf16[64,3584]{1,0:T(8,128)(2,1)S(1)} %collective-permute-done.17.refs_1_), channel_id=1, source_target_pairs={{8,0},{16,8},{24,16},{32,24},{40,32},{48,40},{56,48},{0,56},{9,1},... | collective-permute-start | bytes 1376264 | tf_op jit(solution)/shard_map/ppermute | solution.py:34
  95.3 14.1 %collective-permute-start.21 = (bf16[64,3584]{1,0:T(8,128)(2,1)S(1)}, bf16[64,3584]{1,0:T(8,128)(2,1)S(1)}, u32[]{:S(2)}, u32[]{:S(2)}) collective-permute-start(bf16[64,3584]{1,0:T(8,128)(2,1)S(1)} %collective-permute-done.18.refs_2_), channel_id=1, source_target_pairs={{56,0},{0,8},{8,16},{16,24},{24,32},{32,40},{40,48},{48,56},{57,1}... | collective-permute-start | bytes 1376264 | tf_op jit(solution)/shard_map/ppermute | solution.py:34
  107.9 12.2 %collective-permute-start.20 = (bf16[64,3584]{1,0:T(8,128)(2,1)S(1)}, bf16[64,3584]{1,0:T(8,128)(2,1)S(1)}, u32[]{:S(2)}, u32[]{:S(2)}) collective-permute-start(bf16[64,3584]{1,0:T(8,128)(2,1)S(1)} %collective-permute-done.19.refs_0_), channel_id=1, source_target_pairs={{8,0},{16,8},{24,16},{32,24},{40,32},{48,40},{56,48},{0,56},{9,1},... | collective-permute-start | bytes 1376264 | tf_op jit(solution)/shard_map/ppermute | solution.py:34
  109.4 13.0 %collective-permute-start.22 = (bf16[64,3584]{1,0:T(8,128)(2,1)S(1)}, bf16[64,3584]{1,0:T(8,128)(2,1)S(1)}, u32[]{:S(2)}, u32[]{:S(2)}) collective-permute-start(bf16[64,3584]{1,0:T(8,128)(2,1)S(1)} %collective-permute-done.21.refs_1_), channel_id=1, source_target_pairs={{56,0},{0,8},{8,16},{16,24},{24,32},{32,40},{40,48},{48,56},{57,1}... | collective-permute-start | bytes 1376264 | tf_op jit(solution)/shard_map/ppermute | solution.py:34
  122.4 8.6 %collective-permute-start.25 = (bf16[32,3584]{1,0:T(8,128)(2,1)S(1)}, bf16[32,3584]{1,0:T(8,128)(2,1)S(1)}, u32[]{:S(2)}, u32[]{:S(2)}) collective-permute-start(bf16[32,3584]{1,0:T(8,128)(2,1)S(1)} %slice.14), channel_id=1, source_target_pairs={{8,0},{16,8},{24,16},{32,24},{40,32},{48,40},{56,48},{0,56},{9,1},... | collective-permute-start | bytes 688136 | tf_op jit(solution)/shard_map/ppermute | solution.py:34
  123.0 8.0 %collective-permute-start.26 = (bf16[32,3584]{1,0:T(8,128)(2,1)S(1)}, bf16[32,3584]{1,0:T(8,128)(2,1)S(1)}, u32[]{:S(2)}, u32[]{:S(2)}) collective-permute-start(bf16[32,3584]{1,0:T(8,128)(2,1)S(1)} %slice.15), channel_id=1, source_target_pairs={{56,0},{0,8},{8,16},{16,24},{24,32},{32,40},{40,48},{48,56},{57,1}... | collective-permute-start | bytes 688136 | tf_op jit(solution)/shard_map/ppermute | solution.py:34
  142.2 10.4 %collective-permute-start.32 = (bf16[64,3584]{1,0:T(8,128)(2,1)S(1)}, bf16[64,3584]{1,0:T(8,128)(2,1)S(1)}, u32[]{:S(2)}, u32[]{:S(2)}) collective-permute-start(bf16[64,3584]{1,0:T(8,128)(2,1)S(1)} %shard_map.122), channel_id=1, source_target_pairs={{8,0},{16,8},{24,16},{32,24},{40,32},{48,40},{56,48},{0,56},{9,1},... | collective-permute-start | bytes 1376264 | tf_op jit(solution)/shard_map/ppermute | solution.py:34
  144.6 10.8 %collective-permute-start.28 = (bf16[64,3584]{1,0:T(8,128)(2,1)S(1)}, bf16[64,3584]{1,0:T(8,128)(2,1)S(1)}, u32[]{:S(2)}, u32[]{:S(2)}) collective-permute-start(bf16[64,3584]{1,0:T(8,128)(2,1)S(1)} %shard_map.119), channel_id=1, source_target_pairs={{56,0},{0,8},{8,16},{16,24},{24,32},{32,40},{40,48},{48,56},{57,1}... | collective-permute-start | bytes 1376264 | tf_op jit(solution)/shard_map/ppermute | solution.py:34
  152.7 9.6 %collective-permute-start.33 = (bf16[64,3584]{1,0:T(8,128)(2,1)S(1)}, bf16[64,3584]{1,0:T(8,128)(2,1)S(1)}, u32[]{:S(2)}, u32[]{:S(2)}) collective-permute-start(bf16[64,3584]{1,0:T(8,128)(2,1)S(1)} %shard_map.123), channel_id=1, source_target_pairs={{8,0},{16,8},{24,16},{32,24},{40,32},{48,40},{56,48},{0,56},{9,1},... | collective-permute-start | bytes 1376264 | tf_op jit(solution)/shard_map/ppermute | solution.py:34
  155.5 10.5 %collective-permute-start.29 = (bf16[64,3584]{1,0:T(8,128)(2,1)S(1)}, bf16[64,3584]{1,0:T(8,128)(2,1)S(1)}, u32[]{:S(2)}, u32[]{:S(2)}) collective-permute-start(bf16[64,3584]{1,0:T(8,128)(2,1)S(1)} %shard_map.120), channel_id=1, source_target_pairs={{56,0},{0,8},{8,16},{16,24},{24,32},{32,40},{40,48},{48,56},{57,1}... | collective-permute-start | bytes 1376264 | tf_op jit(solution)/shard_map/ppermute | solution.py:34
  162.3 9.5 %collective-permute-start.34 = (bf16[64,3584]{1,0:T(8,128)(2,1)S(1)}, bf16[64,3584]{1,0:T(8,128)(2,1)S(1)}, u32[]{:S(2)}, u32[]{:S(2)}) collective-permute-start(bf16[64,3584]{1,0:T(8,128)(2,1)S(1)} %shard_map.124), channel_id=1, source_target_pairs={{8,0},{16,8},{24,16},{32,24},{40,32},{48,40},{56,48},{0,56},{9,1},... | collective-permute-start | bytes 1376264 | tf_op jit(solution)/shard_map/ppermute | solution.py:34
  166.1 9.8 %collective-permute-start.30 = (bf16[64,3584]{1,0:T(8,128)(2,1)S(1)}, bf16[64,3584]{1,0:T(8,128)(2,1)S(1)}, u32[]{:S(2)}, u32[]{:S(2)}) collective-permute-start(bf16[64,3584]{1,0:T(8,128)(2,1)S(1)} %shard_map.121), channel_id=1, source_target_pairs={{56,0},{0,8},{8,16},{16,24},{24,32},{32,40},{40,48},{48,56},{57,1}... | collective-permute-start | bytes 1376264 | tf_op jit(solution)/shard_map/ppermute | solution.py:34
  (22 other events, 365.9 us)

commit v6 on v5

--- a/solution.py
+++ b/solution.py
@@ -302,7 +302,7 @@
         h_ref[:, pl.ds(aligned(b, block), block)] = value
 
     repeat(w_ref.shape[0] // (2 * block), unroll, gate_and_up)
-    width = 256 if unroll else 512
+    width = 256 if unroll else 896
 
     def down(c):
         cols = pl.ds(aligned(c, width), width)

time: 186 us -> 186 us (level)
  no operation moved by 1% of the time
where the time goes in v6:
time: 186 us; the launch traced here: 185 us
  waiting for transfers between devices  95.2 us (51%)
  starting transfers between devices  52.3 us (28%)
  Pallas kernels  35.7 us (19%)
    ppermute x37, waiting for transfers between devices, fetch(): return lax.ppermute(x, axis, [((i + k) % n, i) for i in range(n)])  95.2 us
    ppermute x37, starting transfers between devices, fetch(): return lax.ppermute(x, axis, [((i + k) % n, i) for i in range(n)])  51.2 us
    pallas_call x3, Pallas kernels, expert(): pl.pallas_call(functools.partial(expert_kernel, len(xs), unroll), out_sha...  16 us
    pallas_call x1, Pallas kernels, per_device(): pl.pallas_call(functools.partial(project_kernel, steps), out_shape=[jax.S...  5.78 us
    pallas_call x1, Pallas kernels, per_device(): pl.pallas_call(assemble_kernel, out_shape=[jax.ShapeDtypeStruct((4 * hidd...  4.42 us
    pallas_call x1, Pallas kernels, per_device(): pl.pallas_call(functools.partial(attention_kernel, steps), out_shape=[jax...  3.89 us
  transfers between devices with their start and end apart: 38, of which 28 were waited for; matrix products, arithmetic and copies ran while one was open for 0% of the time, Pallas kernels for 15%

profile of v6, /device:TPU:0, one launch (start us, length us, event | category | flops | bytes accessed | tf_op | source)
XLA Modules:
  0.0 185.1 jit_solution(18394756110168830802)
XLA Ops:
  2.8 4.1 %collective-permute-done = bf16[64,256]{1,0:T(8,128)(2,1)S(1)} collective-permute-done((bf16[64,256]{1,0:T(8,128)(2,1)S(1)}, bf16[64,256]{1,0:T(8,128)(2,1)S(1)}, u32[]{:S(2)}, u32[]{:S(2)}) %collective-permute-start) | collective-permute-done | bytes 32800 | tf_op jit(solution)/shard_map/ppermute | solution.py:34
  16.1 3.9 %collective-permute-done.2 = bf16[128,256]{1,0:T(8,128)(2,1)S(1)} collective-permute-done((bf16[128,256]{1,0:T(8,128)(2,1)S(1)}, bf16[128,256]{1,0:T(8,128)(2,1)S(1)}, u32[]{:S(2)}, u32[]{:S(2)}) %collective-permute-start.2) | collective-permute-done | bytes 65568 | tf_op jit(solution)/shard_map/ppermute | solution.py:34
  20.7 5.9 %collective-permute-start.4 = (bf16[512,256]{1,0:T(8,128)(2,1)S(1)}, bf16[512,256]{1,0:T(8,128)(2,1)S(1)}, u32[]{:S(2)}, u32[]{:S(2)}) collective-permute-start(bf16[512,256]{1,0:T(8,128)(2,1)S(1)} %constant_dynamic-update-slice_fusion.2.refs_0_), channel_id=1, source_target_pairs={{8,0},{16,8},{24,16},{32,24},{40,32},{48,40},{56,48},{0,56},{9,1},... | collective-permute-start | bytes 786440 | tf_op jit(solution)/shard_map/ppermute | solution.py:34
  26.5 3.9 %collective-permute-done.4.refs_1_ = bf16[512,256]{1,0:T(8,128)(2,1)S(1)} collective-permute-done((bf16[512,256]{1,0:T(8,128)(2,1)S(1)}, bf16[512,256]{1,0:T(8,128)(2,1)S(1)}, u32[]{:S(2)}, u32[]{:S(2)}) %collective-permute-start.4) | collective-permute-done | bytes 262176 | tf_op jit(solution)/shard_map/ppermute | solution.py:34
  30.4 3.7 %collective-permute-start.6 = (bf16[512,256]{1,0:T(8,128)(2,1)S(1)}, bf16[512,256]{1,0:T(8,128)(2,1)S(1)}, u32[]{:S(2)}, u32[]{:S(2)}) collective-permute-start(bf16[512,256]{1,0:T(8,128)(2,1)S(1)} %collective-permute-done.4.refs_1_), channel_id=1, source_target_pairs={{8,0},{16,8},{24,16},{32,24},{40,32},{48,40},{56,48},{0,56},{9,1},... | collective-permute-start | bytes 786440 | tf_op jit(solution)/shard_map/ppermute | solution.py:34
  34.1 4.1 %collective-permute-done.6.refs_3_ = bf16[512,256]{1,0:T(8,128)(2,1)S(1)} collective-permute-done((bf16[512,256]{1,0:T(8,128)(2,1)S(1)}, bf16[512,256]{1,0:T(8,128)(2,1)S(1)}, u32[]{:S(2)}, u32[]{:S(2)}) %collective-permute-start.6) | collective-permute-done | bytes 262176 | tf_op jit(solution)/shard_map/ppermute | solution.py:34
  38.3 3.7 %collective-permute-start.8 = (bf16[512,256]{1,0:T(8,128)(2,1)S(1)}, bf16[512,256]{1,0:T(8,128)(2,1)S(1)}, u32[]{:S(2)}, u32[]{:S(2)}) collective-permute-start(bf16[512,256]{1,0:T(8,128)(2,1)S(1)} %collective-permute-done.6.refs_3_), channel_id=1, source_target_pairs={{8,0},{16,8},{24,16},{32,24},{40,32},{48,40},{56,48},{0,56},{9,1},... | collective-permute-start | bytes 786440 | tf_op jit(solution)/shard_map/ppermute | solution.py:34
  42.2 4.4 %collective-permute-done.8.refs_0_ = bf16[512,256]{1,0:T(8,128)(2,1)S(1)} collective-permute-done((bf16[512,256]{1,0:T(8,128)(2,1)S(1)}, bf16[512,256]{1,0:T(8,128)(2,1)S(1)}, u32[]{:S(2)}, u32[]{:S(2)}) %collective-permute-start.8) | collective-permute-done | bytes 262176 | tf_op jit(solution)/shard_map/ppermute | solution.py:34
  46.7 3.8 %collective-permute-start.10 = (bf16[256,256]{1,0:T(8,128)(2,1)S(1)}, bf16[256,256]{1,0:T(8,128)(2,1)S(1)}, u32[]{:S(2)}, u32[]{:S(2)}) collective-permute-start(bf16[256,256]{1,0:T(8,128)(2,1)S(1)} %slice.16), channel_id=1, source_target_pairs={{8,0},{16,8},{24,16},{32,24},{40,32},{48,40},{56,48},{0,56},{9,1},... | collective-permute-start | bytes 393224 | tf_op jit(solution)/shard_map/ppermute | solution.py:34
  51.1 3.9 %shard_map.109 = (bf16[448,128]{1,0:T(8,128)(2,1)S(1)}, f32[448,128]{1,0:T(8,128)S(1)}, f32[448,128]{1,0:T(8,128)S(1)}, f32[448,128]{1,0:T(8,128)S(1)}) custom-call(s32[4]{0:T(128)S(1)} %pad_add_fusion.at_ref, s32[64]{0:T(128)S(1)} %copy-done.4, bf16[64,896]{1,0:T(8,128)(2,1)S(1)} %copy-done.5, ...), custom_call_target="tpu_custom_call" | custom-call | flops 587202560 | bytes 1310720 | tf_op jit(solution)/shard_map/pallas_call | solution.py:418
  57.2 5.8 %shard_map.110 = (bf16[32,3584]{1,0:T(8,128)(2,1)S(1)}, bf16[32,3584]{1,0:T(8,128)(2,1)S(1)}) custom-call(s32[4]{0:T(128)S(1)} %pad_add_fusion.at_ref, s32[64]{0:T(128)S(1)} %copy-done.4, bf16[448,128]{1,0:T(8,128)(2,1)S(1)} %get-tuple-element.39.q_all, f32[448,128]{1,0:T(8,128)S(1)} %get-tuple-element.40.top_ref, ...), custom_call_target="tpu_custom_call" | custom-call | flops 763363328 | bytes 7208960 | tf_op jit(solution)/shard_map/pallas_call | solution.py:437
  82.5 10.4 %collective-permute-done.17.refs_1_ = bf16[64,3584]{1,0:T(8,128)(2,1)S(1)} collective-permute-done((bf16[64,3584]{1,0:T(8,128)(2,1)S(1)}, bf16[64,3584]{1,0:T(8,128)(2,1)S(1)}, u32[]{:S(2)}, u32[]{:S(2)}) %collective-permute-start.17) | collective-permute-done | bytes 458784 | tf_op jit(solution)/shard_map/ppermute | solution.py:34
  97.0 10.9 %collective-permute-done.19.refs_0_ = bf16[64,3584]{1,0:T(8,128)(2,1)S(1)} collective-permute-done((bf16[64,3584]{1,0:T(8,128)(2,1)S(1)}, bf16[64,3584]{1,0:T(8,128)(2,1)S(1)}, u32[]{:S(2)}, u32[]{:S(2)}) %collective-permute-start.19) | collective-permute-done | bytes 458784 | tf_op jit(solution)/shard_map/ppermute | solution.py:34
  109.9 4.4 %shard_map.115 = (bf16[1280,3584]{1,0:T(8,128)(2,1)S(1)}, bf16[640,3584]{1,0:T(8,128)(2,1)S(1)}) custom-call(bf16[320,3584]{1,0:T(8,128)(2,1)S(1)} %bitcast.8, bf16[320,3584]{1,0:T(8,128)(2,1)S(1)} %bitcast.10, bf16[320,3584]{1,0:T(8,128)(2,1)S(1)} %copy-done.2, bf16[480,3584]{1,0:T(8,128)(2,1)} %collective-permute-done.23.a_any, ...), custom_call_target="tpu_custom_call" | custom-call | bytes 13762560 | tf_op jit(solution)/shard_map/pallas_call | solution.py:478
  114.4 5.7 %collective-permute-done.20.refs_2_ = bf16[64,3584]{1,0:T(8,128)(2,1)S(1)} collective-permute-done((bf16[64,3584]{1,0:T(8,128)(2,1)S(1)}, bf16[64,3584]{1,0:T(8,128)(2,1)S(1)}, u32[]{:S(2)}, u32[]{:S(2)}) %collective-permute-start.20) | collective-permute-done | bytes 458784 | tf_op jit(solution)/shard_map/ppermute | solution.py:34
  124.8 5.8 %shard_map.116 = (bf16[64,3584]{1,0:T(8,128)(2,1)S(1)}, bf16[64,3584]{1,0:T(8,128)(2,1)S(1)}, bf16[64,3584]{1,0:T(8,128)(2,1)S(1)}, bf16[64,3584]{1,0:T(8,128)(2,1)S(1)}) custom-call(bf16[64,3584]{1,0:T(8,128)(2,1)S(1)} %collective-permute-done.19.refs_0_, bf16[64,3584]{1,0:T(8,128)(2,1)S(1)} %collective-permute-done.21.refs_1_, ...), custom_call_target="tpu_custom_call" | custom-call | flops 3523215360 | bytes 17432576 | tf_op jit(solution)/shard_map/pallas_call | solution.py:343
  130.7 4.5 %shard_map.118 = (bf16[32,3584]{1,0:T(8,128)(2,1)S(1)}, bf16[32,3584]{1,0:T(8,128)(2,1)S(1)}) custom-call(bf16[32,3584]{1,0:T(8,128)(2,1)S(1)} %collective-permute-done.25.refs_0_, bf16[32,3584]{1,0:T(8,128)(2,1)S(1)} %collective-permute-done.26.refs_1_, bf16[1280,3584]{1,0:T(8,128)(2,1)S(1)} %get-tuple-element.56.refs_4_.refs_3_.refs_2_, ...), custom_call_target="tpu_custom_call" | custom-call | flops 880803840 | bytes 14680064 | tf_op jit(solution)/shard_map/pallas_call | solution.py:343
  137.3 4.4 %collective-permute-done.31.refs_1_ = bf16[32,3584]{1,0:T(8,128)(2,1)S(1)} collective-permute-done((bf16[32,3584]{1,0:T(8,128)(2,1)S(1)}, bf16[32,3584]{1,0:T(8,128)(2,1)S(1)}, u32[]{:S(2)}, u32[]{:S(2)}) %collective-permute-start.31) | collective-permute-done | bytes 229408 | tf_op jit(solution)/shard_map/ppermute | solution.py:34
  144.3 7.8 %collective-permute-done.32.refs_1_ = bf16[64,3584]{1,0:T(8,128)(2,1)S(1)} collective-permute-done((bf16[64,3584]{1,0:T(8,128)(2,1)S(1)}, bf16[64,3584]{1,0:T(8,128)(2,1)S(1)}, u32[]{:S(2)}, u32[]{:S(2)}) %collective-permute-start.32) | collective-permute-done | bytes 458784 | tf_op jit(solution)/shard_map/ppermute | solution.py:34
  155.2 5.7 %shard_map.117 = (bf16[64,3584]{1,0:T(8,128)(2,1)S(1)}, bf16[64,3584]{1,0:T(8,128)(2,1)S(1)}, bf16[64,3584]{1,0:T(8,128)(2,1)S(1)}) custom-call(bf16[64,3584]{1,0:T(8,128)(2,1)S(1)} %shard_map.113.refs_0_, bf16[64,3584]{1,0:T(8,128)(2,1)S(1)} %collective-permute-done.17.refs_1_, bf16[64,3584]{1,0:T(8,128)(2,1)S(1)} %collective-permute-done.18.refs_2_, ...), custom_call_target="tpu_custom_call" | custom-call | flops 2642411520 | bytes 16515072 | tf_op jit(solution)/shard_map/pallas_call | solution.py:343
  162.4 3.5 %collective-permute-start.34 = (bf16[64,3584]{1,0:T(8,128)(2,1)S(1)}, bf16[64,3584]{1,0:T(8,128)(2,1)S(1)}, u32[]{:S(2)}, u32[]{:S(2)}) collective-permute-start(bf16[64,3584]{1,0:T(8,128)(2,1)S(1)} %shard_map.124), channel_id=1, source_target_pairs={{8,0},{16,8},{24,16},{32,24},{40,32},{48,40},{56,48},{0,56},{9,1},... | collective-permute-start | bytes 1376264 | tf_op jit(solution)/shard_map/ppermute | solution.py:34
  166.3 5.6 %collective-permute-done.34.refs_2_ = bf16[64,3584]{1,0:T(8,128)(2,1)S(1)} collective-permute-done((bf16[64,3584]{1,0:T(8,128)(2,1)S(1)}, bf16[64,3584]{1,0:T(8,128)(2,1)S(1)}, u32[]{:S(2)}, u32[]{:S(2)}) %collective-permute-start.34) | collective-permute-done | bytes 458784 | tf_op jit(solution)/shard_map/ppermute | solution.py:34
  171.9 4.1 %collective-permute-done.30.refs_1_ = bf16[64,3584]{1,0:T(8,128)(2,1)S(1)} collective-permute-done((bf16[64,3584]{1,0:T(8,128)(2,1)S(1)}, bf16[64,3584]{1,0:T(8,128)(2,1)S(1)}, u32[]{:S(2)}, u32[]{:S(2)}) %collective-permute-start.30) | collective-permute-done | bytes 458784 | tf_op jit(solution)/shard_map/ppermute | solution.py:34
  179.5 4.0 %collective-permute-done.35.refs_1_ = bf16[16,3584]{1,0:T(8,128)(2,1)S(1)} collective-permute-done((bf16[16,3584]{1,0:T(8,128)(2,1)S(1)}, bf16[16,3584]{1,0:T(8,128)(2,1)S(1)}, u32[]{:S(2)}, u32[]{:S(2)}) %collective-permute-start.35) | collective-permute-done | bytes 114720 | tf_op jit(solution)/shard_map/ppermute | solution.py:34
  (100 shorter events, 60.8 us)
Async XLA Ops:
  10.1 84.9 %collective-permute-start.23 = (bf16[480,3584]{1,0:T(8,128)(2,1)}, bf16[480,3584]{1,0:T(8,128)(2,1)}, u32[]{:S(2)}, u32[]{:S(2)}) collective-permute-start(bf16[480,3584]{1,0:T(8,128)(2,1)} %shard_map.114), channel_id=1, source_target_pairs={{0,6},{6,0},{2,4},{4,2},{1,7},{7,1},{3,5},{5,3},{8,14},{14,8},{10,... | collective-permute-start | bytes 10321928 | tf_op jit(solution)/shard_map/ppermute | solution.py:408
  20.7 9.7 %collective-permute-start.4 = (bf16[512,256]{1,0:T(8,128)(2,1)S(1)}, bf16[512,256]{1,0:T(8,128)(2,1)S(1)}, u32[]{:S(2)}, u32[]{:S(2)}) collective-permute-start(bf16[512,256]{1,0:T(8,128)(2,1)S(1)} %constant_dynamic-update-slice_fusion.2.refs_0_), channel_id=1, source_target_pairs={{8,0},{16,8},{24,16},{32,24},{40,32},{48,40},{56,48},{0,56},{9,1},... | collective-permute-start | bytes 786440 | tf_op jit(solution)/shard_map/ppermute | solution.py:34
  26.5 7.6 %collective-permute-start.5 = (bf16[512,256]{1,0:T(8,128)(2,1)S(1)}, bf16[512,256]{1,0:T(8,128)(2,1)S(1)}, u32[]{:S(2)}, u32[]{:S(2)}) collective-permute-start(bf16[512,256]{1,0:T(8,128)(2,1)S(1)} %constant_dynamic-update-slice_fusion.2.refs_0_), channel_id=1, source_target_pairs={{56,0},{0,8},{8,16},{16,24},{24,32},{32,40},{40,48},{48,56},{57,1}... | collective-permute-start | bytes 786440 | tf_op jit(solution)/shard_map/ppermute | solution.py:34
  30.4 7.8 %collective-permute-start.6 = (bf16[512,256]{1,0:T(8,128)(2,1)S(1)}, bf16[512,256]{1,0:T(8,128)(2,1)S(1)}, u32[]{:S(2)}, u32[]{:S(2)}) collective-permute-start(bf16[512,256]{1,0:T(8,128)(2,1)S(1)} %collective-permute-done.4.refs_1_), channel_id=1, source_target_pairs={{8,0},{16,8},{24,16},{32,24},{40,32},{48,40},{56,48},{0,56},{9,1},... | collective-permute-start | bytes 786440 | tf_op jit(solution)/shard_map/ppermute | solution.py:34
  34.1 8.1 %collective-permute-start.7 = (bf16[512,256]{1,0:T(8,128)(2,1)S(1)}, bf16[512,256]{1,0:T(8,128)(2,1)S(1)}, u32[]{:S(2)}, u32[]{:S(2)}) collective-permute-start(bf16[512,256]{1,0:T(8,128)(2,1)S(1)} %collective-permute-done.5.refs_2_), channel_id=1, source_target_pairs={{56,0},{0,8},{8,16},{16,24},{24,32},{32,40},{40,48},{48,56},{57,1}... | collective-permute-start | bytes 786440 | tf_op jit(solution)/shard_map/ppermute | solution.py:34
  38.3 8.4 %collective-permute-start.8 = (bf16[512,256]{1,0:T(8,128)(2,1)S(1)}, bf16[512,256]{1,0:T(8,128)(2,1)S(1)}, u32[]{:S(2)}, u32[]{:S(2)}) collective-permute-start(bf16[512,256]{1,0:T(8,128)(2,1)S(1)} %collective-permute-done.6.refs_3_), channel_id=1, source_target_pairs={{8,0},{16,8},{24,16},{32,24},{40,32},{48,40},{56,48},{0,56},{9,1},... | collective-permute-start | bytes 786440 | tf_op jit(solution)/shard_map/ppermute | solution.py:34
  42.2 8.5 %collective-permute-start.9 = (bf16[512,256]{1,0:T(8,128)(2,1)S(1)}, bf16[512,256]{1,0:T(8,128)(2,1)S(1)}, u32[]{:S(2)}, u32[]{:S(2)}) collective-permute-start(bf16[512,256]{1,0:T(8,128)(2,1)S(1)} %collective-permute-done.7.refs_4_), channel_id=1, source_target_pairs={{56,0},{0,8},{8,16},{16,24},{24,32},{32,40},{40,48},{48,56},{57,1}... | collective-permute-start | bytes 786440 | tf_op jit(solution)/shard_map/ppermute | solution.py:34
  46.7 8.3 %collective-permute-start.10 = (bf16[256,256]{1,0:T(8,128)(2,1)S(1)}, bf16[256,256]{1,0:T(8,128)(2,1)S(1)}, u32[]{:S(2)}, u32[]{:S(2)}) collective-permute-start(bf16[256,256]{1,0:T(8,128)(2,1)S(1)} %slice.16), channel_id=1, source_target_pairs={{8,0},{16,8},{24,16},{32,24},{40,32},{48,40},{56,48},{0,56},{9,1},... | collective-permute-start | bytes 393224 | tf_op jit(solution)/shard_map/ppermute | solution.py:34
  72.7 7.7 %collective-permute-start.16 = (bf16[16,3584]{1,0:T(8,128)(2,1)S(1)}, bf16[16,3584]{1,0:T(8,128)(2,1)S(1)}, u32[]{:S(2)}, u32[]{:S(2)}) collective-permute-start(bf16[16,3584]{1,0:T(8,128)(2,1)S(1)} %get-tuple-element.48.refs_0_), channel_id=1, source_target_pairs={{192,0},{0,64},{64,128},{128,192},{193,1},{1,65},{65,129},{129,193... | collective-permute-start | bytes 344072 | tf_op jit(solution)/shard_map/ppermute | solution.py:34
  80.4 12.5 %collective-permute-start.17 = (bf16[64,3584]{1,0:T(8,128)(2,1)S(1)}, bf16[64,3584]{1,0:T(8,128)(2,1)S(1)}, u32[]{:S(2)}, u32[]{:S(2)}) collective-permute-start(bf16[64,3584]{1,0:T(8,128)(2,1)S(1)} %shard_map.113.refs_0_), channel_id=1, source_target_pairs={{8,0},{16,8},{24,16},{32,24},{40,32},{48,40},{56,48},{0,56},{9,1},... | collective-permute-start | bytes 1376264 | tf_op jit(solution)/shard_map/ppermute | solution.py:34
  81.6 13.4 %collective-permute-start.18 = (bf16[64,3584]{1,0:T(8,128)(2,1)S(1)}, bf16[64,3584]{1,0:T(8,128)(2,1)S(1)}, u32[]{:S(2)}, u32[]{:S(2)}) collective-permute-start(bf16[64,3584]{1,0:T(8,128)(2,1)S(1)} %shard_map.113.refs_0_), channel_id=1, source_target_pairs={{56,0},{0,8},{8,16},{16,24},{24,32},{32,40},{40,48},{48,56},{57,1}... | collective-permute-start | bytes 1376264 | tf_op jit(solution)/shard_map/ppermute | solution.py:34
  95.0 15.0 %collective-permute-start.24 = (bf16[480,3584]{1,0:T(8,128)(2,1)}, bf16[480,3584]{1,0:T(8,128)(2,1)S(1)}, u32[]{:S(2)}, u32[]{:S(2)}) collective-permute-start(bf16[480,3584]{1,0:T(8,128)(2,1)} %collective-permute-done.23.a_any), channel_id=1, source_target_pairs={{1,0},{0,1},{3,2},{2,3},{5,4},{4,5},{7,6},{6,7},{9,8},{8,9},{11,10... | collective-permute-start | bytes 10321928 | tf_op jit(solution)/shard_map/ppermute | solution.py:34
  95.0 12.9 %collective-permute-start.19 = (bf16[64,3584]{1,0:T(8,128)(2,1)S(1)}, bf16[64,3584]{1,0:T(8,128)(2,1)S(1)}, u32[]{:S(2)}, u32[]{:S(2)}) collective-permute-start(bf16[64,3584]{1,0:T(8,128)(2,1)S(1)} %collective-permute-done.17.refs_1_), channel_id=1, source_target_pairs={{8,0},{16,8},{24,16},{32,24},{40,32},{48,40},{56,48},{0,56},{9,1},... | collective-permute-start | bytes 1376264 | tf_op jit(solution)/shard_map/ppermute | solution.py:34
  95.3 14.1 %collective-permute-start.21 = (bf16[64,3584]{1,0:T(8,128)(2,1)S(1)}, bf16[64,3584]{1,0:T(8,128)(2,1)S(1)}, u32[]{:S(2)}, u32[]{:S(2)}) collective-permute-start(bf16[64,3584]{1,0:T(8,128)(2,1)S(1)} %collective-permute-done.18.refs_2_), channel_id=1, source_target_pairs={{56,0},{0,8},{8,16},{16,24},{24,32},{32,40},{40,48},{48,56},{57,1}... | collective-permute-start | bytes 1376264 | tf_op jit(solution)/shard_map/ppermute | solution.py:34
  107.9 12.2 %collective-permute-start.20 = (bf16[64,3584]{1,0:T(8,128)(2,1)S(1)}, bf16[64,3584]{1,0:T(8,128)(2,1)S(1)}, u32[]{:S(2)}, u32[]{:S(2)}) collective-permute-start(bf16[64,3584]{1,0:T(8,128)(2,1)S(1)} %collective-permute-done.19.refs_0_), channel_id=1, source_target_pairs={{8,0},{16,8},{24,16},{32,24},{40,32},{48,40},{56,48},{0,56},{9,1},... | collective-permute-start | bytes 1376264 | tf_op jit(solution)/shard_map/ppermute | solution.py:34
  109.4 13.0 %collective-permute-start.22 = (bf16[64,3584]{1,0:T(8,128)(2,1)S(1)}, bf16[64,3584]{1,0:T(8,128)(2,1)S(1)}, u32[]{:S(2)}, u32[]{:S(2)}) collective-permute-start(bf16[64,3584]{1,0:T(8,128)(2,1)S(1)} %collective-permute-done.21.refs_1_), channel_id=1, source_target_pairs={{56,0},{0,8},{8,16},{16,24},{24,32},{32,40},{40,48},{48,56},{57,1}... | collective-permute-start | bytes 1376264 | tf_op jit(solution)/shard_map/ppermute | solution.py:34
  122.4 8.2 %collective-permute-start.25 = (bf16[32,3584]{1,0:T(8,128)(2,1)S(1)}, bf16[32,3584]{1,0:T(8,128)(2,1)S(1)}, u32[]{:S(2)}, u32[]{:S(2)}) collective-permute-start(bf16[32,3584]{1,0:T(8,128)(2,1)S(1)} %slice.14), channel_id=1, source_target_pairs={{8,0},{16,8},{24,16},{32,24},{40,32},{48,40},{56,48},{0,56},{9,1},... | collective-permute-start | bytes 688136 | tf_op jit(solution)/shard_map/ppermute | solution.py:34
  123.0 7.6 %collective-permute-start.26 = (bf16[32,3584]{1,0:T(8,128)(2,1)S(1)}, bf16[32,3584]{1,0:T(8,128)(2,1)S(1)}, u32[]{:S(2)}, u32[]{:S(2)}) collective-permute-start(bf16[32,3584]{1,0:T(8,128)(2,1)S(1)} %slice.15), channel_id=1, source_target_pairs={{56,0},{0,8},{8,16},{16,24},{24,32},{32,40},{40,48},{48,56},{57,1}... | collective-permute-start | bytes 688136 | tf_op jit(solution)/shard_map/ppermute | solution.py:34
  141.8 10.3 %collective-permute-start.32 = (bf16[64,3584]{1,0:T(8,128)(2,1)S(1)}, bf16[64,3584]{1,0:T(8,128)(2,1)S(1)}, u32[]{:S(2)}, u32[]{:S(2)}) collective-permute-start(bf16[64,3584]{1,0:T(8,128)(2,1)S(1)} %shard_map.122), channel_id=1, source_target_pairs={{8,0},{16,8},{24,16},{32,24},{40,32},{48,40},{56,48},{0,56},{9,1},... | collective-permute-start | bytes 1376264 | tf_op jit(solution)/shard_map/ppermute | solution.py:34
  144.2 10.8 %collective-permute-start.28 = (bf16[64,3584]{1,0:T(8,128)(2,1)S(1)}, bf16[64,3584]{1,0:T(8,128)(2,1)S(1)}, u32[]{:S(2)}, u32[]{:S(2)}) collective-permute-start(bf16[64,3584]{1,0:T(8,128)(2,1)S(1)} %shard_map.119), channel_id=1, source_target_pairs={{56,0},{0,8},{8,16},{16,24},{24,32},{32,40},{40,48},{48,56},{57,1}... | collective-permute-start | bytes 1376264 | tf_op jit(solution)/shard_map/ppermute | solution.py:34
  152.3 10.0 %collective-permute-start.33 = (bf16[64,3584]{1,0:T(8,128)(2,1)S(1)}, bf16[64,3584]{1,0:T(8,128)(2,1)S(1)}, u32[]{:S(2)}, u32[]{:S(2)}) collective-permute-start(bf16[64,3584]{1,0:T(8,128)(2,1)S(1)} %shard_map.123), channel_id=1, source_target_pairs={{8,0},{16,8},{24,16},{32,24},{40,32},{48,40},{56,48},{0,56},{9,1},... | collective-permute-start | bytes 1376264 | tf_op jit(solution)/shard_map/ppermute | solution.py:34
  155.1 11.0 %collective-permute-start.29 = (bf16[64,3584]{1,0:T(8,128)(2,1)S(1)}, bf16[64,3584]{1,0:T(8,128)(2,1)S(1)}, u32[]{:S(2)}, u32[]{:S(2)}) collective-permute-start(bf16[64,3584]{1,0:T(8,128)(2,1)S(1)} %shard_map.120), channel_id=1, source_target_pairs={{56,0},{0,8},{8,16},{16,24},{24,32},{32,40},{40,48},{48,56},{57,1}... | collective-permute-start | bytes 1376264 | tf_op jit(solution)/shard_map/ppermute | solution.py:34
  162.4 9.5 %collective-permute-start.34 = (bf16[64,3584]{1,0:T(8,128)(2,1)S(1)}, bf16[64,3584]{1,0:T(8,128)(2,1)S(1)}, u32[]{:S(2)}, u32[]{:S(2)}) collective-permute-start(bf16[64,3584]{1,0:T(8,128)(2,1)S(1)} %shard_map.124), channel_id=1, source_target_pairs={{8,0},{16,8},{24,16},{32,24},{40,32},{48,40},{56,48},{0,56},{9,1},... | collective-permute-start | bytes 1376264 | tf_op jit(solution)/shard_map/ppermute | solution.py:34
  166.2 9.8 %collective-permute-start.30 = (bf16[64,3584]{1,0:T(8,128)(2,1)S(1)}, bf16[64,3584]{1,0:T(8,128)(2,1)S(1)}, u32[]{:S(2)}, u32[]{:S(2)}) collective-permute-start(bf16[64,3584]{1,0:T(8,128)(2,1)S(1)} %shard_map.121), channel_id=1, source_target_pairs={{56,0},{0,8},{8,16},{16,24},{24,32},{32,40},{40,48},{48,56},{57,1}... | collective-permute-start | bytes 1376264 | tf_op jit(solution)/shard_map/ppermute | solution.py:34
  (22 other events, 366.0 us)
